TPU v7x, 32 devices: a whole 2x2x4 slice. The times are simulated.
32 devices in a mesh: ctx: 8 (over z, x), fsdp: 4 (over y, core).
Axes of the slice: x: 2, y: 2, z: 4, core: 2. Of those that a mesh axis runs over, the one named last changes fastest.
Arguments:
- layer_input: bfloat16 [2, 4, 1024, 1024], P(None, 'fsdp', 'ctx'), may hold values from -6 to 6
- segments: int32 [2, 4, 1024], P(None, 'fsdp', 'ctx'), may hold values from 0 to 15, never falling along the last dimension, each value on 1 to 512 neighbouring positions
- cotangent: bfloat16 [2, 4, 1024, 1024], P(None, 'fsdp', 'ctx'), may hold values from -6 to 6
- query_weight: bfloat16 [1024, 1024], P('fsdp'), may hold values from -0.1875 to 0.1875
- key_weight: bfloat16 [1024, 1024], P('fsdp'), may hold values from -0.1875 to 0.1875
- value_weight: bfloat16 [1024, 1024], P('fsdp'), may hold values from -0.1875 to 0.1875
- output_weight: bfloat16 [1024, 1024], P('fsdp'), may hold values from -0.75 to 0.75
- expand_weight: bfloat16 [1024, 4096], P('fsdp'), may hold values from -0.1875 to 0.1875
- contract_weight: bfloat16 [4096, 1024], P('fsdp'), may hold values from -0.09375 to 0.09375
- query_bias: bfloat16 [1024], P('fsdp'), may hold values from -3 to 3
- value_bias: bfloat16 [1024], P('fsdp'), may hold values from -3 to 3
- output_bias: bfloat16 [1024], P('fsdp'), may hold values from -3 to 3
- first_gain: bfloat16 [1024], P('fsdp'), may hold values from 0.099609375 to 1.8984375
- first_shift: bfloat16 [1024], P('fsdp'), may hold values from -3 to 3
- expand_bias: bfloat16 [4096], P('fsdp'), may hold values from -3 to 3
- contract_bias: bfloat16 [1024], P('fsdp'), may hold values from -3 to 3
- second_gain: bfloat16 [1024], P('fsdp'), may hold values from 0.099609375 to 1.8984375
- second_shift: bfloat16 [1024], P('fsdp'), may hold values from -3 to 3
Outputs:
- layer_output: bfloat16 [2, 4, 1024, 1024], P(None, 'fsdp', 'ctx')
- input_grad: float32 [2, 4, 1024, 1024], P(None, 'fsdp', 'ctx')
- query_weight_grad: float32 [1024, 1024], P('fsdp')
- key_weight_grad: float32 [1024, 1024], P('fsdp')
- value_weight_grad: float32 [1024, 1024], P('fsdp')
- output_weight_grad: float32 [1024, 1024], P('fsdp')
- expand_weight_grad: float32 [1024, 4096], P('fsdp')
- contract_weight_grad: float32 [4096, 1024], P('fsdp')
- query_bias_grad: float32 [1024], P('fsdp')
- value_bias_grad: float32 [1024], P('fsdp')
- output_bias_grad: float32 [1024], P('fsdp')
- first_gain_grad: float32 [1024], P('fsdp')
- first_shift_grad: float32 [1024], P('fsdp')
- expand_bias_grad: float32 [4096], P('fsdp')
- contract_bias_grad: float32 [1024], P('fsdp')
- second_gain_grad: float32 [1024], P('fsdp')
- second_shift_grad: float32 [1024], P('fsdp')
Inputs may be any that keep to these rules, and one draw needn't show every extreme that they name: `segments`: in each sequence the ids never fall along the positions; each document holds 1 to 512 positions, and one holds exactly 512.
All inputs are finite; a program needn't handle non-finite values.
Results may differ from a plain program's by a relative error of at most 0.025.
Values may be sent and summed in bfloat16 or wider, within the bound.
A program may use at most 192 MiB of HBM per device.

v0:
```python
import jax
import jax.numpy as jnp
from jax import lax
from jax.sharding import PartitionSpec as P

HEADS = 16
HEAD_DIM = 64


def as_sent(x):
    return jax.tree.map(lambda a: a.astype(jnp.bfloat16) if a.dtype == jnp.float32 else a, x)


def plain_dot(left_side, right_side):
    return jnp.dot(left_side, right_side, preferred_element_type=jnp.float32)


def left_dot(left_side, right_side):
    return lax.dot_general(
        left_side, right_side, (((0,), (0,)), ((), ())), preferred_element_type=jnp.float32
    )


def right_dot(left_side, right_side):
    return lax.dot_general(
        left_side, right_side, (((1,), (1,)), ((), ())), preferred_element_type=jnp.float32
    )


def norm_forward(hidden, gain_row, offset_row):
    centre = hidden - jnp.mean(hidden, axis=-1, keepdims=True)
    inverse = lax.rsqrt(jnp.mean(centre * centre, axis=-1, keepdims=True) + 1e-05)
    normed = centre * inverse
    return (normed * gain_row.astype(jnp.float32) + offset_row.astype(jnp.float32), normed, inverse)


def norm_backward(grad_out, normed, inverse, gain_row):
    scaled = grad_out * gain_row.astype(jnp.float32)
    grad_in = inverse * (
        scaled
        - jnp.mean(scaled, axis=-1, keepdims=True)
        - normed * jnp.mean(scaled * normed, axis=-1, keepdims=True)
    )
    return (grad_in, jnp.sum(grad_out * normed, axis=0), jnp.sum(grad_out, axis=0))


def gather_weights(shards):
    return (
        lax.all_gather(shards[0], "fsdp", axis=0, tiled=True),
        lax.all_gather(shards[1], "fsdp", axis=0, tiled=True),
        lax.all_gather(shards[2], "fsdp", axis=0, tiled=True),
        lax.all_gather(shards[3], "fsdp", axis=0, tiled=True),
        lax.all_gather(shards[4], "fsdp", axis=0, tiled=True),
        lax.all_gather(shards[5], "fsdp", axis=0, tiled=True),
        lax.all_gather(shards[6], "fsdp", axis=0, tiled=True),
        lax.all_gather(shards[7], "fsdp", axis=0, tiled=True),
        lax.all_gather(shards[8], "fsdp", axis=0, tiled=True),
        lax.all_gather(shards[9], "fsdp", axis=0, tiled=True),
        lax.all_gather(shards[10], "fsdp", axis=0, tiled=True),
        lax.all_gather(shards[11], "fsdp", axis=0, tiled=True),
        lax.all_gather(shards[12], "fsdp", axis=0, tiled=True),
        lax.all_gather(shards[13], "fsdp", axis=0, tiled=True),
        lax.all_gather(shards[14], "fsdp", axis=0, tiled=True),
    )


def attend_forward(query_bf, key_bf, value_bf, seg_local):
    row_count = query_bf.shape[0]
    score_scale = HEAD_DIM ** (-0.5)
    query_heads = query_bf.reshape(row_count, HEADS, HEAD_DIM)
    run_max = jnp.full((HEADS, row_count), -1e30, jnp.float32)
    key_rows = lax.all_gather(key_bf, "ctx", axis=0, tiled=True)
    value_rows = lax.all_gather(value_bf, "ctx", axis=0, tiled=True)
    key_seg = lax.all_gather(seg_local, "ctx", axis=0, tiled=True)
    piece_rows = key_rows.shape[0]
    key_heads = key_rows.reshape(piece_rows, HEADS, HEAD_DIM)
    value_heads = value_rows.reshape(piece_rows, HEADS, HEAD_DIM)
    scores = (
        jnp.einsum("rhd,khd->hrk", query_heads, key_heads, preferred_element_type=jnp.float32)
        * score_scale
    )
    same_doc = seg_local[:, None] == key_seg[None, :]
    scores = jnp.where(same_doc[None], scores, -1e30)
    new_max = jnp.maximum(run_max, jnp.max(scores, axis=-1))
    numerators = jnp.exp(scores - new_max[..., None])
    run_sum = jnp.sum(numerators, axis=-1)
    accumulated = jnp.einsum(
        "hrk,khd->hrd",
        numerators.astype(jnp.bfloat16),
        value_heads,
        preferred_element_type=jnp.float32,
    )
    run_max, run_sum, accumulated = (new_max, run_sum, accumulated)
    context = jnp.transpose(accumulated / run_sum[..., None], (1, 0, 2)).reshape(
        row_count, HEADS * HEAD_DIM
    )
    return (context, run_max + jnp.log(run_sum))


def block_grads(
    query_heads, grad_heads, query_seg, log_sum, row_delta, key_heads, value_heads, key_seg
):
    score_scale = HEAD_DIM ** (-0.5)
    scores = (
        jnp.einsum("rhd,khd->hrk", query_heads, key_heads, preferred_element_type=jnp.float32)
        * score_scale
    )
    same_doc = query_seg[:, None] == key_seg[None, :]
    scores = jnp.where(same_doc[None], scores, -1e30)
    probs_full = jnp.exp(scores - log_sum[..., None])
    grad_probs = jnp.einsum(
        "rhd,khd->hrk", grad_heads, value_heads, preferred_element_type=jnp.float32
    )
    grad_scores = (probs_full * (grad_probs - row_delta[..., None])).astype(jnp.bfloat16)
    return (probs_full, grad_scores)


def attend_backward(query_bf, key_bf, value_bf, seg_local, context, log_sum, grad_context):
    row_count = query_bf.shape[0]
    score_scale = HEAD_DIM ** (-0.5)
    key_every, value_every, seg_every = (
        lax.all_gather(key_bf, "ctx", axis=0, tiled=True),
        lax.all_gather(value_bf, "ctx", axis=0, tiled=True),
        lax.all_gather(seg_local, "ctx", axis=0, tiled=True),
    )
    length = key_every.shape[0]
    block_len = min(512, length)
    query_heads = query_bf.reshape(row_count, HEADS, HEAD_DIM)
    grad_heads = grad_context.reshape(row_count, HEADS, HEAD_DIM)
    row_delta = jnp.sum(
        (grad_context.astype(jnp.float32) * context).reshape(row_count, HEADS, HEAD_DIM), axis=-1
    ).T

    def visit_block(grad_query, block_num):
        first_row = block_num * block_len
        key_heads = lax.dynamic_slice_in_dim(key_every, first_row, block_len, 0).reshape(
            block_len, HEADS, HEAD_DIM
        )
        value_heads = lax.dynamic_slice_in_dim(value_every, first_row, block_len, 0).reshape(
            block_len, HEADS, HEAD_DIM
        )
        key_seg = lax.dynamic_slice_in_dim(seg_every, first_row, block_len, 0)
        probs_full, grad_scores = block_grads(
            query_heads, grad_heads, seg_local, log_sum, row_delta, key_heads, value_heads, key_seg
        )
        grad_query = (
            grad_query
            + jnp.einsum("hrk,khd->rhd", grad_scores, key_heads, preferred_element_type=jnp.float32)
            * score_scale
        )
        grad_keys = (
            jnp.einsum("hrk,rhd->khd", grad_scores, query_heads, preferred_element_type=jnp.float32)
            * score_scale
        )
        grad_values = jnp.einsum(
            "hrk,rhd->khd",
            probs_full.astype(jnp.bfloat16),
            grad_heads,
            preferred_element_type=jnp.float32,
        )
        stacked = jnp.stack(
            (
                grad_keys.reshape(block_len, HEADS * HEAD_DIM),
                grad_values.reshape(block_len, HEADS * HEAD_DIM),
            ),
            axis=1,
        )
        return (grad_query, stacked)

    grad_query, pieces = lax.scan(
        visit_block,
        jnp.zeros((row_count, HEADS, HEAD_DIM), jnp.float32),
        jnp.arange(length // block_len),
    )
    key_terms = pieces.reshape(length, 2, HEADS * HEAD_DIM)
    own_rows = lax.psum_scatter(
        key_terms.astype(jnp.bfloat16), "ctx", scatter_dimension=0, tiled=True
    ).astype(jnp.float32)
    grad_keyed = own_rows[:, 0].astype(jnp.bfloat16)
    grad_valued = own_rows[:, 1].astype(jnp.bfloat16)
    grad_queries = grad_query.reshape(row_count, HEADS * HEAD_DIM).astype(jnp.bfloat16)
    return (grad_queries, grad_keyed, grad_valued)


def layer_forward(inputs, seg_local, full_weights):
    (
        query_weight,
        key_weight,
        value_weight,
        output_weight,
        expand_weight,
        contract_weight,
        query_bias,
        value_bias,
        output_bias,
        first_gain,
        first_shift,
        expand_bias,
        contract_bias,
        second_gain,
        second_shift,
    ) = full_weights
    query_bf = (plain_dot(inputs, query_weight) + query_bias.astype(jnp.float32)).astype(
        jnp.bfloat16
    )
    key_bf = plain_dot(inputs, key_weight).astype(jnp.bfloat16)
    value_bf = (plain_dot(inputs, value_weight) + value_bias.astype(jnp.float32)).astype(
        jnp.bfloat16
    )
    context, log_sum = attend_forward(query_bf, key_bf, value_bf, seg_local)
    context_bf = context.astype(jnp.bfloat16)
    first_sum = (
        inputs.astype(jnp.float32)
        + plain_dot(context_bf, output_weight)
        + output_bias.astype(jnp.float32)
    )
    first_out, normed_one, inverse_one = norm_forward(first_sum, first_gain, first_shift)
    first_bf = first_out.astype(jnp.bfloat16)
    hidden = plain_dot(first_bf, expand_weight) + expand_bias.astype(jnp.float32)
    gelled_bf = jax.nn.gelu(hidden, approximate=False).astype(jnp.bfloat16)
    second_sum = (
        first_out + plain_dot(gelled_bf, contract_weight) + contract_bias.astype(jnp.float32)
    )
    result, normed_two, inverse_two = norm_forward(second_sum, second_gain, second_shift)
    kept_state = (
        query_bf,
        key_bf,
        value_bf,
        context,
        log_sum,
        context_bf,
        normed_one,
        inverse_one,
        first_bf,
        hidden,
        gelled_bf,
        normed_two,
        inverse_two,
    )
    return (result.astype(jnp.bfloat16), kept_state)


def layer_backward(inputs, seg_local, grad_out, kept_state, full_weights):
    (
        query_weight,
        key_weight,
        value_weight,
        output_weight,
        expand_weight,
        contract_weight,
        query_bias,
        value_bias,
        output_bias,
        first_gain,
        first_shift,
        expand_bias,
        contract_bias,
        second_gain,
        second_shift,
    ) = full_weights
    (
        query_bf,
        key_bf,
        value_bf,
        context,
        log_sum,
        context_bf,
        normed_one,
        inverse_one,
        first_bf,
        hidden,
        gelled_bf,
        normed_two,
        inverse_two,
    ) = kept_state
    grad_second, second_gain_grad, second_shift_grad = norm_backward(
        grad_out.astype(jnp.float32), normed_two, inverse_two, second_gain
    )
    grad_branch = grad_second.astype(jnp.bfloat16)
    contract_weight_grad = left_dot(gelled_bf, grad_branch)
    contract_bias_grad = jnp.sum(grad_branch.astype(jnp.float32), axis=0)
    grad_gelled = right_dot(grad_branch, contract_weight)
    gelu_pull = jax.vjp(lambda values: jax.nn.gelu(values, approximate=False), hidden)[1]
    grad_hidden = gelu_pull(grad_gelled)[0].astype(jnp.bfloat16)
    expand_weight_grad = left_dot(first_bf, grad_hidden)
    expand_bias_grad = jnp.sum(grad_hidden.astype(jnp.float32), axis=0)
    grad_first = grad_second + right_dot(grad_hidden, expand_weight)
    grad_attn, first_gain_grad, first_shift_grad = norm_backward(
        grad_first, normed_one, inverse_one, first_gain
    )
    grad_attn_low = grad_attn.astype(jnp.bfloat16)
    output_weight_grad = left_dot(context_bf, grad_attn_low)
    output_bias_grad = jnp.sum(grad_attn_low.astype(jnp.float32), axis=0)
    grad_context = right_dot(grad_attn_low, output_weight).astype(jnp.bfloat16)
    grad_queries, grad_keyed, grad_valued = attend_backward(
        query_bf, key_bf, value_bf, seg_local, context, log_sum, grad_context
    )
    query_weight_grad = left_dot(inputs, grad_queries)
    key_weight_grad = left_dot(inputs, grad_keyed)
    value_weight_grad = left_dot(inputs, grad_valued)
    query_bias_grad = jnp.sum(grad_queries.astype(jnp.float32), axis=0)
    value_bias_grad = jnp.sum(grad_valued.astype(jnp.float32), axis=0)
    grad_input = (
        grad_attn
        + right_dot(grad_queries, query_weight)
        + right_dot(grad_keyed, key_weight)
        + right_dot(grad_valued, value_weight)
    )
    grad_terms = (
        query_weight_grad,
        key_weight_grad,
        value_weight_grad,
        output_weight_grad,
        expand_weight_grad,
        contract_weight_grad,
        query_bias_grad,
        value_bias_grad,
        output_bias_grad,
        first_gain_grad,
        first_shift_grad,
        expand_bias_grad,
        contract_bias_grad,
        second_gain_grad,
        second_shift_grad,
    )
    return (grad_input, grad_terms)


def per_device(
    layer_input,
    segments,
    cotangent,
    query_weight,
    key_weight,
    value_weight,
    output_weight,
    expand_weight,
    contract_weight,
    query_bias,
    value_bias,
    output_bias,
    first_gain,
    first_shift,
    expand_bias,
    contract_bias,
    second_gain,
    second_shift,
):
    shards = (
        query_weight,
        key_weight,
        value_weight,
        output_weight,
        expand_weight,
        contract_weight,
        query_bias,
        value_bias,
        output_bias,
        first_gain,
        first_shift,
        expand_bias,
        contract_bias,
        second_gain,
        second_shift,
    )
    micro_count = layer_input.shape[0]
    results = []
    grad_inputs = []
    totals = None
    for micro_step in range(micro_count):
        inputs = layer_input[micro_step, 0]
        seg_local = segments[micro_step, 0].astype(jnp.bfloat16)
        front_weights = gather_weights(shards)
        result, kept_state = layer_forward(inputs, seg_local, front_weights)
        behind = gather_weights(shards)
        grad_input, grad_terms = layer_backward(
            inputs, seg_local, cotangent[micro_step, 0], kept_state, behind
        )
        results.append(result)
        grad_inputs.append(grad_input)
        if totals is None:
            totals = grad_terms
        else:
            totals = tuple(
                (left_side + right_side for left_side, right_side in zip(totals, grad_terms))
            )
    reduced = jax.tree.map(
        lambda part: part.astype(jnp.float32),
        lax.psum_scatter(as_sent(totals), "fsdp", scatter_dimension=0, tiled=True),
    )
    summed = jax.tree.map(lambda part: part.astype(jnp.float32), lax.psum(as_sent(reduced), "ctx"))
    layer_output = jnp.stack(results, axis=0)[:, None]
    input_grad = jnp.stack(grad_inputs, axis=0)[:, None]
    return (
        layer_output,
        input_grad,
        summed[0],
        summed[1],
        summed[2],
        summed[3],
        summed[4],
        summed[5],
        summed[6],
        summed[7],
        summed[8],
        summed[9],
        summed[10],
        summed[11],
        summed[12],
        summed[13],
        summed[14],
    )


def solution(mesh):
    in_specs = (
        P(None, "fsdp", "ctx", None),
        P(None, "fsdp", "ctx"),
        P(None, "fsdp", "ctx", None),
        P("fsdp", None),
        P("fsdp", None),
        P("fsdp", None),
        P("fsdp", None),
        P("fsdp", None),
        P("fsdp", None),
        P("fsdp"),
        P("fsdp"),
        P("fsdp"),
        P("fsdp"),
        P("fsdp"),
        P("fsdp"),
        P("fsdp"),
        P("fsdp"),
        P("fsdp"),
    )
    out_specs = (
        P(None, "fsdp", "ctx", None),
        P(None, "fsdp", "ctx", None),
        P("fsdp", None),
        P("fsdp", None),
        P("fsdp", None),
        P("fsdp", None),
        P("fsdp", None),
        P("fsdp", None),
        P("fsdp"),
        P("fsdp"),
        P("fsdp"),
        P("fsdp"),
        P("fsdp"),
        P("fsdp"),
        P("fsdp"),
        P("fsdp"),
        P("fsdp"),
    )
    return jax.shard_map(
        per_device, mesh=mesh, in_specs=in_specs, out_specs=out_specs, check_vma=False
    )
```

profile of v0, /device:TPU:0, one launch (start us, length us, event | category | flops | bytes accessed | tf_op | source)
XLA Modules:
  0.0 1220.2 jit_solution(14195021096110765214)
XLA Ops:
  10.1 6.0 all-gather.3
  16.1 18.8 %all-gather.27.cloned.1.call-done = bf16[1024,1024]{1,0:T(8,128)(2,1)} async-done(((bf16[256,1024]{1,0:T(8,128)(2,1)}), bf16[1024,1024]{1,0:T(8,128)(2,1)}) %all-gather.27.cloned.1.call-update) | async-done | bytes 2097168 | tf_op jit(solution)/shard_map/all_gather | solution.py:51
  37.8 21.3 %all-gather.23.cloned.1.call-done = bf16[1024,1024]{1,0:T(8,128)(2,1)} async-done(((bf16[256,1024]{1,0:T(8,128)(2,1)}), bf16[1024,1024]{1,0:T(8,128)(2,1)}) %all-gather.23.cloned.1.call-update) | async-done | bytes 2097168 | tf_op jit(solution)/shard_map/all_gather | solution.py:50
  103.9 20.6 %all-gather = bf16[1,1,1024]{2,1,0:T(2,128)(2,1)S(1)} all-gather(bf16[1,1,128]{2,1,0:T(2,128)(2,1)S(1)} %get-tuple-element.466), channel_id=2, replica_groups=mesh['ctx'=8,'fsdp'=4] {'ctx'}, dimensions={2}, use_global_device_ids=true | all-gather | bytes 2304 | tf_op jit(solution)/shard_map/all_gather | solution.py:74
  124.6 16.3 %all-gather.1 = bf16[1,1,1024]{2,1,0:T(2,128)(2,1)S(1)} all-gather(bf16[1,1,128]{2,1,0:T(2,128)(2,1)S(1)} %get-tuple-element.465), channel_id=3, replica_groups=mesh['ctx'=8,'fsdp'=4] {'ctx'}, dimensions={2}, use_global_device_ids=true | all-gather | bytes 2304 | tf_op jit(solution)/shard_map/all_gather | solution.py:74
  154.5 31.1 %all-gather.25.cloned.1.call-done = bf16[1024,1024]{1,0:T(8,128)(2,1)} async-done(((bf16[128,1024]{1,0:T(8,128)(2,1)}), bf16[1024,1024]{1,0:T(8,128)(2,1)}) %all-gather.25.cloned.1.call-update) | async-done | bytes 2097168 | tf_op jit(solution)/shard_map/all_gather | solution.py:72
  199.6 36.4 %all-gather.39.cloned.1.call-done = bf16[1024,1024]{1,0:T(8,128)(2,1)} async-done(((bf16[128,1024]{1,0:T(8,128)(2,1)}), bf16[1024,1024]{1,0:T(8,128)(2,1)}) %all-gather.39.cloned.1.call-update) | async-done | bytes 2097168 | tf_op jit(solution)/shard_map/all_gather | solution.py:73
  239.9 46.6 %all-gather.37.cloned.1.call-done = bf16[1024,1024]{1,0:T(8,128)(2,1)} async-done(((bf16[128,1024]{1,0:T(8,128)(2,1)}), bf16[1024,1024]{1,0:T(8,128)(2,1)}) %all-gather.37.cloned.1.call-update) | async-done | bytes 2097168 | tf_op jit(solution)/shard_map/all_gather | solution.py:72
  290.4 18.7 %all-gather.31.cloned.1.call-done = bf16[1024,1024]{1,0:T(8,128)(2,1)} async-done(((bf16[256,1024]{1,0:T(8,128)(2,1)}), bf16[1024,1024]{1,0:T(8,128)(2,1)}) %all-gather.31.cloned.1.call-update) | async-done | bytes 2097168 | tf_op jit(solution)/shard_map/all_gather | solution.py:52
  322.7 46.4 %all-gather.33.cloned.1.call-done = bf16[1024,4096]{1,0:T(8,128)(2,1)} async-done(((bf16[256,4096]{1,0:T(8,128)(2,1)}), bf16[1024,4096]{1,0:T(8,128)(2,1)}) %all-gather.33.cloned.1.call-update) | async-done | bytes 8388624 | tf_op jit(solution)/shard_map/all_gather | solution.py:53
  369.1 6.1 convolution_add_fusion.1
  375.2 53.6 %all-gather.35.cloned.1.call-done = bf16[4096,1024]{1,0:T(8,128)(2,1)} async-done(((bf16[1024,1024]{1,0:T(8,128)(2,1)}), bf16[4096,1024]{1,0:T(8,128)(2,1)}) %all-gather.35.cloned.1.call-update) | async-done | bytes 8388624 | tf_op jit(solution)/shard_map/all_gather | solution.py:54
  428.8 9.7 fusion.170
  442.1 5.7 fusion.172
  451.0 8.1 convert_reduce_fusion.1
  462.8 8.1 convert_reduce_fusion
  479.8 34.4 %while.26 = (s32[]{:T(128)}, f32[128,16,64]{0,2,1:T(8,128)}, bf16[2,512,2,1024]{3,1,0,2:T(8,128)(2,1)}, s32[2]{0:T(128)S(1)}, bf16[1024,1024]{0,1:T(8,128)(2,1)}...) while((s32[]{:T(128)}, f32[128,16,64]{0,2,1:T(8,128)}, ...), condition=%wide.region_18.19_spmd.clone, body=%wide.region_17.18_spmd.clone.sunk | while | flops 684130304 | bytes 77819448 | solution.py:170
  523.4 34.7 %while.27 = (s32[]{:T(128)}, f32[128,16,64]{0,2,1:T(8,128)}, bf16[2,512,2,1024]{3,1,0,2:T(8,128)(2,1)}, s32[2]{0:T(128)S(1)}, bf16[1024,1024]{0,1:T(8,128)(2,1)}...) while((s32[]{:T(128)}, f32[128,16,64]{0,2,1:T(8,128)}, ...), condition=%wide.region_26.27_spmd.clone, body=%wide.region_25.26_spmd.clone.sunk | while | flops 684130304 | bytes 77819448 | solution.py:170
  566.4 36.0 %reduce-scatter.9.cloned.1.call-done = bf16[128,2,1024]{2,0,1:T(8,128)(2,1)} async-done(((bf16[1024,2,1024]{2,0,1:T(8,128)(2,1)}), bf16[128,2,1024]{2,0,1:T(8,128)(2,1)}) %reduce-scatter.9.cloned.1.call-update) | async-done | bytes 524304 | tf_op jit(solution)/shard_map/reduce_scatter | solution.py:176
  606.1 88.5 %reduce-scatter.11.cloned.1.call-done = bf16[128,2,1024]{2,0,1:T(8,128)(2,1)} async-done(((bf16[1024,2,1024]{2,0,1:T(8,128)(2,1)}), bf16[128,2,1024]{2,0,1:T(8,128)(2,1)}) %reduce-scatter.11.cloned.1.call-update) | async-done | bytes 524304 | tf_op jit(solution)/shard_map/reduce_scatter | solution.py:176
  704.2 8.2 fusion.164
  712.4 11.8 add_convert_fusion.1
  725.8 10.9 fusion.148
  736.8 12.7 %add_convert_fusion = bf16[4096,1024]{1,0:T(8,128)(2,1)} fusion(f32[4096,1024]{1,0:T(8,128)} %fusion.148, f32[128,1024]{1,0:T(8,128)S(1)} %copy-done.51, f32[128,4096]{1,0:T(8,128)S(1)} %copy-done.46), kind=kOutput, calls=%fused_computation.44 | convolution fusion | flops 1116340224 | bytes 27787264 | tf_op jit(solution)/shard_map/dot_general | solution.py:19
  749.8 12.5 %reduce-scatter.19.cloned.1.call-done = bf16[256,1024]{1,0:T(8,128)(2,1)} async-done(((bf16[1024,1024]{1,0:T(8,128)(2,1)}), bf16[256,1024]{1,0:T(8,128)(2,1)}) %reduce-scatter.19.cloned.1.call-update) | async-done | bytes 524304 | tf_op jit(solution)/shard_map/reduce_scatter | solution.py:389
  762.4 34.4 %reduce-scatter.15.cloned.1.call-done = bf16[256,1024]{0,1:T(8,128)(2,1)} async-done(((bf16[1024,1024]{0,1:T(8,128)(2,1)}), bf16[256,1024]{0,1:T(8,128)(2,1)}) %reduce-scatter.15.cloned.1.call-update) | async-done | bytes 524304 | tf_op jit(solution)/shard_map/reduce_scatter | solution.py:389
  796.7 34.6 %reduce-scatter.17.cloned.1.call-done = bf16[256,1024]{0,1:T(8,128)(2,1)} async-done(((bf16[1024,1024]{0,1:T(8,128)(2,1)}), bf16[256,1024]{0,1:T(8,128)(2,1)}) %reduce-scatter.17.cloned.1.call-update) | async-done | bytes 524304 | tf_op jit(solution)/shard_map/reduce_scatter | solution.py:389
  831.3 74.2 %reduce-scatter.21.cloned.1.call-done = bf16[256,4096]{1,0:T(8,128)(2,1)} async-done(((bf16[1024,4096]{1,0:T(8,128)(2,1)}), bf16[256,4096]{1,0:T(8,128)(2,1)}) %reduce-scatter.21.cloned.1.call-update) | async-done | bytes 2097168 | tf_op jit(solution)/shard_map/reduce_scatter | solution.py:389
  905.5 74.4 %reduce-scatter.23.cloned.1.call-done = bf16[1024,1024]{1,0:T(8,128)(2,1)} async-done(((bf16[4096,1024]{1,0:T(8,128)(2,1)}), bf16[1024,1024]{1,0:T(8,128)(2,1)}) %reduce-scatter.23.cloned.1.call-update) | async-done | bytes 2097168 | tf_op jit(solution)/shard_map/reduce_scatter | solution.py:389
  990.0 11.3 all-reduce.11
  1002.0 23.1 %all-reduce.9 = (bf16[256]{0:T(256)(128)(2,1)S(1)}, bf16[256]{0:T(256)(128)(2,1)S(1)}, bf16[256]{0:T(256)(128)(2,1)S(1)}, bf16[256]{0:T(256)(128)(2,1)S(1)}, bf1...) all-reduce(bf16[256]{0:T(256)(128)(2,1)S(1)} %dynamic-slice.1, ...), channel_id=1, replica_groups=mesh['ctx'=8,'fsdp'=4] {'ctx'}, use_global_device_ids=true, to_apply=%region_43.44 | all-reduce | flops 3072 | bytes 12288 | tf_op jit(solution)/shard_map/psum | solution.py:391
  1037.3 164.1 %all-reduce.14.cloned.1.call-done = (bf16[256,1024]{0,1:T(8,128)(2,1)}, bf16[256,1024]{0,1:T(8,128)(2,1)}, bf16[256,1024]{0,1:T(8,128)(2,1)}, bf16[256,1024]{1,0...) async-done(((bf16[256,1024]{0,1:T(8,128)(2,1)}, bf16[256,1024]{0,1:T(8,128)(2,1)}, bf16[256,1024]{0,1:T(8,128)(2,1)}, bf16[256,1024]{1,0:T(8,128)(2,1)}, ...) | async-done | bytes 6291472 | tf_op jit(solution)/shard_map/psum | solution.py:391
  (456 shorter events, 250.0 us)
Async XLA Ops:
  7.2 27.7 %all-gather.27.cloned.1.call-start = ((), (), s32[]{:S(2)}) async-start(), calls=%async_computation.11 | async-start | bytes 2621440 | tf_op jit(solution)/shard_map/all_gather | solution.py:51
  7.9 51.2 %copy-start.13 = (bf16[2,1,128,1024]{3,2,1,0:T(8,128)(2,1)S(1)}, bf16[2,1,128,1024]{3,2,1,0:T(8,128)(2,1)}, u32[]{:S(2)}) copy-start(bf16[2,1,128,1024]{3,2,1,0:T(8,128)(2,1)} %param.22) | copy-start | bytes 1572868
  7.9 51.2 %all-gather.23.cloned.1.call-start = ((), (), s32[]{:S(2)}) async-start(), calls=%async_computation.9 | async-start | bytes 2621440 | tf_op jit(solution)/shard_map/all_gather | solution.py:50
  8.7 138.7 %all-gather.21.cloned.1.call-start = ((), (), s32[]{:S(2)}) async-start(), calls=%async_computation.8 | async-start | bytes 2621440 | tf_op jit(solution)/shard_map/all_gather | solution.py:49
  9.4 141.1 %all-gather.29.cloned.1.call-start = ((), (), s32[]{:S(2)}) async-start(), calls=%async_computation.12 | async-start | bytes 2359296 | tf_op jit(solution)/shard_map/all_gather | solution.py:73
  37.8 147.9 %all-gather.25.cloned.1.call-start = ((), (), s32[]{:S(2)}) async-start(), calls=%async_computation.10 | async-start | bytes 2359296 | tf_op jit(solution)/shard_map/all_gather | solution.py:72
  61.9 174.1 %all-gather.39.cloned.1.call-start = ((), (), s32[]{:S(2)}) async-start(), calls=%async_computation.17 | async-start | bytes 2359296 | tf_op jit(solution)/shard_map/all_gather | solution.py:73
  63.1 223.4 %all-gather.37.cloned.1.call-start = ((), (), s32[]{:S(2)}) async-start(), calls=%async_computation.16 | async-start | bytes 2359296 | tf_op jit(solution)/shard_map/all_gather | solution.py:72
  65.9 243.3 %all-gather.31.cloned.1.call-start = ((), (), s32[]{:S(2)}) async-start(), calls=%async_computation.13 | async-start | bytes 2621440 | tf_op jit(solution)/shard_map/all_gather | solution.py:52
  66.7 32.1 %copy-start.97 = (bf16[256]{0:T(256)(128)(2,1)S(1)}, bf16[256]{0:T(256)(128)(2,1)}, u32[]{:S(2)}) copy-start(bf16[256]{0:T(256)(128)(2,1)} %param.38) | copy-start | bytes 1540
  66.8 74.1 %copy-start.98 = (bf16[256]{0:T(256)(128)(2,1)S(1)}, bf16[256]{0:T(256)(128)(2,1)}, u32[]{:S(2)}) copy-start(bf16[256]{0:T(256)(128)(2,1)} %param.39) | copy-start | bytes 1540
  66.8 302.3 %all-gather.33.cloned.1.call-start = ((), (), s32[]{:S(2)}) async-start(), calls=%async_computation.14 | async-start | bytes 10485760 | tf_op jit(solution)/shard_map/all_gather | solution.py:53
  67.5 361.3 %all-gather.35.cloned.1.call-start = ((), (), s32[]{:S(2)}) async-start(), calls=%async_computation.15 | async-start | bytes 10485760 | tf_op jit(solution)/shard_map/all_gather | solution.py:54
  68.1 534.3 %reduce-scatter.9.cloned.1.call-start = ((), (), s32[]{:S(2)}) async-start(), calls=%async_computation.18 | async-start | bytes 4718592 | tf_op jit(solution)/shard_map/reduce_scatter | solution.py:176
  93.7 346.4 %copy-start.56 = (f32[4,1,256]{2,1,0:T(1,128)}, f32[4,1,256]{2,1,0:T(1,128)S(1)}, u32[]{:S(2)}) copy-start(f32[4,1,256]{2,1,0:T(1,128)S(1)} %convert_element_type.499) | copy-start | bytes 12292
  103.9 46.4 %copy-start.70 = (bf16[128]{0:T(256)(128)(2,1)}, bf16[128]{0:T(256)(128)(2,1)S(1)}, u32[]{:S(2)}) copy-start(bf16[128]{0:T(256)(128)(2,1)S(1)} %get-tuple-element.654) | copy-start | bytes 772
  103.9 46.4 %copy-start.72 = (bf16[128]{0:T(256)(128)(2,1)}, bf16[128]{0:T(256)(128)(2,1)S(1)}, u32[]{:S(2)}) copy-start(bf16[128]{0:T(256)(128)(2,1)S(1)} %get-tuple-element.702) | copy-start | bytes 772
  150.5 161.1 %copy-start.4 = (bf16[128,1024]{0,1:T(8,128)(2,1)}, bf16[128,1024]{0,1:T(8,128)(2,1)S(1)}, u32[]{:S(2)}) copy-start(bf16[128,1024]{0,1:T(8,128)(2,1)S(1)} %copy.100) | copy-start | bytes 786436
  198.6 110.6 %copy-start.31 = (f32[128,16,64]{0,2,1:T(8,128)}, f32[128,16,64]{0,2,1:T(8,128)S(1)}, u32[]{:S(2)}) copy-start(f32[128,16,64]{0,2,1:T(8,128)S(1)} %fusion.74) | copy-start | bytes 1572868
  311.3 159.6 %copy-start.15 = (f32[128,1024]{1,0:T(8,128)}, f32[128,1024]{1,0:T(8,128)S(1)}, u32[]{:S(2)}) copy-start(f32[128,1024]{1,0:T(8,128)S(1)} %get-tuple-element.470) | copy-start | bytes 1572868
  311.3 159.6 %copy-start.74 = (f32[128]{0:T(128)}, f32[128]{0:T(128)S(1)}, u32[]{:S(2)}) copy-start(f32[128]{0:T(128)S(1)} %broadcast_multiply_fusion.11) | copy-start | bytes 1540
  322.6 148.3 %copy-start.76 = (f32[128]{0:T(128)}, f32[128]{0:T(128)S(1)}, u32[]{:S(2)}) copy-start(f32[128]{0:T(128)S(1)} %add_rsqrt_fusion.3) | copy-start | bytes 1540
  514.3 180.3 %reduce-scatter.11.cloned.1.call-start = ((), (), s32[]{:S(2)}) async-start(), calls=%async_computation.19 | async-start | bytes 4718592 | tf_op jit(solution)/shard_map/reduce_scatter | solution.py:176
  558.1 191.7 %reduce-scatter.13.cloned.1.call-start = ((), (), s32[]{:S(2)}) async-start(), calls=%async_computation.20 | async-start | bytes 2621440 | tf_op jit(solution)/shard_map/reduce_scatter | solution.py:389
  562.4 199.9 %reduce-scatter.19.cloned.1.call-start = ((), (), s32[]{:S(2)}) async-start(), calls=%async_computation.23 | async-start | bytes 2621440 | tf_op jit(solution)/shard_map/reduce_scatter | solution.py:389
  566.3 230.4 %reduce-scatter.15.cloned.1.call-start = ((), (), s32[]{:S(2)}) async-start(), calls=%async_computation.21 | async-start | bytes 2621440 | tf_op jit(solution)/shard_map/reduce_scatter | solution.py:389
  699.0 132.4 %reduce-scatter.17.cloned.1.call-start = ((), (), s32[]{:S(2)}) async-start(), calls=%async_computation.22 | async-start | bytes 2621440 | tf_op jit(solution)/shard_map/reduce_scatter | solution.py:389
  702.8 202.7 %reduce-scatter.21.cloned.1.call-start = ((), (), s32[]{:S(2)}) async-start(), calls=%async_computation.24 | async-start | bytes 10485760 | tf_op jit(solution)/shard_map/reduce_scatter | solution.py:389
  724.3 255.6 %reduce-scatter.23.cloned.1.call-start = ((), (), s32[]{:S(2)}) async-start(), calls=%async_computation.25 | async-start | bytes 10485760 | tf_op jit(solution)/shard_map/reduce_scatter | solution.py:389
  749.5 451.9 %all-reduce.14.cloned.1.call-start = ((), (), s32[]{:S(2)}) async-start(), calls=%async_computation.26 | async-start | bytes 12582912 | tf_op jit(solution)/shard_map/psum | solution.py:391
  989.9 42.9 %copy-start.7 = (bf16[1024,1024]{1,0:T(8,128)(2,1)S(1)}, bf16[1024,1024]{1,0:T(8,128)(2,1)}, u32[]{:S(2)}) copy-start(bf16[1024,1024]{1,0:T(8,128)(2,1)} %all-gather.27.cloned.1.call-done) | copy-start | bytes 6291460
  989.9 42.9 %copy-start.41 = (bf16[128,2,1024]{2,0,1:T(8,128)(2,1)S(1)}, bf16[128,2,1024]{2,0,1:T(8,128)(2,1)}, u32[]{:S(2)}) copy-start(bf16[128,2,1024]{2,0,1:T(8,128)(2,1)} %reduce-scatter.11.cloned.1.call-done) | copy-start | bytes 1572868
  (95 other events, 505.9 us)
Sparse Core Ops, SparseCore 0:
  9.6 25.2 all-gather.26
  36.5 22.5 all-gather.22
  60.7 22.6 all-gather.20
  85.9 49.3 all-gather.28
  137.8 47.7 all-gather.24
  188.2 47.7 all-gather.38
  238.7 47.7 all-gather.36
  288.1 21.0 all-gather.30
  310.8 58.2 all-gather.32
  370.5 58.2 all-gather.34
  514.4 87.8 reduce-scatter.8
  606.9 87.6 reduce-scatter.10
  697.1 31.1 reduce-scatter.12
  730.9 31.4 reduce-scatter.18
  765.3 31.3 reduce-scatter.14
  799.8 31.4 reduce-scatter.16
  833.8 71.7 reduce-scatter.20
  908.1 71.6 reduce-scatter.22
  984.9 216.4 all-reduce.13
where the time goes:
time: 1230 us; the launch traced here: 1220 us
  waiting for transfers between devices  796 us (65%)
  matrix products  178 us (14%)
  blocking collectives  119 us (10%)
  local copies, waits for them, and re-layouts  74.1 us (6%)
  other arithmetic  32.8 us (3%)
  between operations  16.9 us (1%)
    reduce_scatter x6, waiting for transfers between devices, per_device(): lax.psum_scatter(as_sent(totals), 'fsdp', scatter_dimension=0, tiled=True)  230 us
    psum x1, waiting for transfers between devices, per_device(): lax.psum(as_sent(reduced), 'ctx')  164 us
    reduce_scatter x2, waiting for transfers between devices, attend_backward(): lax.psum_scatter(key_terms.astype(jnp.bfloat16), 'ctx', scatter_dimension...  125 us
    all_gather x2, waiting for transfers between devices, attend_forward(): key_rows = lax.all_gather(key_bf, 'ctx', axis=0, tiled=True)  77.7 us
    dot_general x12, matrix products, left_dot(): lax.dot_general(left_side, right_side, (((0,), (0,)), ((), ())), preferre...  60 us
    all_gather x1, waiting for transfers between devices, gather_weights(): lax.all_gather(shards[5], 'fsdp', axis=0, tiled=True)  53.6 us
    all_gather x1, waiting for transfers between devices, gather_weights(): lax.all_gather(shards[4], 'fsdp', axis=0, tiled=True)  46.4 us
    dot_general x12, matrix products, plain_dot(): return jnp.dot(left_side, right_side, preferred_element_type=jnp.float32)  37.6 us
  transfers between devices with their start and end apart: 19, of which 16 were waited for; matrix products, arithmetic and copies ran while one was open for 15% of the time, Pallas kernels for 0%

commit v1 on v0

--- a/solution.py
+++ b/solution.py
@@ -1,6 +1,8 @@
 import jax
 import jax.numpy as jnp
 from jax import lax
+from jax.experimental import pallas as pl
+from jax.experimental.pallas import tpu as pltpu
 from jax.sharding import PartitionSpec as P
 
 HEADS = 16
@@ -412,6 +414,773 @@
     )
 
 
+MESH = pl.DeviceIdType.MESH
+BF = jnp.bfloat16
+F32 = jnp.float32
+CHUNKS = 24
+SLOTS = 3
+
+
+def coords():
+    c, f = lax.axis_index("ctx"), lax.axis_index("fsdp")
+    return c // 2, c % 2, f // 2, f % 2
+
+
+def dev(z, x, y, k):
+    return (z * 2 + x, y * 2 + k)
+
+
+def greet(z, x, y, k):
+    barrier = pltpu.get_barrier_semaphore()
+    for step in range(1, 8):
+        place = (z * 2 + k + step) % 8
+        pl.semaphore_signal(
+            barrier, inc=1, device_id=dev(place // 2, x, y, place % 2), device_id_type=MESH
+        )
+    pl.semaphore_signal(barrier, inc=1, device_id=dev(z, 1 - x, y, k), device_id_type=MESH)
+    pl.semaphore_signal(barrier, inc=1, device_id=dev(z, x, 1 - y, k), device_id_type=MESH)
+    pl.semaphore_wait(barrier, 9)
+
+
+def remote(src, dst, send, recv, to):
+    return pltpu.make_async_remote_copy(
+        src_ref=src, dst_ref=dst, send_sem=send, recv_sem=recv, device_id=to, device_id_type=MESH
+    )
+
+
+def rows_of(start, size, unit=16):
+    return pl.ds(pl.multiple_of(start, unit), size)
+
+
+def gather_kernel(
+    inp, cot, seg, wq, wk, wv, wo, we, wc, vec,
+    xf, cotf, segf, fq, fk, fv, fo, fe, fc, vecf,
+    a_send, a_recv, g_send, g_recv, w_send, w_recv, v_send, v_recv,
+):
+    z, x, y, k = coords()
+    f = y * 2 + k
+    other = (1 - y) * 2 + k
+    sib, xn, yn = dev(z, x, y, 1 - k), dev(z, 1 - x, y, k), dev(z, x, 1 - y, k)
+    zn = dev(z + 1 - 2 * (z % 2), x, y, k)
+    color = (z % 2) * 2 + x
+    c_x, c_z, c_o = color + 1 - 2 * x, (color + 2) % 4, 3 - color
+    greet(z, x, y, k)
+
+    def block_moves(mb):
+        to_z, to_k = mb * 2 + k, z // 2
+        row = x * 512 + z * 128
+        slot = z % 2
+        mine = (to_z == z) & (to_k == k)
+        moves = (
+            (inp.at[mb, 0], xf.at[rows_of(row, 128)], 0),
+            (seg.at[mb], segf.at[x * 4 + z], 1),
+            (cot.at[mb, 0], cotf.at[rows_of(slot * 128, 128)], 2),
+        )
+        return mine, dev(to_z, x, y, to_k), slot, moves
+
+    def start_blocks(which):
+        for mb in range(2):
+            mine, to, slot, moves = block_moves(mb)
+            for src, dst, n in moves:
+                if n not in which:
+                    continue
+
+                @pl.when(mine)
+                def _():
+                    pltpu.make_async_copy(src, dst, a_recv.at[n, slot]).start()
+
+                @pl.when(jnp.logical_not(mine))
+                def _():
+                    remote(src, dst, a_send.at[n, mb], a_recv.at[n, slot], to).start()
+
+    def finish_blocks(which):
+        for mb in range(2):
+            mine, to, slot, moves = block_moves(mb)
+            for src, dst, n in moves:
+                if n not in which:
+                    continue
+
+                @pl.when(jnp.logical_not(mine))
+                def _():
+                    remote(src, dst, a_send.at[n, mb], a_recv.at[n, slot], to).wait_send()
+
+    def arrive_blocks(which):
+        for slot in range(2):
+            zz = 2 * k + slot
+            for n in which:
+                if n == 0:
+                    dst = xf.at[rows_of(x * 512 + zz * 128, 128)]
+                elif n == 1:
+                    dst = segf.at[x * 4 + zz]
+                else:
+                    dst = cotf.at[pl.ds(slot * 128, 128)]
+                pltpu.make_async_copy(dst, dst, a_recv.at[n, slot]).wait()
+
+    def group_copy(step):
+        who = x if step < 2 else 1 - x
+        src = xf.at[rows_of(who * 512 + k * 256, 256)]
+        sseg = segf.at[pl.ds(who * 4 + k * 2, 2)]
+        to = (sib, xn, sib)[step]
+        return (
+            remote(src, src, g_send.at[0, step], g_recv.at[0, step], to),
+            remote(sseg, sseg, g_send.at[1, step], g_recv.at[1, step], to),
+        )
+
+    def group_arrive(step):
+        who = (x, 1 - x, 1 - x)[step]
+        kk = (1 - k, k, 1 - k)[step]
+        src = xf.at[rows_of(who * 512 + kk * 256, 256)]
+        sseg = segf.at[pl.ds(who * 4 + kk * 2, 2)]
+        pltpu.make_async_copy(src, src, g_recv.at[0, step]).wait()
+        pltpu.make_async_copy(sseg, sseg, g_recv.at[1, step]).wait()
+
+    items = []
+    for shard, full in ((wq, fq), (wk, fk), (wv, fv), (wo, fo)):
+        items.append((shard, full, 0, 0, 256))
+    for j in range(4):
+        items.append((we, fe, 0, j * 1024, 256))
+    for j in range(4):
+        items.append((wc, fc, j * 256, 0, 1024))
+    n_items = len(items)
+
+    def part(i, quarter, start, size, own_src=False):
+        shard, full, row, col, step = items[i]
+        if own_src:
+            return shard.at[rows_of(row + start, size), pl.ds(col, 1024)]
+        return full.at[rows_of(quarter * step + row + start, size), pl.ds(col, 1024)]
+
+    def send_copy(i, kind):
+        sems = (w_send.at[kind, i], w_recv.at[kind, i])
+        if kind == 0:
+            return remote(part(i, f, color * 64, 64, True), part(i, f, color * 64, 64), *sems, yn)
+        if kind == 1:
+            return remote(part(i, f, c_o * 64, 32, True), part(i, f, c_o * 64, 32), *sems, yn)
+        if kind == 2:
+            src = part(i, other, color * 64, 64)
+            return remote(src, src, *sems, xn)
+        if kind == 3:
+            src = part(i, other, c_z * 64 + 32, 16)
+            return remote(src, src, *sems, xn)
+        if kind == 4:
+            src = part(i, other, color * 64, 64)
+            return remote(src, src, *sems, zn)
+        if kind == 5:
+            src = part(i, other, c_x * 64 + 48, 16)
+            return remote(src, src, *sems, zn)
+        if kind == 6:
+            return remote(part(i, f, 0, 256, True), part(i, f, 0, 256), *sems, sib)
+        src = part(i, other, 0, 256)
+        return remote(src, src, *sems, sib)
+
+    def arrive(i, kind):
+        if kind == 0:
+            dst = part(i, other, color * 64, 64)
+        elif kind == 1:
+            dst = part(i, other, c_o * 64, 32)
+        elif kind == 2:
+            dst = part(i, other, c_x * 64, 64)
+        elif kind == 3:
+            dst = part(i, other, c_o * 64 + 32, 16)
+        elif kind == 4:
+            dst = part(i, other, c_z * 64, 64)
+        elif kind == 5:
+            dst = part(i, other, c_o * 64 + 48, 16)
+        elif kind == 6:
+            dst = part(i, y * 2 + 1 - k, 0, 256)
+        else:
+            dst = part(i, (1 - y) * 2 + 1 - k, 0, 256)
+        pltpu.make_async_copy(dst, dst, w_recv.at[kind, i]).wait()
+
+    def own_copy(i):
+        return pltpu.make_async_copy(
+            part(i, f, 0, 256, True), part(i, f, 0, 256), w_recv.at[8, i]
+        )
+
+    vec_copies = (
+        remote(vec, vecf.at[f], v_send.at[0], v_recv.at[0], yn),
+        remote(vec, vecf.at[f], v_send.at[1], v_recv.at[1], sib),
+        remote(vecf.at[other], vecf.at[other], v_send.at[2], v_recv.at[2], sib),
+    )
+    vec_own = pltpu.make_async_copy(vec, vecf.at[f], v_recv.at[3])
+
+    start_blocks((0, 1))
+    vec_own.start()
+    vec_copies[0].start()
+    vec_copies[1].start()
+    for t in range(n_items + 3):
+        if t < n_items:
+            send_copy(t, 0).start()
+            send_copy(t, 1).start()
+            send_copy(t, 6).start()
+            own_copy(t).start()
+        if t == 1:
+            arrive_blocks((0, 1))
+            for step in range(2):
+                for move in group_copy(step):
+                    move.start()
+            pltpu.make_async_copy(vecf.at[other], vecf.at[other], v_recv.at[0]).wait()
+            vec_copies[2].start()
+        if t == 4:
+            group_arrive(1)
+            for move in group_copy(2):
+                move.start()
+            start_blocks((2,))
+        if 1 <= t <= n_items:
+            i = t - 1
+            arrive(i, 0)
+            send_copy(i, 2).start()
+            send_copy(i, 4).start()
+        if 2 <= t <= n_items + 1:
+            i = t - 2
+            arrive(i, 4)
+            send_copy(i, 3).start()
+            arrive(i, 2)
+            send_copy(i, 5).start()
+        if 3 <= t:
+            i = t - 3
+            arrive(i, 1)
+            arrive(i, 3)
+            arrive(i, 5)
+            send_copy(i, 7).start()
+    for i in range(n_items):
+        arrive(i, 6)
+        arrive(i, 7)
+        own_copy(i).wait()
+        for kind in range(8):
+            send_copy(i, kind).wait_send()
+    arrive_blocks((2,))
+    finish_blocks((0, 1, 2))
+    group_arrive(0)
+    group_arrive(2)
+    for step in range(3):
+        for move in group_copy(step):
+            move.wait_send()
+    sib_own, sib_other = vecf.at[y * 2 + 1 - k], vecf.at[(1 - y) * 2 + 1 - k]
+    pltpu.make_async_copy(sib_own, sib_own, v_recv.at[1]).wait()
+    pltpu.make_async_copy(sib_other, sib_other, v_recv.at[2]).wait()
+    for move in vec_copies:
+        move.wait_send()
+    vec_own.wait()
+
+
+def gather_call(inp, cot, seg, weights, vec):
+    any_spec = pl.BlockSpec(memory_space=pl.ANY)
+    outs = [
+        jax.ShapeDtypeStruct((1024, 1024), BF),
+        jax.ShapeDtypeStruct((256, 1024), BF),
+        jax.ShapeDtypeStruct((8, 1, 128), jnp.int32),
+    ]
+    outs += [jax.ShapeDtypeStruct((1024, 1024), BF)] * 4
+    outs += [
+        jax.ShapeDtypeStruct((1024, 4096), BF),
+        jax.ShapeDtypeStruct((4096, 1024), BF),
+        jax.ShapeDtypeStruct((4, 32, 128), BF),
+    ]
+    dma = pltpu.SemaphoreType.DMA
+    return pl.pallas_call(
+        gather_kernel,
+        out_shape=outs,
+        in_specs=[any_spec] * 10,
+        out_specs=[any_spec] * 10,
+        scratch_shapes=[
+            dma((3, 2)), dma((3, 2)), dma((2, 3)), dma((2, 3)),
+            dma((8, 12)), dma((9, 12)), dma((3,)), dma((4,)),
+        ],
+        compiler_params=pltpu.CompilerParams(collective_id=0, has_side_effects=True),
+        name="gather_all",
+    )(inp, cot, seg, *weights, vec)
+
+
+def two_heads(block):
+    lane = lax.broadcasted_iota(jnp.int32, block.shape, 1)
+    zero = jnp.zeros_like(block)
+    return jnp.concatenate(
+        [jnp.where(lane < HEAD_DIM, block, zero), jnp.where(lane >= HEAD_DIM, block, zero)], axis=0
+    )
+
+
+def one_block(pair):
+    rows = pair.shape[0] // 2
+    lane = lax.broadcasted_iota(jnp.int32, (rows, pair.shape[1]), 1)
+    return jnp.where(lane < HEAD_DIM, pair[:rows], pair[rows:])
+
+
+def softmax_pair(q_ref, k_ref, same_ref):
+    queries = two_heads(q_ref[...] * BF(HEAD_DIM**-0.5))
+    scores = right_dot(queries, k_ref[...])
+    same = same_ref[...]
+    scores = jnp.where(jnp.concatenate([same, same], axis=0) > 0, scores, -1e30)
+    numer = jnp.exp(scores - jnp.max(scores, axis=-1, keepdims=True))
+    return queries, numer * (1.0 / jnp.sum(numer, axis=-1, keepdims=True))
+
+
+def attend_kernel(q_ref, k_ref, v_ref, sq_ref, sk_ref, o_ref, same_ref):
+    @pl.when(pl.program_id(0) == 0)
+    def _():
+        same_ref[...] = (sq_ref[...] == sk_ref[...]).astype(F32)
+
+    probs = softmax_pair(q_ref, k_ref, same_ref)[1]
+    o_ref[...] = one_block(plain_dot(probs.astype(BF), v_ref[...])).astype(BF)
+
+
+def attend_back_kernel(
+    q_ref, k_ref, v_ref, g_ref, sq_ref, sk_ref, dq_ref, dk_ref, dv_ref, same_ref
+):
+    @pl.when(pl.program_id(0) == 0)
+    def _():
+        same_ref[...] = (sq_ref[...] == sk_ref[...]).astype(F32)
+
+    queries, probs = softmax_pair(q_ref, k_ref, same_ref)
+    grads = two_heads(g_ref[...])
+    grad_probs = right_dot(grads, v_ref[...])
+    delta = jnp.sum(probs * grad_probs, axis=-1, keepdims=True)
+    grad_scores = (probs * (grad_probs - delta)).astype(BF)
+    dv_ref[...] = left_dot(probs.astype(BF), grads).astype(BF)
+    dk_ref[...] = left_dot(grad_scores, queries).astype(BF)
+    dq = one_block(plain_dot(grad_scores, k_ref[...]))
+    dq_ref[...] = (dq * HEAD_DIM**-0.5).astype(BF)
+
+
+def attention_specs():
+    rows = pl.BlockSpec((256, 128), lambda h: (0, h))
+    full = pl.BlockSpec((1024, 128), lambda h: (0, h))
+    sq = pl.BlockSpec((256, 1), lambda h: (0, 0))
+    sk = pl.BlockSpec((1, 1024), lambda h: (0, 0))
+    return rows, full, sq, sk
+
+
+def attend(q, k, v, sq, sk):
+    rows, full, sqs, sks = attention_specs()
+    return pl.pallas_call(
+        attend_kernel,
+        grid=(8,),
+        out_shape=jax.ShapeDtypeStruct((256, 1024), BF),
+        in_specs=[rows, full, full, sqs, sks],
+        out_specs=rows,
+        scratch_shapes=[pltpu.VMEM((256, 1024), F32)],
+        compiler_params=pltpu.CompilerParams(vmem_limit_bytes=40 << 20),
+        name="attend",
+    )(q, k, v, sq, sk)
+
+
+def attend_back(q, k, v, g, sq, sk):
+    rows, full, sqs, sks = attention_specs()
+    return pl.pallas_call(
+        attend_back_kernel,
+        grid=(8,),
+        out_shape=[
+            jax.ShapeDtypeStruct((256, 1024), BF),
+            jax.ShapeDtypeStruct((1024, 1024), BF),
+            jax.ShapeDtypeStruct((1024, 1024), BF),
+        ],
+        in_specs=[rows, full, full, rows, sqs, sks],
+        out_specs=[rows, full, full],
+        scratch_shapes=[pltpu.VMEM((256, 1024), F32)],
+        compiler_params=pltpu.CompilerParams(vmem_limit_bytes=40 << 20),
+        name="attend_back",
+    )(q, k, v, g, sq, sk)
+
+
+def reduce_kernel(
+    gel, gb, fb, gh, ctx, gal, xo, dq, xf, dk, dv, dxo, dxp, res,
+    out, resf, dxf,
+    s_d, l_d, r_d, b_y, r_y, b_x, r_x, b_1, r_1, b_2, r_2,
+    dx_r, dx_s, dx_y, dx_b,
+    ss, rs, ds, dr, a_send, a_recv,
+):
+    z, x, y, k = coords()
+    sib, xn, yn = dev(z, x, y, 1 - k), dev(z, 1 - x, y, k), dev(z, x, 1 - y, k)
+    bit1, bit2 = z % 2, z // 2
+    z1 = dev(z + 1 - 2 * bit1, x, y, k)
+    z2 = dev((z + 2) % 4, x, y, k)
+    greet(z, x, y, k)
+
+    def back(n, slot):
+        to_z = 2 * k + slot
+        to_k = z % 2
+        mb = z // 2
+        mine = (to_z == z) & (to_k == k)
+        src = (res, dx_b)[n].at[pl.ds(slot * 128, 128)]
+        dst = (resf, dxf)[n].at[mb, 0]
+
+        def far():
+            return remote(
+                src, dst, a_send.at[n, slot], a_recv.at[n, mb], dev(to_z, x, y, to_k)
+            )
+
+        def near():
+            return pltpu.make_async_copy(src, dst, a_recv.at[n, mb])
+
+        return mine, far, near
+
+    def start_back(n):
+        for slot in range(2):
+            mine, far, near = back(n, slot)
+
+            @pl.when(mine)
+            def _():
+                near().start()
+
+            @pl.when(jnp.logical_not(mine))
+            def _():
+                far().start()
+
+    def finish_back(n):
+        for slot in range(2):
+            mine, far, _ = back(n, slot)
+
+            @pl.when(jnp.logical_not(mine))
+            def _():
+                far().wait_send()
+
+        for mb in range(2):
+            dst = (resf, dxf)[n].at[mb, 0]
+            pltpu.make_async_copy(dst, dst, a_recv.at[n, mb]).wait()
+
+    start_back(0)
+
+    def dx_core(g):
+        who = x if g == 0 else 1 - x
+        src = dxp.at[rows_of(who * 512 + (1 - k) * 256, 256)]
+        return remote(src, dx_r.at[g], ds.at[g], dr.at[g], sib)
+
+    dx_far = remote(dx_s, dx_y, ds.at[2], dr.at[2], xn)
+    dx_core(1).start()
+    dx_core(0).start()
+
+    def send(stage, i, src, dst, to):
+        return remote(src, dst, ss.at[stage, i % SLOTS], rs.at[stage, i], to)
+
+    def landed(stage, i, dst):
+        pltpu.make_async_copy(dst, dst, rs.at[stage, i]).wait()
+
+    def copies(stage, i):
+        slot = i % SLOTS
+        if stage == 0:
+            return send(0, i, s_d.at[slot], r_d.at[i], sib)
+        if stage == 1:
+            return send(1, i, b_y.at[slot, 1 - y], r_y.at[i], yn)
+        if stage == 2:
+            return send(2, i, b_x.at[slot, rows_of((1 - x) * 64, 64)], r_x.at[i], xn)
+        if stage == 3:
+            return send(3, i, b_1.at[slot, rows_of((1 - bit1) * 32, 32)], r_1.at[i], z1)
+        if stage == 4:
+            return send(4, i, b_2.at[slot, rows_of((1 - bit2) * 16, 16)], r_2.at[i], z2)
+        if stage == 5:
+            own = out.at[i, rows_of(x * 64 + bit1 * 32 + bit2 * 16, 16)]
+            return send(5, i, own, own, z2)
+        if stage == 6:
+            own = out.at[i, rows_of(x * 64 + bit1 * 32, 32)]
+            return send(6, i, own, own, z1)
+        own = out.at[i, rows_of(x * 64, 64)]
+        return send(7, i, own, own, xn)
+
+    def launch(stage, i):
+        copies(stage, i).start()
+
+    def clear(stage, i):
+        @pl.when(i >= SLOTS)
+        def _():
+            copies(stage, i - SLOTS).wait_send()
+
+    def add(a, b):
+        return (a.astype(F32) + b.astype(F32)).astype(BF)
+
+    def terms(i, a_ref, b_ref, a_base, a_step, b_col):
+        slot = i % SLOTS
+        right = b_ref[:, b_col]
+        for plane in range(2):
+            for core in range(2):
+                quarter = plane * 2 + (k if core == 0 else 1 - k)
+                left = a_ref[:, pl.ds(pl.multiple_of(a_base + quarter * a_step, 128), 128)]
+                product = left_dot(left, right).astype(BF)
+                if core == 0:
+                    l_d[slot, plane] = product
+                else:
+                    s_d[slot, plane] = product
+
+    every = pl.ds(0, 1024)
+
+    def tick(t, carry):
+        def at(stage):
+            i = t - stage
+            return i, (i >= 0) & (i < CHUNKS)
+
+        i0, live0 = at(0)
+
+        @pl.when(live0)
+        def _():
+            clear(0, i0)
+
+        @pl.when(i0 < 8)
+        def _():
+            terms(i0, gel, gb, i0 * 128, 1024, every)
+
+        @pl.when((i0 >= 8) & (i0 < 16))
+        def _():
+            j = i0 - 8
+            terms(i0, fb, gh, (j % 2) * 128, 256, rows_of((j // 2) * 1024, 1024, 1024))
+
+        @pl.when((i0 >= 16) & (i0 < 18))
+        def _():
+            terms(i0, ctx, gal, (i0 - 16) * 128, 256, every)
+
+        @pl.when((i0 >= 18) & (i0 < 20))
+        def _():
+            terms(i0, xo, dq, (i0 - 18) * 128, 256, every)
+
+        @pl.when((i0 >= 20) & (i0 < 22))
+        def _():
+            terms(i0, xf, dk, (i0 - 20) * 128, 256, every)
+
+        @pl.when((i0 >= 22) & (i0 < 24))
+        def _():
+            terms(i0, xf, dv, (i0 - 22) * 128, 256, every)
+
+        @pl.when(live0)
+        def _():
+            launch(0, i0)
+
+        i1, live1 = at(1)
+
+        @pl.when(live1)
+        def _():
+            slot = i1 % SLOTS
+            clear(1, i1)
+            landed(0, i1, r_d.at[i1])
+            for plane in range(2):
+                b_y[slot, plane] = add(l_d[slot, plane], r_d[i1, plane])
+            launch(1, i1)
+
+        i2, live2 = at(2)
+
+        @pl.when(live2)
+        def _():
+            slot = i2 % SLOTS
+            clear(2, i2)
+            landed(1, i2, r_y.at[i2])
+            b_x[slot] = add(b_y[slot, y], r_y[i2])
+            launch(2, i2)
+
+        i3, live3 = at(3)
+
+        @pl.when(live3)
+        def _():
+            slot = i3 % SLOTS
+            clear(3, i3)
+            landed(2, i3, r_x.at[i3])
+            b_1[slot] = add(b_x[slot, rows_of(x * 64, 64)], r_x[i3])
+            launch(3, i3)
+
+        i4, live4 = at(4)
+
+        @pl.when(live4)
+        def _():
+            slot = i4 % SLOTS
+            clear(4, i4)
+            landed(3, i4, r_1.at[i4])
+            b_2[slot] = add(b_1[slot, rows_of(bit1 * 32, 32)], r_1[i4])
+            launch(4, i4)
+
+        i5, live5 = at(5)
+
+        @pl.when(live5)
+        def _():
+            slot = i5 % SLOTS
+            clear(5, i5)
+            landed(4, i5, r_2.at[i5])
+            out[i5, rows_of(x * 64 + bit1 * 32 + bit2 * 16, 16)] = add(
+                b_2[slot, rows_of(bit2 * 16, 16)], r_2[i5]
+            )
+            launch(5, i5)
+
+        i6, live6 = at(6)
+
+        @pl.when(live6)
+        def _():
+            clear(6, i6)
+            landed(5, i6, out.at[i6, rows_of(x * 64 + bit1 * 32 + (1 - bit2) * 16, 16)])
+            launch(6, i6)
+
+        i7, live7 = at(7)
+
+        @pl.when(live7)
+        def _():
+            clear(7, i7)
+            landed(6, i7, out.at[i7, rows_of(x * 64 + (1 - bit1) * 32, 32)])
+            launch(7, i7)
+
+        i8, live8 = at(8)
+
+        @pl.when(live8)
+        def _():
+            landed(7, i8, out.at[i8, rows_of((1 - x) * 64, 64)])
+
+        @pl.when(t == 1)
+        def _():
+            pltpu.make_async_copy(dx_r.at[1], dx_r.at[1], dr.at[1]).wait()
+            dx_s[...] = add(dxp[rows_of((1 - x) * 512 + k * 256, 256)], dx_r[1])
+            dx_far.start()
+
+        @pl.when(t == 5)
+        def _():
+            pltpu.make_async_copy(dx_r.at[0], dx_r.at[0], dr.at[0]).wait()
+            pltpu.make_async_copy(dx_y, dx_y, dr.at[2]).wait()
+            dx_b[...] = (dxo[...] + dx_r[0].astype(F32) + dx_y[...].astype(F32)).astype(BF)
+            start_back(1)
+
+        return carry
+
+    lax.fori_loop(0, CHUNKS + 8, tick, 0)
+    for stage in range(8):
+        for i in range(CHUNKS - SLOTS, CHUNKS):
+            copies(stage, i).wait_send()
+    dx_core(0).wait_send()
+    dx_core(1).wait_send()
+    dx_far.wait_send()
+    finish_back(0)
+    finish_back(1)
+
+
+def reduce_call(*operands):
+    vmem = pl.BlockSpec(memory_space=pltpu.VMEM)
+    any_spec = pl.BlockSpec(memory_space=pl.ANY)
+    dma = pltpu.SemaphoreType.DMA
+    return pl.pallas_call(
+        reduce_kernel,
+        out_shape=[
+            jax.ShapeDtypeStruct((CHUNKS, 128, 1024), BF),
+            jax.ShapeDtypeStruct((2, 1, 128, 1024), BF),
+            jax.ShapeDtypeStruct((2, 1, 128, 1024), BF),
+        ],
+        in_specs=[vmem] * 14,
+        out_specs=[vmem, any_spec, any_spec],
+        scratch_shapes=[
+            pltpu.VMEM((SLOTS, 2, 128, 1024), BF),
+            pltpu.VMEM((SLOTS, 2, 128, 1024), BF),
+            pltpu.VMEM((CHUNKS, 2, 128, 1024), BF),
+            pltpu.VMEM((SLOTS, 2, 128, 1024), BF),
+            pltpu.VMEM((CHUNKS, 128, 1024), BF),
+            pltpu.VMEM((SLOTS, 128, 1024), BF),
+            pltpu.VMEM((CHUNKS, 64, 1024), BF),
+            pltpu.VMEM((SLOTS, 64, 1024), BF),
+            pltpu.VMEM((CHUNKS, 32, 1024), BF),
+            pltpu.VMEM((SLOTS, 32, 1024), BF),
+            pltpu.VMEM((CHUNKS, 16, 1024), BF),
+            pltpu.VMEM((2, 256, 1024), BF),
+            pltpu.VMEM((256, 1024), BF),
+            pltpu.VMEM((256, 1024), BF),
+            pltpu.VMEM((256, 1024), BF),
+            dma((8, SLOTS)), dma((8, CHUNKS)), dma((3,)), dma((3,)), dma((2, 2)), dma((2, 2)),
+        ],
+        compiler_params=pltpu.CompilerParams(
+            collective_id=1, has_side_effects=True, vmem_limit_bytes=61 << 20
+        ),
+        name="reduce_all",
+    )(*operands)
+
+
+def per_group_device(
+    layer_input, segments, cotangent,
+    query_weight, key_weight, value_weight, output_weight, expand_weight, contract_weight,
+    query_bias, value_bias, output_bias, first_gain, first_shift, expand_bias, contract_bias,
+    second_gain, second_shift,
+):
+    weights = (
+        query_weight, key_weight, value_weight, output_weight, expand_weight, contract_weight
+    )
+    packed = jnp.concatenate(
+        [
+            query_bias, value_bias, output_bias, first_gain, first_shift, contract_bias,
+            second_gain, second_shift, expand_bias, jnp.zeros((1024,), BF),
+        ]
+    ).reshape(32, 128)
+    xf, cot, seg, wq, wk, wv, wo, we, wc, vecs = gather_call(
+        layer_input, cotangent, segments, weights, packed
+    )
+    small = [vecs[:, 2 * i : 2 * i + 2].reshape(1024).astype(F32) for i in range(8)]
+    bq, bv, bo, gain_one, shift_one, bc, gain_two, shift_two = small
+    be = vecs[:, 16:24].reshape(4096).astype(F32)
+    z, x, y, k = coords()
+    own = x * 512 + k * 256
+    xo = lax.dynamic_slice_in_dim(xf, own, 256, 0)
+    sk = seg.reshape(1, 1024)
+    sq = lax.dynamic_slice_in_dim(seg, x * 4 + k * 2, 2, 0).reshape(256, 1)
+
+    q = (plain_dot(xo, wq) + bq).astype(BF)
+    key = plain_dot(xf, wk).astype(BF)
+    val = (plain_dot(xf, wv) + bv).astype(BF)
+    ctx = attend(q, key, val, sq, sk)
+    first_sum = xo.astype(F32) + plain_dot(ctx, wo) + bo
+    first_out, normed_one, inverse_one = norm_forward(first_sum, gain_one, shift_one)
+    first_bf = first_out.astype(BF)
+    hidden = plain_dot(first_bf, we) + be
+    gelled = jax.nn.gelu(hidden, approximate=False).astype(BF)
+    second_sum = first_out + plain_dot(gelled, wc) + bc
+    result, normed_two, inverse_two = norm_forward(second_sum, gain_two, shift_two)
+    grad_out = cot.astype(F32)
+    grad_second, gain_two_grad, shift_two_grad = norm_backward(
+        grad_out, normed_two, inverse_two, gain_two
+    )
+    gb = grad_second.astype(BF)
+    grad_gelled = right_dot(gb, wc)
+    gelu_pull = jax.vjp(lambda values: jax.nn.gelu(values, approximate=False), hidden)[1]
+    gh = gelu_pull(grad_gelled)[0].astype(BF)
+    grad_first = grad_second + right_dot(gh, we)
+    grad_attn, gain_one_grad, shift_one_grad = norm_backward(
+        grad_first, normed_one, inverse_one, gain_one
+    )
+    gal = grad_attn.astype(BF)
+    grad_ctx = right_dot(gal, wo).astype(BF)
+    dq, dk, dv = attend_back(q, key, val, grad_ctx, sq, sk)
+    dxp = right_dot(dk, wk) + right_dot(dv, wv)
+    dxo = grad_attn + right_dot(dq, wq) + lax.dynamic_slice_in_dim(dxp, own, 256, 0)
+
+    def column(v):
+        return jnp.sum(v.astype(F32), axis=0)
+
+    terms = [
+        column(dq), column(dv), column(gal), gain_one_grad, shift_one_grad, column(gb),
+        gain_two_grad, shift_two_grad,
+    ]
+    sums = jnp.concatenate(
+        [v.reshape(4, 256) for v in terms] + [column(gh).reshape(4, 1024)], axis=1
+    )
+    sums = lax.psum(sums, ("ctx", "fsdp"))
+    mine = lax.dynamic_slice_in_dim(sums, y * 2 + k, 1, 0)[0]
+    vec_grads = [mine[i * 256 : (i + 1) * 256] for i in range(8)]
+
+    out, resf, dxf = reduce_call(
+        gelled, gb, first_bf, gh, ctx, gal, xo, dq, xf, dk, dv, dxo, dxp.astype(BF),
+        result.astype(BF),
+    )
+    grads = out.astype(F32)
+
+    def square(start):
+        return grads[start : start + 2].reshape(256, 1024)
+
+    expand_grad = grads[8:16].reshape(4, 256, 1024).transpose(1, 0, 2).reshape(256, 4096)
+    return (
+        resf,
+        dxf.astype(F32),
+        square(18),
+        square(20),
+        square(22),
+        square(16),
+        expand_grad,
+        grads[0:8].reshape(1024, 1024),
+        vec_grads[0],
+        vec_grads[1],
+        vec_grads[2],
+        vec_grads[3],
+        vec_grads[4],
+        mine[2048:],
+        vec_grads[5],
+        vec_grads[6],
+        vec_grads[7],
+    )
+
+
 def solution(mesh):
     in_specs = (
         P(None, "fsdp", "ctx", None),
@@ -452,6 +1221,15 @@
         P("fsdp"),
         P("fsdp"),
     )
-    return jax.shard_map(
-        per_device, mesh=mesh, in_specs=in_specs, out_specs=out_specs, check_vma=False
-    )
+    def whole(layer_input, segments, *rest):
+        grouped = (
+            dict(mesh.shape) == {"ctx": 8, "fsdp": 4}
+            and layer_input.shape == (2, 4, 1024, 1024)
+            and rest[5].shape == (1024, 4096)
+        )
+        body = per_group_device if grouped else per_device
+        return jax.shard_map(
+            body, mesh=mesh, in_specs=in_specs, out_specs=out_specs, check_vma=False
+        )(layer_input, segments, *rest)
+
+    return whole

time: 1230 us -> 573 us (0.47)
  waiting for transfers between devices: 796 us -> 0 us
  Pallas kernels: 0 us -> 437 us
  matrix products: 178 us -> 54.3 us
  blocking collectives: 119 us -> 38.5 us
  local copies, waits for them, and re-layouts: 74.1 us -> 27 us
  other arithmetic: 32.8 us -> 6.68 us
  between operations: 16.9 us -> 1.72 us
    pallas_call x0 -> x4, Pallas kernels: none -> 437 us  [the longest x1 215 us: gather_call(): pl.pallas_call(gather_kernel, out_shape=outs, in_specs=[any_spec] * 10, o...]
    reduce_scatter x8 -> x0, waiting for transfers between devices: 355 us -> none  [the longest x6 230 us: per_device(): lax.psum_scatter(as_sent(totals), 'fsdp', scatter_dimension=0, tiled=True)]
    all_gather x10 -> x0, waiting for transfers between devices: 273 us -> none  [the longest x2 77.7 us: attend_forward(): key_rows = lax.all_gather(key_bf, 'ctx', axis=0, tiled=True)]
    psum x1 -> x0, waiting for transfers between devices: 164 us -> none  [per_device(): lax.psum(as_sent(reduced), 'ctx')]
    dot_general x36 -> x0, matrix products: 104 us -> none  [the longest x12 60 us: left_dot(): lax.dot_general(left_side, right_side, (((0,), (0,)), ((), ())), preferre...]
    all_gather x11 -> x0, blocking collectives: 84.1 us -> none  [the longest x2 36.9 us: attend_forward(): key_seg = lax.all_gather(seg_local, 'ctx', axis=0, tiled=True)]
    dynamic_update_slice x8 -> x0, local copies, waits for them, and re-layouts: 18 us -> none  [attend_backward(): lax.scan(visit_block, jnp.zeros((row_count, HEADS, HEAD_DIM), jnp.float32...]
    all_gather x4 -> x0, local copies, waits for them, and re-layouts: 15.8 us -> none  [the longest x2 7.96 us: attend_forward(): value_rows = lax.all_gather(value_bf, 'ctx', axis=0, tiled=True)]
  transfers between devices with their start and end apart: 19 -> 0, of which waited for: 16 -> 0; matrix products, arithmetic and copies ran while one was open for 15% -> 0% of each run, Pallas kernels for 0% -> 0%
where the time goes in v1:
time: 573 us; the launch traced here: 565 us
  Pallas kernels  437 us (76%)
  matrix products  54.3 us (9%)
  blocking collectives  38.5 us (7%)
  local copies, waits for them, and re-layouts  27 us (5%)
  other arithmetic  6.68 us (1%)
    pallas_call x1, Pallas kernels, gather_call(): pl.pallas_call(gather_kernel, out_shape=outs, in_specs=[any_spec] * 10, o...  215 us
    pallas_call x1, Pallas kernels, reduce_call(): pl.pallas_call(reduce_kernel, out_shape=[jax.ShapeDtypeStruct((CHUNKS, 12...  185 us
    psum x1, blocking collectives, per_group_device(): sums = lax.psum(sums, ('ctx', 'fsdp'))  38.5 us
    dot_general x6, matrix products, right_dot(): lax.dot_general(left_side, right_side, (((1,), (1,)), ((), ())), preferre...  29.1 us
    dot_general x6, matrix products, plain_dot(): return jnp.dot(left_side, right_side, preferred_element_type=jnp.float32)  25.2 us
    pallas_call x1, Pallas kernels, attend_back(): pl.pallas_call(attend_back_kernel, grid=(8,), out_shape=[jax.ShapeDtypeSt...  20.9 us
    pallas_call x1, Pallas kernels, attend(): pl.pallas_call(attend_kernel, grid=(8,), out_shape=jax.ShapeDtypeStruct((...  15.5 us
    unnamed x74, local copies, waits for them, and re-layouts  13.4 us

profile of v1, /device:TPU:0, one launch (start us, length us, event | category | flops | bytes accessed | tf_op | source)
XLA Modules:
  0.0 565.2 jit_solution(15632354477497053626)
XLA Ops:
  0.7 0.9 dynamic-update-slice.9
  1.5 0.8 dynamic-update-slice.10
  2.4 0.8 dynamic-update-slice.11
  3.2 0.8 dynamic-update-slice.12
  4.0 0.8 dynamic-update-slice.13
  8.7 215.0 %gather_all.1 = (bf16[1024,1024]{1,0:T(8,128)(2,1)}, bf16[256,1024]{1,0:T(8,128)(2,1)}, s32[8,1,128]{2,1,0:T(1,128)}, bf16[1024,1024]{1,0:T(8,128)(2,1)}, bf16[1...) custom-call(bf16[2,1,128,1024]{3,2,1,0:T(8,128)(2,1)} %inp.1, ...), custom_call_target="tpu_custom_call" | custom-call | tf_op jit(solution)/shard_map/gather_all/pallas_call | solution.py:680
  223.7 1.2 constant_dynamic-slice_fusion.1.xo
  225.0 1.0 fusion.24
  226.0 2.3 fusion.12.q_ref
  228.6 4.1 add_convert_fusion.1.v_ref
  232.7 2.3 convolution_convert_fusion.k_ref
  235.0 15.5 %attend.1.ctx = bf16[256,1024]{1,0:T(8,128)(2,1)S(1)} custom-call(bf16[256,1024]{1,0:T(8,128)(2,1)S(1)} %fusion.12.q_ref, bf16[1024,1024]{1,0:T(8,128)(2,1)S(1)} %convolution_convert_fusion.k_ref, bf16[1024,1024]{1,0:T(8,128)(2,1)S(1)} %add_convert_fusion.1.v_ref, s32[256,1]{1,0:T(8,128)S(1)} %copy.36.sq_ref, s32[1,1024]{1,0:T(1,128)S(1)} %bitcast.66), custom_call_target="tpu_custom_call" | custom-call | tf_op jit(solution)/shard_map/attend/pallas_call | solution.py:754
  252.0 1.2 bitcast_convert_fusion
  253.2 13.0 %multiply_convert_fusion = (bf16[256,4096]{1,0:T(8,128)(2,1)S(1)}, f32[256,4096]{1,0:T(8,128)}, f32[256,4096]{1,0:T(8,128)}) fusion(f32[4096]{0:T(1024)S(1)} %bitcast_convert_fusion, bf16[256,1024]{1,0:T(8,128)(2,1)S(1)} %fusion.17.fb, bf16[1024,4096]{1,0:T(8,128)(2,1)S(1)} %bitcast.94), kind=kOutput, calls=%fused_computation.6 | convolution fusion | flops 2216689664 | bytes 19415040 | tf_op jit(solution)/shard_map/dot_general | solution.py:17
  266.3 2.6 fusion.26
  269.7 1.3 convert_reduce_fusion.3
  271.0 11.9 %convert_reduce_fusion = (f32[4096]{0:T(1024)S(1)}, bf16[256,4096]{1,0:T(8,128)(2,1)S(1)}) fusion(f32[256,4096]{1,0:T(8,128)} %get-tuple-element.65, f32[256,4096]{1,0:T(8,128)} %get-tuple-element.91, bf16[256,1024]{1,0:T(8,128)(2,1)S(1)} %get-tuple-element.60.gb, bf16[4096,1024]{1,0:T(8,128)(2,1)} %get-tuple-element.41), kind=kOutput, calls=%fused_computation.3 | convolution fusion | flops 2164256768 | bytes 19415040 | tf_op jit(solution)/shard_map/dot_general | solution.py:27
  282.9 1.3 copy-done.12
  284.2 6.3 %multiply_reduce_fusion = (f32[1024]{0:T(1024)S(1)}, f32[256]{0:T(256)S(1)}, f32[256]{0:T(256)S(1)}, f32[1024]{0:T(1024)S(1)}, f32[256,1024]{1,0:T(8,128)S(1)}) fusion(f32[256,1024]{1,0:T(8,128)S(1)} %get-tuple-element.90, f32[256]{0:T(256)S(1)} %add_rsqrt_fusion.1, f32[256]{0:T(256)S(1)} %broadcast_multiply_fusion.5, f32[1024]{0:T(1024)S(1)} %convert.12, ...), kind=kOutput, calls=%fused_computation.44 | convolution fusion | flops 2152199680 | bytes 14180352 | tf_op jit(solution)/shard_map/dot_general | solution.py:27
  290.6 1.3 convert_reduce_fusion.4
  292.7 20.9 %attend_back.1 = (bf16[256,1024]{1,0:T(8,128)(2,1)S(1)}, bf16[1024,1024]{1,0:T(8,128)(2,1)S(1)}, bf16[1024,1024]{1,0:T(8,128)(2,1)S(1)}) custom-call(bf16[256,1024]{1,0:T(8,128)(2,1)S(1)} %copy-done.5, bf16[1024,1024]{1,0:T(8,128)(2,1)S(1)} %convolution_convert_fusion.k_ref, bf16[1024,1024]{1,0:T(8,128)(2,1)S(1)} %add_convert_fusion.1.v_ref, ...), custom_call_target="tpu_custom_call" | custom-call | tf_op jit(solution)/shard_map/attend_back/pallas_call | solution.py:768
  313.6 1.3 copy-done.2
  315.6 38.5 %psum.7 = f32[4,3072]{1,0:T(4,128)S(1)} all-reduce(f32[4,3072]{1,0:T(4,128)S(1)} %constant_dynamic-update-slice_fusion), channel_id=1, replica_groups=mesh['ctx'=8,'fsdp'=4] {'ctx','fsdp'}, use_global_device_ids=true, to_apply=%region_17.18 | all-reduce | flops 12288 | bytes 98304 | tf_op jit(solution)/shard_map/psum | solution.py:1149
  355.5 4.7 fusion.28
  360.3 3.7 fusion.27
  364.1 1.7 fusion.9.dxo
  365.8 185.5 %reduce_all.1 = (bf16[24,128,1024]{2,1,0:T(8,128)(2,1)}, bf16[2,1,128,1024]{3,2,1,0:T(8,128)(2,1)}, bf16[2,1,128,1024]{3,2,1,0:T(8,128)(2,1)}) custom-call(bf16[256,4096]{1,0:T(8,128)(2,1)} %copy-done.11, bf16[256,1024]{1,0:T(8,128)(2,1)} %copy-done.13, bf16[256,1024]{1,0:T(8,128)(2,1)} %copy-done.15, bf16[256,4096]{1,0:T(8,128)(2,1)} %copy-done.12, ...), custom_call_target="tpu_custom_call" | custom-call | tf_op jit(solution)/shard_map/reduce_all/pallas_call | solution.py:1049
  551.3 5.1 fusion.21
  556.4 2.4 copy.39
  558.8 1.9 copy-done.7
  560.7 2.2 fusion.22
  562.9 1.1 convert_element_type.181
  (107 shorter events, 9.7 us)
Async XLA Ops:
  8.1 0.6 copy-start.20
  223.7 4.6 copy-start.6
  223.7 4.8 copy-start.9
  225.0 25.6 %copy-start.16 = (bf16[256,1024]{1,0:T(8,128)(2,1)}, bf16[256,1024]{1,0:T(8,128)(2,1)S(1)}, u32[]{:S(2)}) copy-start(bf16[256,1024]{1,0:T(8,128)(2,1)S(1)} %constant_dynamic-slice_fusion.1.xo) | copy-start | bytes 1572868
  228.3 6.7 %copy-start.4 = (bf16[256,1024]{1,0:T(8,128)(2,1)}, bf16[256,1024]{1,0:T(8,128)(2,1)S(1)}, u32[]{:S(2)}) copy-start(bf16[256,1024]{1,0:T(8,128)(2,1)S(1)} %fusion.12.q_ref) | copy-start | bytes 1572868
  228.5 4.1 copy-start.22
  232.6 20.5 %slice-start = ((s8[8388608]{0:T(1024)(128)(4,1)}), s8[4194304]{0:T(1024)(128)(4,1)S(1)}, s32[]{:S(2)}) async-start(s8[8388608]{0:T(1024)(128)(4,1)} %bitcast.93), calls=%async_computation | async-start | bytes 8388608
  232.7 20.5 %slice-start.1 = ((s8[8388608]{0:T(1024)(128)(4,1)}), s8[4194304]{0:T(1024)(128)(4,1)S(1)}, s32[]{:S(2)}) async-start(s8[8388608]{0:T(1024)(128)(4,1)} %bitcast.93), calls=%async_computation.1 | async-start | bytes 8388608
  235.0 15.6 %copy-start.23 = (bf16[1024,1024]{1,0:T(8,128)(2,1)S(1)}, bf16[1024,1024]{1,0:T(8,128)(2,1)}, u32[]{:S(2)}) copy-start(bf16[1024,1024]{1,0:T(8,128)(2,1)} %get-tuple-element.39) | copy-start | bytes 6291460
  250.6 15.7 %copy-start.3 = (bf16[256,1024]{1,0:T(8,128)(2,1)}, bf16[256,1024]{1,0:T(8,128)(2,1)S(1)}, u32[]{:S(2)}) copy-start(bf16[256,1024]{1,0:T(8,128)(2,1)S(1)} %attend.1.ctx) | copy-start | bytes 1572868
  251.4 14.8 %slice-start.2 = ((s8[8388608]{0:T(1024)(128)(4,1)}), s8[4194304]{0:T(1024)(128)(4,1)S(1)}, s32[]{:S(2)}) async-start(s8[8388608]{0:T(1024)(128)(4,1)} %bitcast.95), calls=%async_computation.2 | async-start | bytes 8388608
  252.0 14.2 %copy-start.15 = (bf16[256,1024]{1,0:T(8,128)(2,1)}, bf16[256,1024]{1,0:T(8,128)(2,1)S(1)}, u32[]{:S(2)}) copy-start(bf16[256,1024]{1,0:T(8,128)(2,1)S(1)} %fusion.17.fb) | copy-start | bytes 1572868
  253.2 13.1 %slice-start.3 = ((s8[8388608]{0:T(1024)(128)(4,1)}), s8[4194304]{0:T(1024)(128)(4,1)S(1)}, s32[]{:S(2)}) async-start(s8[8388608]{0:T(1024)(128)(4,1)} %bitcast.95), calls=%async_computation.3 | async-start | bytes 8388608
  266.2 2.6 copy-start.11
  266.3 2.9 copy-start.14
  271.0 11.9 %copy-start.13 = (bf16[256,1024]{1,0:T(8,128)(2,1)}, bf16[256,1024]{1,0:T(8,128)(2,1)S(1)}, u32[]{:S(2)}) copy-start(bf16[256,1024]{1,0:T(8,128)(2,1)S(1)} %get-tuple-element.60.gb) | copy-start | bytes 1572868
  282.9 1.3 copy-start.12
  290.5 2.1 copy-start.5
  291.9 21.7 %copy-start.17 = (bf16[256,1024]{1,0:T(8,128)(2,1)}, bf16[256,1024]{1,0:T(8,128)(2,1)S(1)}, u32[]{:S(2)}) copy-start(bf16[256,1024]{1,0:T(8,128)(2,1)S(1)} %get-tuple-element.62.gal) | copy-start | bytes 1572868
  313.6 1.3 copy-start.2
  314.9 45.4 %copy-start = (bf16[1024,1024]{1,0:T(8,128)(2,1)}, bf16[1024,1024]{1,0:T(8,128)(2,1)S(1)}, u32[]{:S(2)}) copy-start(bf16[1024,1024]{1,0:T(8,128)(2,1)S(1)} %get-tuple-element.45.dv) | copy-start | bytes 6291460
  314.9 49.1 %copy-start.1 = (bf16[256,1024]{1,0:T(8,128)(2,1)}, bf16[256,1024]{1,0:T(8,128)(2,1)S(1)}, u32[]{:S(2)}) copy-start(bf16[256,1024]{1,0:T(8,128)(2,1)S(1)} %get-tuple-element.43.dq) | copy-start | bytes 1572868
  355.5 4.8 copy-start.21
  360.3 3.8 copy-start.8
  360.3 3.7 copy-start.10
  556.4 4.3 copy-start.7
  560.7 2.2 copy-start.18
  560.7 3.3 copy-start.19

commit v2 on v1

--- a/solution.py
+++ b/solution.py
@@ -419,6 +419,7 @@
 F32 = jnp.float32
 CHUNKS = 24
 SLOTS = 3
+LAND = 4
 
 
 def coords():
@@ -455,7 +456,7 @@
 def gather_kernel(
     inp, cot, seg, wq, wk, wv, wo, we, wc, vec,
     xf, cotf, segf, fq, fk, fv, fo, fe, fc, vecf,
-    a_send, a_recv, g_send, g_recv, w_send, w_recv, v_send, v_recv,
+    own, a_send, a_recv, g_send, g_recv, w_send, w_recv, v_send, v_recv,
 ):
     z, x, y, k = coords()
     f = y * 2 + k
@@ -591,10 +592,11 @@
             dst = part(i, (1 - y) * 2 + 1 - k, 0, 256)
         pltpu.make_async_copy(dst, dst, w_recv.at[kind, i]).wait()
 
-    def own_copy(i):
-        return pltpu.make_async_copy(
-            part(i, f, 0, 256, True), part(i, f, 0, 256), w_recv.at[8, i]
-        )
+    def own_in(i):
+        return pltpu.make_async_copy(part(i, f, 0, 256, True), own.at[i], w_recv.at[8, i])
+
+    def own_out(i):
+        return pltpu.make_async_copy(own.at[i], part(i, f, 0, 256), w_recv.at[9, i])
 
     vec_copies = (
         remote(vec, vecf.at[f], v_send.at[0], v_recv.at[0], yn),
@@ -605,6 +607,8 @@
 
     start_blocks((0, 1))
     vec_own.start()
+    for i in range(n_items):
+        own_in(i).start()
     vec_copies[0].start()
     vec_copies[1].start()
     for t in range(n_items + 3):
@@ -612,7 +616,6 @@
             send_copy(t, 0).start()
             send_copy(t, 1).start()
             send_copy(t, 6).start()
-            own_copy(t).start()
         if t == 1:
             arrive_blocks((0, 1))
             for step in range(2):
@@ -627,6 +630,8 @@
             start_blocks((2,))
         if 1 <= t <= n_items:
             i = t - 1
+            own_in(i).wait()
+            own_out(i).start()
             arrive(i, 0)
             send_copy(i, 2).start()
             send_copy(i, 4).start()
@@ -645,7 +650,7 @@
     for i in range(n_items):
         arrive(i, 6)
         arrive(i, 7)
-        own_copy(i).wait()
+        own_out(i).wait()
         for kind in range(8):
             send_copy(i, kind).wait_send()
     arrive_blocks((2,))
@@ -683,10 +688,13 @@
         in_specs=[any_spec] * 10,
         out_specs=[any_spec] * 10,
         scratch_shapes=[
+            pltpu.VMEM((12, 256, 1024), BF),
             dma((3, 2)), dma((3, 2)), dma((2, 3)), dma((2, 3)),
-            dma((8, 12)), dma((9, 12)), dma((3,)), dma((4,)),
+            dma((8, 12)), dma((10, 12)), dma((3,)), dma((4,)),
         ],
-        compiler_params=pltpu.CompilerParams(collective_id=0, has_side_effects=True),
+        compiler_params=pltpu.CompilerParams(
+            collective_id=0, has_side_effects=True, vmem_limit_bytes=32 << 20
+        ),
         name="gather_all",
     )(inp, cot, seg, *weights, vec)
 
@@ -782,11 +790,11 @@
 
 
 def reduce_kernel(
-    gel, gb, fb, gh, ctx, gal, xo, dq, xf, dk, dv, dxo, dxp, res,
-    out, resf, dxf,
+    gel, gb, fb, gh, ctx, gal, xo, dq, xf, dk, dv, dxo, dxp, res, vec,
+    out, resf, dxf, vec_out,
     s_d, l_d, r_d, b_y, r_y, b_x, r_x, b_1, r_1, b_2, r_2,
-    dx_r, dx_s, dx_y, dx_b,
-    ss, rs, ds, dr, a_send, a_recv,
+    dx_r, dx_s, dx_y, dx_b, v_s, v_d, v_r,
+    ss, rs, ds, dr, a_send, a_recv, v_send, v_recv,
 ):
     z, x, y, k = coords()
     sib, xn, yn = dev(z, x, y, 1 - k), dev(z, 1 - x, y, k), dev(z, x, 1 - y, k)
@@ -848,24 +856,52 @@
     dx_core(1).start()
     dx_core(0).start()
 
+    v_peers = (sib, yn, xn, z1, z2)
+
+    def v_copy(stage):
+        if stage == 0:
+            return remote(v_d.at[1], v_d.at[2], v_send.at[0], v_recv.at[0], sib)
+        src = v_s.at[0, 1 - y] if stage == 1 else v_s.at[stage - 1, 0]
+        return remote(src, v_r.at[stage - 1], v_send.at[stage], v_recv.at[stage], v_peers[stage])
+
+    def v_step(stage):
+        if stage == 0:
+            for plane in range(2):
+                v_d[0, plane] = vec[plane * 2 + k]
+                v_d[1, plane] = vec[plane * 2 + 1 - k]
+        elif stage == 1:
+            pltpu.make_async_copy(v_d.at[2], v_d.at[2], v_recv.at[0]).wait()
+            v_s[0] = v_d[0] + v_d[2]
+        else:
+            dst = v_r.at[stage - 2]
+            pltpu.make_async_copy(dst, dst, v_recv.at[stage - 1]).wait()
+            mine = v_s[0, y] if stage == 2 else v_s[stage - 2, 0]
+            total = mine + v_r[stage - 2]
+            if stage == 5:
+                vec_out[...] = total
+            else:
+                v_s[stage - 1, 0] = total
+        if stage < 5:
+            v_copy(stage).start()
+
     def send(stage, i, src, dst, to):
-        return remote(src, dst, ss.at[stage, i % SLOTS], rs.at[stage, i], to)
+        return remote(src, dst, ss.at[stage, i % SLOTS], rs.at[stage, i % LAND], to)
 
     def landed(stage, i, dst):
-        pltpu.make_async_copy(dst, dst, rs.at[stage, i]).wait()
+        pltpu.make_async_copy(dst, dst, rs.at[stage, i % LAND]).wait()
 
     def copies(stage, i):
         slot = i % SLOTS
         if stage == 0:
-            return send(0, i, s_d.at[slot], r_d.at[i], sib)
+            return send(0, i, s_d.at[slot], r_d.at[i % LAND], sib)
         if stage == 1:
-            return send(1, i, b_y.at[slot, 1 - y], r_y.at[i], yn)
+            return send(1, i, b_y.at[slot, 1 - y], r_y.at[i % LAND], yn)
         if stage == 2:
-            return send(2, i, b_x.at[slot, rows_of((1 - x) * 64, 64)], r_x.at[i], xn)
+            return send(2, i, b_x.at[slot, rows_of((1 - x) * 64, 64)], r_x.at[i % LAND], xn)
         if stage == 3:
-            return send(3, i, b_1.at[slot, rows_of((1 - bit1) * 32, 32)], r_1.at[i], z1)
+            return send(3, i, b_1.at[slot, rows_of((1 - bit1) * 32, 32)], r_1.at[i % LAND], z1)
         if stage == 4:
-            return send(4, i, b_2.at[slot, rows_of((1 - bit2) * 16, 16)], r_2.at[i], z2)
+            return send(4, i, b_2.at[slot, rows_of((1 - bit2) * 16, 16)], r_2.at[i % LAND], z2)
         if stage == 5:
             own = out.at[i, rows_of(x * 64 + bit1 * 32 + bit2 * 16, 16)]
             return send(5, i, own, own, z2)
@@ -947,9 +983,9 @@
         def _():
             slot = i1 % SLOTS
             clear(1, i1)
-            landed(0, i1, r_d.at[i1])
+            landed(0, i1, r_d.at[i1 % LAND])
             for plane in range(2):
-                b_y[slot, plane] = add(l_d[slot, plane], r_d[i1, plane])
+                b_y[slot, plane] = add(l_d[slot, plane], r_d[i1 % LAND, plane])
             launch(1, i1)
 
         i2, live2 = at(2)
@@ -958,8 +994,8 @@
         def _():
             slot = i2 % SLOTS
             clear(2, i2)
-            landed(1, i2, r_y.at[i2])
-            b_x[slot] = add(b_y[slot, y], r_y[i2])
+            landed(1, i2, r_y.at[i2 % LAND])
+            b_x[slot] = add(b_y[slot, y], r_y[i2 % LAND])
             launch(2, i2)
 
         i3, live3 = at(3)
@@ -968,8 +1004,8 @@
         def _():
             slot = i3 % SLOTS
             clear(3, i3)
-            landed(2, i3, r_x.at[i3])
-            b_1[slot] = add(b_x[slot, rows_of(x * 64, 64)], r_x[i3])
+            landed(2, i3, r_x.at[i3 % LAND])
+            b_1[slot] = add(b_x[slot, rows_of(x * 64, 64)], r_x[i3 % LAND])
             launch(3, i3)
 
         i4, live4 = at(4)
@@ -978,8 +1014,8 @@
         def _():
             slot = i4 % SLOTS
             clear(4, i4)
-            landed(3, i4, r_1.at[i4])
-            b_2[slot] = add(b_1[slot, rows_of(bit1 * 32, 32)], r_1[i4])
+            landed(3, i4, r_1.at[i4 % LAND])
+            b_2[slot] = add(b_1[slot, rows_of(bit1 * 32, 32)], r_1[i4 % LAND])
             launch(4, i4)
 
         i5, live5 = at(5)
@@ -988,9 +1024,9 @@
         def _():
             slot = i5 % SLOTS
             clear(5, i5)
-            landed(4, i5, r_2.at[i5])
+            landed(4, i5, r_2.at[i5 % LAND])
             out[i5, rows_of(x * 64 + bit1 * 32 + bit2 * 16, 16)] = add(
-                b_2[slot, rows_of(bit2 * 16, 16)], r_2[i5]
+                b_2[slot, rows_of(bit2 * 16, 16)], r_2[i5 % LAND]
             )
             launch(5, i5)
 
@@ -1015,6 +1051,12 @@
         @pl.when(live8)
         def _():
             landed(7, i8, out.at[i8, rows_of((1 - x) * 64, 64)])
+
+        for stage in range(6):
+
+            @pl.when(t == 2 * stage)
+            def _():
+                v_step(stage)
 
         @pl.when(t == 1)
         def _():
@@ -1035,6 +1077,8 @@
     for stage in range(8):
         for i in range(CHUNKS - SLOTS, CHUNKS):
             copies(stage, i).wait_send()
+    for stage in range(5):
+        v_copy(stage).wait_send()
     dx_core(0).wait_send()
     dx_core(1).wait_send()
     dx_far.wait_send()
@@ -1052,26 +1096,31 @@
             jax.ShapeDtypeStruct((CHUNKS, 128, 1024), BF),
             jax.ShapeDtypeStruct((2, 1, 128, 1024), BF),
             jax.ShapeDtypeStruct((2, 1, 128, 1024), BF),
+            jax.ShapeDtypeStruct((24, 128), F32),
         ],
-        in_specs=[vmem] * 14,
-        out_specs=[vmem, any_spec, any_spec],
+        in_specs=[vmem] * 15,
+        out_specs=[vmem, any_spec, any_spec, vmem],
         scratch_shapes=[
             pltpu.VMEM((SLOTS, 2, 128, 1024), BF),
             pltpu.VMEM((SLOTS, 2, 128, 1024), BF),
-            pltpu.VMEM((CHUNKS, 2, 128, 1024), BF),
+            pltpu.VMEM((LAND, 2, 128, 1024), BF),
             pltpu.VMEM((SLOTS, 2, 128, 1024), BF),
-            pltpu.VMEM((CHUNKS, 128, 1024), BF),
+            pltpu.VMEM((LAND, 128, 1024), BF),
             pltpu.VMEM((SLOTS, 128, 1024), BF),
-            pltpu.VMEM((CHUNKS, 64, 1024), BF),
+            pltpu.VMEM((LAND, 64, 1024), BF),
             pltpu.VMEM((SLOTS, 64, 1024), BF),
-            pltpu.VMEM((CHUNKS, 32, 1024), BF),
+            pltpu.VMEM((LAND, 32, 1024), BF),
             pltpu.VMEM((SLOTS, 32, 1024), BF),
-            pltpu.VMEM((CHUNKS, 16, 1024), BF),
+            pltpu.VMEM((LAND, 16, 1024), BF),
             pltpu.VMEM((2, 256, 1024), BF),
             pltpu.VMEM((256, 1024), BF),
             pltpu.VMEM((256, 1024), BF),
             pltpu.VMEM((256, 1024), BF),
-            dma((8, SLOTS)), dma((8, CHUNKS)), dma((3,)), dma((3,)), dma((2, 2)), dma((2, 2)),
+            pltpu.VMEM((4, 2, 24, 128), F32),
+            pltpu.VMEM((3, 2, 24, 128), F32),
+            pltpu.VMEM((4, 24, 128), F32),
+            dma((8, SLOTS)), dma((8, LAND)), dma((3,)), dma((3,)), dma((2, 2)), dma((2, 2)),
+            dma((5,)), dma((5,)),
         ],
         compiler_params=pltpu.CompilerParams(
             collective_id=1, has_side_effects=True, vmem_limit_bytes=61 << 20
@@ -1146,14 +1195,12 @@
     sums = jnp.concatenate(
         [v.reshape(4, 256) for v in terms] + [column(gh).reshape(4, 1024)], axis=1
     )
-    sums = lax.psum(sums, ("ctx", "fsdp"))
-    mine = lax.dynamic_slice_in_dim(sums, y * 2 + k, 1, 0)[0]
+    out, resf, dxf, vec = reduce_call(
+        gelled, gb, first_bf, gh, ctx, gal, xo, dq, xf, dk, dv, dxo, dxp.astype(BF),
+        result.astype(BF), sums.reshape(4, 24, 128),
+    )
+    mine = vec.reshape(3072)
     vec_grads = [mine[i * 256 : (i + 1) * 256] for i in range(8)]
-
-    out, resf, dxf = reduce_call(
-        gelled, gb, first_bf, gh, ctx, gal, xo, dq, xf, dk, dv, dxo, dxp.astype(BF),
-        result.astype(BF),
-    )
     grads = out.astype(F32)
 
     def square(start):

time: 573 us -> 421 us (0.73)
  Pallas kernels: 437 us -> 308 us
  blocking collectives: 38.5 us -> 0 us
  local copies, waits for them, and re-layouts: 27 us -> 43.9 us
    pallas_call x1, Pallas kernels: 215 us -> 84.3 us  [gather_call(): pl.pallas_call(gather_kernel, out_shape=outs, in_specs=[any_spec] * 10, o...]
    psum x1 -> x0, blocking collectives: 38.5 us -> none  [per_group_device(): sums = lax.psum(sums, ('ctx', 'fsdp'))]
    unnamed x74 -> x111, local copies, waits for them, and re-layouts: 13.4 us -> 31.7 us
where the time goes in v2:
time: 421 us; the launch traced here: 418 us
  Pallas kernels  308 us (73%)
  matrix products  54.8 us (13%)
  local copies, waits for them, and re-layouts  43.9 us (10%)
  other arithmetic  9.38 us (2%)
    pallas_call x1, Pallas kernels, reduce_call(): pl.pallas_call(reduce_kernel, out_shape=[jax.ShapeDtypeStruct((CHUNKS, 12...  187 us
    pallas_call x1, Pallas kernels, gather_call(): pl.pallas_call(gather_kernel, out_shape=outs, in_specs=[any_spec] * 10, o...  84.3 us
    unnamed x111, local copies, waits for them, and re-layouts  31.7 us
    dot_general x6, matrix products, right_dot(): lax.dot_general(left_side, right_side, (((1,), (1,)), ((), ())), preferre...  30.6 us
    dot_general x6, matrix products, plain_dot(): return jnp.dot(left_side, right_side, preferred_element_type=jnp.float32)  24.1 us
    pallas_call x1, Pallas kernels, attend_back(): pl.pallas_call(attend_back_kernel, grid=(8,), out_shape=[jax.ShapeDtypeSt...  21.1 us
    pallas_call x1, Pallas kernels, attend(): pl.pallas_call(attend_kernel, grid=(8,), out_shape=jax.ShapeDtypeStruct((...  15.5 us

profile of v2, /device:TPU:0, one launch (start us, length us, event | category | flops | bytes accessed | tf_op | source)
XLA Modules:
  0.0 417.7 jit_solution(13303372168551555076)
XLA Ops:
  8.1 1.6 copy-done.7
  9.7 1.6 copy-done.8
  11.3 1.0 copy-done.15
  18.2 84.3 %gather_all.1 = (bf16[1024,1024]{1,0:T(8,128)(2,1)S(1)}, bf16[256,1024]{1,0:T(8,128)(2,1)S(1)}, s32[8,1,128]{2,1,0:T(1,128)S(1)}, bf16[1024,1024]{1,0:T(8,128)(2...) custom-call(bf16[2,1,128,1024]{3,2,1,0:T(8,128)(2,1)S(1)} %copy-done, ...), custom_call_target="tpu_custom_call" | custom-call | tf_op jit(solution)/shard_map/gather_all/pallas_call | solution.py:685
  102.5 1.3 copy-done.9
  103.8 1.4 copy-done.22
  105.2 1.4 copy-done.25
  106.5 1.3 copy-done.27
  108.2 3.0 fusion.12.q_ref
  111.2 2.3 add_convert_fusion.1.v_ref
  113.6 2.3 convolution_convert_fusion.k_ref
  116.0 15.5 %attend.1.ctx = bf16[256,1024]{1,0:T(8,128)(2,1)S(1)} custom-call(bf16[256,1024]{1,0:T(8,128)(2,1)S(1)} %fusion.12.q_ref, bf16[1024,1024]{1,0:T(8,128)(2,1)S(1)} %convolution_convert_fusion.k_ref, bf16[1024,1024]{1,0:T(8,128)(2,1)S(1)} %add_convert_fusion.1.v_ref, s32[256,1]{1,0:T(8,128)S(1)} %copy.36.sq_ref, s32[1,1024]{1,0:T(1,128)S(1)} %bitcast.79), custom_call_target="tpu_custom_call" | custom-call | tf_op jit(solution)/shard_map/attend/pallas_call | solution.py:762
  133.0 13.0 %multiply_convert_fusion = (bf16[256,4096]{1,0:T(8,128)(2,1)S(1)}, f32[256,4096]{1,0:T(8,128)}, f32[256,4096]{1,0:T(8,128)}) fusion(f32[4096]{0:T(1024)S(1)} %bitcast_convert_fusion, bf16[256,1024]{1,0:T(8,128)(2,1)S(1)} %fusion.17.fb, bf16[1024,4096]{1,0:T(8,128)(2,1)S(1)} %bitcast.100), kind=kOutput, calls=%fused_computation.6 | convolution fusion | flops 2216689664 | bytes 19415040 | tf_op jit(solution)/shard_map/dot_general | solution.py:17
  146.2 2.5 fusion.25
  150.2 2.5 convert_reduce_fusion.3
  152.7 11.7 %convert_reduce_fusion = (f32[4096]{0:T(1024)S(1)}, bf16[256,4096]{1,0:T(8,128)(2,1)S(1)}) fusion(f32[256,4096]{1,0:T(8,128)} %get-tuple-element.67, f32[256,4096]{1,0:T(8,128)} %get-tuple-element.93, bf16[256,1024]{1,0:T(8,128)(2,1)S(1)} %get-tuple-element.62.gb, bf16[4096,1024]{1,0:T(8,128)(2,1)} %get-tuple-element.42), kind=kOutput, calls=%fused_computation.3 | convolution fusion | flops 2164256768 | bytes 19415040 | tf_op jit(solution)/shard_map/dot_general | solution.py:27
  164.5 7.9 %multiply_reduce_fusion = (f32[1024]{0:T(1024)S(1)}, f32[256]{0:T(256)S(1)}, f32[256]{0:T(256)S(1)}, f32[1024]{0:T(1024)S(1)}, f32[256,1024]{1,0:T(8,128)}) fusion(f32[256,1024]{1,0:T(8,128)S(1)} %copy-done.33, f32[256]{0:T(256)S(1)} %add_rsqrt_fusion.1, f32[256]{0:T(256)S(1)} %broadcast_multiply_fusion.5, f32[1024]{0:T(1024)S(1)} %convert.12, ...), kind=kOutput, calls=%fused_computation.44 | convolution fusion | flops 2152199680 | bytes 14180352 | tf_op jit(solution)/shard_map/dot_general | solution.py:27
  172.5 2.9 convert_reduce_fusion.4
  177.0 1.6 copy-done.2
  178.6 1.6 copy-done.4
  180.2 21.1 %attend_back.1 = (bf16[256,1024]{1,0:T(8,128)(2,1)S(1)}, bf16[1024,1024]{1,0:T(8,128)(2,1)S(1)}, bf16[1024,1024]{1,0:T(8,128)(2,1)S(1)}) custom-call(bf16[256,1024]{1,0:T(8,128)(2,1)S(1)} %copy-done.14, bf16[1024,1024]{1,0:T(8,128)(2,1)S(1)} %copy-done.4, bf16[1024,1024]{1,0:T(8,128)(2,1)S(1)} %copy-done.2, ...), custom_call_target="tpu_custom_call" | custom-call | tf_op jit(solution)/shard_map/attend_back/pallas_call | solution.py:776
  201.3 1.3 copy-done.11
  204.2 4.7 %fusion.27 = f32[1024,1024]{1,0:T(8,128)S(1)} fusion(bf16[1024,1024]{1,0:T(8,128)(2,1)} %copy-done.11, bf16[1024,1024]{1,0:T(8,128)(2,1)} %copy-done.25), kind=kOutput, calls=%fused_computation.96 | convolution fusion | flops 2147483648 | bytes 8388608 | tf_op jit(solution)/shard_map/dot_general | solution.py:27
  209.0 3.8 fusion.26
  212.7 1.7 fusion.9.dxo
  214.5 187.1 %reduce_all.1 = (bf16[24,128,1024]{2,1,0:T(8,128)(2,1)}, bf16[2,1,128,1024]{3,2,1,0:T(8,128)(2,1)}, bf16[2,1,128,1024]{3,2,1,0:T(8,128)(2,1)}, f32[24,128]{1,0:T(8,128)}) custom-call(bf16[256,4096]{1,0:T(8,128)(2,1)} %copy-done.35, bf16[256,1024]{1,0:T(8,128)(2,1)} %copy-done.37, bf16[256,1024]{1,0:T(8,128)(2,1)} %copy-done.38, ...), custom_call_target="tpu_custom_call" | custom-call | tf_op jit(solution)/shard_map/reduce_all/pallas_call | solution.py:1093
  401.6 1.3 slice_bitcast_fusion
  402.9 1.4 slice_bitcast_fusion.1
  404.3 2.1 convert_element_type.186
  406.4 3.9 fusion.22
  411.4 2.9 fusion.21
  414.3 2.3 copy.39
  (143 shorter events, 21.4 us)
Async XLA Ops:
  8.1 1.6 copy-start.7
  9.7 1.6 copy-start.8
  107.8 5.7 %copy-start.6 = (bf16[1024,1024]{1,0:T(8,128)(2,1)}, bf16[1024,1024]{1,0:T(8,128)(2,1)S(1)}, u32[]{:S(2)}) copy-start(bf16[1024,1024]{1,0:T(8,128)(2,1)S(1)} %get-tuple-element.34.xf) | copy-start | bytes 6291460
  108.1 3.1 copy-start.23
  108.2 23.4 %copy-start.39 = (bf16[256,1024]{1,0:T(8,128)(2,1)}, bf16[256,1024]{1,0:T(8,128)(2,1)S(1)}, u32[]{:S(2)}) copy-start(bf16[256,1024]{1,0:T(8,128)(2,1)S(1)} %constant_dynamic-slice_fusion.xo) | copy-start | bytes 1572868
  111.2 4.8 %copy-start.13 = (bf16[256,1024]{1,0:T(8,128)(2,1)}, bf16[256,1024]{1,0:T(8,128)(2,1)S(1)}, u32[]{:S(2)}) copy-start(bf16[256,1024]{1,0:T(8,128)(2,1)S(1)} %fusion.12.q_ref) | copy-start | bytes 1572868
  111.2 2.4 copy-start.26
  111.2 21.7 %slice-start = ((s8[8388608]{0:T(1024)(128)(4,1)}), s8[4194304]{0:T(1024)(128)(4,1)S(1)}, s32[]{:S(2)}) async-start(s8[8388608]{0:T(1024)(128)(4,1)} %bitcast.99), calls=%async_computation | async-start | bytes 8388608
  113.6 2.4 copy-start.1
  113.6 19.4 %slice-start.1 = ((s8[8388608]{0:T(1024)(128)(4,1)}), s8[4194304]{0:T(1024)(128)(4,1)S(1)}, s32[]{:S(2)}) async-start(s8[8388608]{0:T(1024)(128)(4,1)} %bitcast.99), calls=%async_computation.1 | async-start | bytes 8388608
  116.0 16.4 %copy-start.3 = (bf16[1024,1024]{1,0:T(8,128)(2,1)}, bf16[1024,1024]{1,0:T(8,128)(2,1)S(1)}, u32[]{:S(2)}) copy-start(bf16[1024,1024]{1,0:T(8,128)(2,1)S(1)} %convolution_convert_fusion.k_ref) | copy-start | bytes 6291460
  116.0 15.5 %copy-start.28 = (bf16[1024,1024]{1,0:T(8,128)(2,1)S(1)}, bf16[1024,1024]{1,0:T(8,128)(2,1)}, u32[]{:S(2)}) copy-start(bf16[1024,1024]{1,0:T(8,128)(2,1)} %copy-done.27) | copy-start | bytes 6291460
  131.6 14.5 %copy-start.12 = (bf16[256,1024]{1,0:T(8,128)(2,1)}, bf16[256,1024]{1,0:T(8,128)(2,1)S(1)}, u32[]{:S(2)}) copy-start(bf16[256,1024]{1,0:T(8,128)(2,1)S(1)} %attend.1.ctx) | copy-start | bytes 1572868
  132.4 13.7 %copy-start.32 = (f32[256,1024]{1,0:T(8,128)}, f32[256,1024]{1,0:T(8,128)S(1)}, u32[]{:S(2)}) copy-start(f32[256,1024]{1,0:T(8,128)S(1)} %get-tuple-element.92) | copy-start | bytes 3145732
  132.4 13.7 %slice-start.2 = ((s8[8388608]{0:T(1024)(128)(4,1)}), s8[4194304]{0:T(1024)(128)(4,1)S(1)}, s32[]{:S(2)}) async-start(s8[8388608]{0:T(1024)(128)(4,1)} %bitcast.101), calls=%async_computation.2 | async-start | bytes 8388608
  133.0 13.1 %copy-start.38 = (bf16[256,1024]{1,0:T(8,128)(2,1)}, bf16[256,1024]{1,0:T(8,128)(2,1)S(1)}, u32[]{:S(2)}) copy-start(bf16[256,1024]{1,0:T(8,128)(2,1)S(1)} %fusion.17.fb) | copy-start | bytes 1572868
  133.0 13.1 %slice-start.3 = ((s8[8388608]{0:T(1024)(128)(4,1)}), s8[4194304]{0:T(1024)(128)(4,1)S(1)}, s32[]{:S(2)}) async-start(s8[8388608]{0:T(1024)(128)(4,1)} %bitcast.101), calls=%async_computation.3 | async-start | bytes 8388608
  146.1 2.6 copy-start.35
  152.7 11.7 %copy-start.37 = (bf16[256,1024]{1,0:T(8,128)(2,1)}, bf16[256,1024]{1,0:T(8,128)(2,1)S(1)}, u32[]{:S(2)}) copy-start(bf16[256,1024]{1,0:T(8,128)(2,1)S(1)} %get-tuple-element.62.gb) | copy-start | bytes 1572868
  152.7 11.8 %copy-start.31 = (f32[256,1024]{1,0:T(8,128)S(1)}, f32[256,1024]{1,0:T(8,128)}, u32[]{:S(2)}) copy-start(f32[256,1024]{1,0:T(8,128)} %copy-done.30) | copy-start | bytes 3145732
  152.7 11.8 %copy-start.33 = (f32[256,1024]{1,0:T(8,128)S(1)}, f32[256,1024]{1,0:T(8,128)}, u32[]{:S(2)}) copy-start(f32[256,1024]{1,0:T(8,128)} %copy-done.32) | copy-start | bytes 3145732
  164.5 8.0 %copy-start.36 = (bf16[256,4096]{1,0:T(8,128)(2,1)}, bf16[256,4096]{1,0:T(8,128)(2,1)S(1)}, u32[]{:S(2)}) copy-start(bf16[256,4096]{1,0:T(8,128)(2,1)S(1)} %get-tuple-element.60.gh) | copy-start | bytes 6291460
  172.5 4.5 %copy-start.14 = (bf16[256,1024]{1,0:T(8,128)(2,1)S(1)}, bf16[256,1024]{1,0:T(8,128)(2,1)}, u32[]{:S(2)}) copy-start(bf16[256,1024]{1,0:T(8,128)(2,1)} %copy-done.13) | copy-start | bytes 1572868
  177.0 1.6 copy-start.2
  178.6 1.6 copy-start.4
  202.6 6.3 %copy-start = (bf16[1024,1024]{1,0:T(8,128)(2,1)}, bf16[1024,1024]{1,0:T(8,128)(2,1)S(1)}, u32[]{:S(2)}) copy-start(bf16[1024,1024]{1,0:T(8,128)(2,1)S(1)} %get-tuple-element.46.dv) | copy-start | bytes 6291460
  202.6 10.1 %copy-start.5 = (bf16[256,1024]{1,0:T(8,128)(2,1)}, bf16[256,1024]{1,0:T(8,128)(2,1)S(1)}, u32[]{:S(2)}) copy-start(bf16[256,1024]{1,0:T(8,128)(2,1)S(1)} %get-tuple-element.44.dq) | copy-start | bytes 1572868
  204.2 4.8 %copy-start.24 = (bf16[1024,1024]{1,0:T(8,128)(2,1)S(1)}, bf16[1024,1024]{1,0:T(8,128)(2,1)}, u32[]{:S(2)}) copy-start(bf16[1024,1024]{1,0:T(8,128)(2,1)} %copy-done.22) | copy-start | bytes 6291460
  208.9 3.8 copy-start.10
  208.9 3.8 copy-start.34
  406.4 4.9 %copy-start.29 = (bf16[24,128,1024]{2,1,0:T(8,128)(2,1)S(1)}, bf16[24,128,1024]{2,1,0:T(8,128)(2,1)}, u32[]{:S(2)}) copy-start(bf16[24,128,1024]{2,1,0:T(8,128)(2,1)} %get-tuple-element.49) | copy-start | bytes 18874372
  414.3 2.3 copy-start.41
  (14 other events, 15.4 us)

commit v3 on v2

--- a/solution.py
+++ b/solution.py
@@ -420,6 +420,7 @@
 CHUNKS = 24
 SLOTS = 3
 LAND = 4
+ROOM = 8
 
 
 def coords():
@@ -713,52 +714,32 @@
     return jnp.where(lane < HEAD_DIM, pair[:rows], pair[rows:])
 
 
-def softmax_pair(q_ref, k_ref, same_ref):
-    queries = two_heads(q_ref[...] * BF(HEAD_DIM**-0.5))
-    scores = right_dot(queries, k_ref[...])
-    same = same_ref[...]
-    scores = jnp.where(jnp.concatenate([same, same], axis=0) > 0, scores, -1e30)
+def attention_bias(sq_ref, sk_ref):
+    return jnp.where(sq_ref[...] == sk_ref[...], 0.0, -1e30).astype(F32)
+
+
+def softmax_pair(queries, keys, bias):
+    scores = right_dot(queries, keys)
+    scores = scores + jnp.concatenate([bias, bias], axis=0)
     numer = jnp.exp(scores - jnp.max(scores, axis=-1, keepdims=True))
-    return queries, numer * (1.0 / jnp.sum(numer, axis=-1, keepdims=True))
-
-
-def attend_kernel(q_ref, k_ref, v_ref, sq_ref, sk_ref, o_ref, same_ref):
+    return numer * (1.0 / jnp.sum(numer, axis=-1, keepdims=True))
+
+
+def attend_kernel(q_ref, k_ref, v_ref, sq_ref, sk_ref, o_ref, bias_ref):
     @pl.when(pl.program_id(0) == 0)
     def _():
-        same_ref[...] = (sq_ref[...] == sk_ref[...]).astype(F32)
-
-    probs = softmax_pair(q_ref, k_ref, same_ref)[1]
+        bias_ref[...] = attention_bias(sq_ref, sk_ref)
+
+    queries = two_heads(q_ref[...] * BF(HEAD_DIM**-0.5))
+    probs = softmax_pair(queries, k_ref[...], bias_ref[...])
     o_ref[...] = one_block(plain_dot(probs.astype(BF), v_ref[...])).astype(BF)
 
 
-def attend_back_kernel(
-    q_ref, k_ref, v_ref, g_ref, sq_ref, sk_ref, dq_ref, dk_ref, dv_ref, same_ref
-):
-    @pl.when(pl.program_id(0) == 0)
-    def _():
-        same_ref[...] = (sq_ref[...] == sk_ref[...]).astype(F32)
-
-    queries, probs = softmax_pair(q_ref, k_ref, same_ref)
-    grads = two_heads(g_ref[...])
-    grad_probs = right_dot(grads, v_ref[...])
-    delta = jnp.sum(probs * grad_probs, axis=-1, keepdims=True)
-    grad_scores = (probs * (grad_probs - delta)).astype(BF)
-    dv_ref[...] = left_dot(probs.astype(BF), grads).astype(BF)
-    dk_ref[...] = left_dot(grad_scores, queries).astype(BF)
-    dq = one_block(plain_dot(grad_scores, k_ref[...]))
-    dq_ref[...] = (dq * HEAD_DIM**-0.5).astype(BF)
-
-
-def attention_specs():
+def attend(q, k, v, sq, sk):
     rows = pl.BlockSpec((256, 128), lambda h: (0, h))
     full = pl.BlockSpec((1024, 128), lambda h: (0, h))
-    sq = pl.BlockSpec((256, 1), lambda h: (0, 0))
-    sk = pl.BlockSpec((1, 1024), lambda h: (0, 0))
-    return rows, full, sq, sk
-
-
-def attend(q, k, v, sq, sk):
-    rows, full, sqs, sks = attention_specs()
+    sqs = pl.BlockSpec((256, 1), lambda h: (0, 0))
+    sks = pl.BlockSpec((1, 1024), lambda h: (0, 0))
     return pl.pallas_call(
         attend_kernel,
         grid=(8,),
@@ -771,36 +752,38 @@
     )(q, k, v, sq, sk)
 
 
-def attend_back(q, k, v, g, sq, sk):
-    rows, full, sqs, sks = attention_specs()
-    return pl.pallas_call(
-        attend_back_kernel,
-        grid=(8,),
-        out_shape=[
-            jax.ShapeDtypeStruct((256, 1024), BF),
-            jax.ShapeDtypeStruct((1024, 1024), BF),
-            jax.ShapeDtypeStruct((1024, 1024), BF),
-        ],
-        in_specs=[rows, full, full, rows, sqs, sks],
-        out_specs=[rows, full, full],
-        scratch_shapes=[pltpu.VMEM((256, 1024), F32)],
-        compiler_params=pltpu.CompilerParams(vmem_limit_bytes=40 << 20),
-        name="attend_back",
-    )(q, k, v, g, sq, sk)
-
-
-def reduce_kernel(
-    gel, gb, fb, gh, ctx, gal, xo, dq, xf, dk, dv, dxo, dxp, res, vec,
-    out, resf, dxf, vec_out,
-    s_d, l_d, r_d, b_y, r_y, b_x, r_x, b_1, r_1, b_2, r_2,
-    dx_r, dx_s, dx_y, dx_b, v_s, v_d, v_r,
-    ss, rs, ds, dr, a_send, a_recv, v_send, v_recv,
+def backward_kernel(
+    gel, gb, gs, fb, gp, n1, inv1, gain1, ctx, q, key, val, xf, sq, sk, res, g2, s2,
+    we, wc, wo, wq, wk, wv,
+    o_q, o_k, o_v, o_o, o_e, o_c, resf, dxf, vec_out,
+    s_d, l_d, r_d, b_y, r_y, b_x, r_x, b_1, r_1, b_2, r_2, o_b,
+    gh, acc, ga, gal, dctx, dq, dk, dv, bias, we_b, wc_b, w_b,
+    dx_p, dx_r, dx_s, dx_y, dx_b, vec, v_s, v_d, v_r,
+    ss, rs, ds, dr, a_send, a_recv, v_send, v_recv, w_sem, o_sem,
 ):
     z, x, y, k = coords()
     sib, xn, yn = dev(z, x, y, 1 - k), dev(z, 1 - x, y, k), dev(z, x, 1 - y, k)
     bit1, bit2 = z % 2, z // 2
     z1 = dev(z + 1 - 2 * bit1, x, y, k)
     z2 = dev((z + 2) % 4, x, y, k)
+
+    def load_c(j):
+        return pltpu.make_async_copy(
+            wc.at[rows_of(j * 512, 512)], wc_b.at[j % 2], w_sem.at[j % 2]
+        )
+
+    def load_e(j):
+        return pltpu.make_async_copy(
+            we.at[:, rows_of(j * 512, 512, 512)], we_b.at[j % 2], w_sem.at[2 + j % 2]
+        )
+
+    def load_w(n):
+        return pltpu.make_async_copy((wo, wk, wv, wq)[n], w_b.at[n], w_sem.at[4 + n])
+
+    load_c(0).start()
+    load_e(0).start()
+    for n in range(4):
+        load_w(n).start()
     greet(z, x, y, k)
 
     def back(n, slot):
@@ -847,14 +830,14 @@
 
     start_back(0)
 
-    def dx_core(g):
-        who = x if g == 0 else 1 - x
-        src = dxp.at[rows_of(who * 512 + (1 - k) * 256, 256)]
-        return remote(src, dx_r.at[g], ds.at[g], dr.at[g], sib)
-
-    dx_far = remote(dx_s, dx_y, ds.at[2], dr.at[2], xn)
-    dx_core(1).start()
-    dx_core(0).start()
+    def column(v):
+        return jnp.sum(v.astype(F32), axis=0, keepdims=True)
+
+    def keep(i, row):
+        for quarter in range(4):
+            for half in range(2):
+                col = quarter * 256 + half * 128
+                vec[quarter, pl.ds(2 * i + half, 1)] = row[:, col : col + 128]
 
     v_peers = (sib, yn, xn, z1, z2)
 
@@ -891,24 +874,24 @@
         pltpu.make_async_copy(dst, dst, rs.at[stage, i % LAND]).wait()
 
     def copies(stage, i):
-        slot = i % SLOTS
+        slot, land, room = i % SLOTS, i % LAND, i % ROOM
         if stage == 0:
-            return send(0, i, s_d.at[slot], r_d.at[i % LAND], sib)
+            return send(0, i, s_d.at[slot], r_d.at[land], sib)
         if stage == 1:
-            return send(1, i, b_y.at[slot, 1 - y], r_y.at[i % LAND], yn)
+            return send(1, i, b_y.at[slot, 1 - y], r_y.at[land], yn)
         if stage == 2:
-            return send(2, i, b_x.at[slot, rows_of((1 - x) * 64, 64)], r_x.at[i % LAND], xn)
+            return send(2, i, b_x.at[slot, rows_of((1 - x) * 64, 64)], r_x.at[land], xn)
         if stage == 3:
-            return send(3, i, b_1.at[slot, rows_of((1 - bit1) * 32, 32)], r_1.at[i % LAND], z1)
+            return send(3, i, b_1.at[slot, rows_of((1 - bit1) * 32, 32)], r_1.at[land], z1)
         if stage == 4:
-            return send(4, i, b_2.at[slot, rows_of((1 - bit2) * 16, 16)], r_2.at[i % LAND], z2)
+            return send(4, i, b_2.at[slot, rows_of((1 - bit2) * 16, 16)], r_2.at[land], z2)
         if stage == 5:
-            own = out.at[i, rows_of(x * 64 + bit1 * 32 + bit2 * 16, 16)]
+            own = o_b.at[room, rows_of(x * 64 + bit1 * 32 + bit2 * 16, 16)]
             return send(5, i, own, own, z2)
         if stage == 6:
-            own = out.at[i, rows_of(x * 64 + bit1 * 32, 32)]
+            own = o_b.at[room, rows_of(x * 64 + bit1 * 32, 32)]
             return send(6, i, own, own, z1)
-        own = out.at[i, rows_of(x * 64, 64)]
+        own = o_b.at[room, rows_of(x * 64, 64)]
         return send(7, i, own, own, xn)
 
     def launch(stage, i):
@@ -922,13 +905,14 @@
     def add(a, b):
         return (a.astype(F32) + b.astype(F32)).astype(BF)
 
-    def terms(i, a_ref, b_ref, a_base, a_step, b_col):
+    def terms(i, a_ref, b_ref, a_base, a_step, b_col, a_rows=None):
         slot = i % SLOTS
         right = b_ref[:, b_col]
         for plane in range(2):
             for core in range(2):
                 quarter = plane * 2 + (k if core == 0 else 1 - k)
-                left = a_ref[:, pl.ds(pl.multiple_of(a_base + quarter * a_step, 128), 128)]
+                cols = pl.ds(pl.multiple_of(a_base + quarter * a_step, 128), 128)
+                left = a_ref[:, cols] if a_rows is None else a_ref[a_rows, cols]
                 product = left_dot(left, right).astype(BF)
                 if core == 0:
                     l_d[slot, plane] = product
@@ -936,97 +920,249 @@
                     s_d[slot, plane] = product
 
     every = pl.ds(0, 1024)
+    own_rows = rows_of(x * 512 + k * 256, 256)
+
+    def stage_zero(i):
+        @pl.when((i >= 0) & (i < CHUNKS))
+        def _():
+            clear(0, i)
+
+        @pl.when(i < 8)
+        def _():
+            terms(i, gel, gb, i * 128, 1024, every)
+
+        @pl.when((i >= 8) & (i < 16))
+        def _():
+            j = i - 8
+            terms(i, fb, gh, (j % 2) * 128, 256, rows_of((j // 2) * 1024, 1024, 1024))
+
+        @pl.when((i >= 16) & (i < 18))
+        def _():
+            terms(i, ctx, gal, (i - 16) * 128, 256, every)
+
+        @pl.when((i >= 18) & (i < 20))
+        def _():
+            terms(i, xf, dq, (i - 18) * 128, 256, every, own_rows)
+
+        @pl.when((i >= 20) & (i < 22))
+        def _():
+            terms(i, xf, dk, (i - 20) * 128, 256, every)
+
+        @pl.when((i >= 22) & (i < 24))
+        def _():
+            terms(i, xf, dv, (i - 22) * 128, 256, every)
+
+        @pl.when((i >= 0) & (i < CHUNKS))
+        def _():
+            launch(0, i)
+
+    def stored():
+        pltpu.make_async_copy(o_b.at[0], o_b.at[0], o_sem).wait()
+
+    def store(i):
+        src = o_b.at[i % ROOM]
+
+        @pl.when(i >= 1)
+        def _():
+            stored()
+
+        @pl.when(i < 8)
+        def _():
+            pltpu.make_async_copy(src, o_c.at[rows_of(i * 128, 128)], o_sem).start()
+
+        @pl.when((i >= 8) & (i < 16))
+        def _():
+            j = i - 8
+            dst = o_e.at[rows_of((j % 2) * 128, 128), rows_of((j // 2) * 1024, 1024, 1024)]
+            pltpu.make_async_copy(src, dst, o_sem).start()
+
+        for n, ref in enumerate((o_o, o_q, o_k, o_v)):
+            first = 16 + 2 * n
+
+            @pl.when((i >= first) & (i < first + 2))
+            def _():
+                dst = ref.at[rows_of((i - first) * 128, 128)]
+                pltpu.make_async_copy(src, dst, o_sem).start()
+
+    def feed_forward(j):
+        slot = j % 2
+        cols = rows_of(j * 512, 512, 512)
+        load_c(j).wait()
+        load_e(j).wait()
+
+        @pl.when(j < 7)
+        def _():
+            load_c(j + 1).start()
+            load_e(j + 1).start()
+
+        grads = (right_dot(gb[...], wc_b[slot]) * gp[:, cols].astype(F32)).astype(BF)
+        gh[:, cols] = grads
+        acc[...] += right_dot(grads, we_b[slot])
+        row = column(grads)
+        for n in range(4):
+            vec[j // 2, pl.ds(16 + (j % 2) * 4 + n, 1)] = row[:, n * 128 : n * 128 + 128]
+
+    def first_norm():
+        normed = n1[...]
+        grad_first = acc[...]
+        keep(3, column(grad_first * normed))
+        keep(4, column(grad_first))
+        scaled = grad_first * gain1[...]
+        grad_attn = inv1[...] * (
+            scaled
+            - jnp.mean(scaled, axis=-1, keepdims=True)
+            - normed * jnp.mean(scaled * normed, axis=-1, keepdims=True)
+        )
+        ga[...] = grad_attn
+        low = grad_attn.astype(BF)
+        gal[...] = low
+        keep(2, column(low))
+        load_w(0).wait()
+        dctx[...] = right_dot(low, w_b[0]).astype(BF)
+
+    def attention(h):
+        cols = rows_of(h * 128, 128, 128)
+        queries = two_heads(q[:, cols] * BF(HEAD_DIM**-0.5))
+        keys = key[:, cols]
+        probs = softmax_pair(queries, keys, bias[...])
+        grads = two_heads(dctx[:, cols])
+        grad_probs = right_dot(grads, val[:, cols])
+        delta = jnp.sum(probs * grad_probs, axis=-1, keepdims=True)
+        grad_scores = (probs * (grad_probs - delta)).astype(BF)
+        dv[:, cols] = left_dot(probs.astype(BF), grads).astype(BF)
+        dk[:, cols] = left_dot(grad_scores, queries).astype(BF)
+        dq[:, cols] = (one_block(plain_dot(grad_scores, keys)) * HEAD_DIM**-0.5).astype(BF)
+
+    def dx_core(g):
+        return remote(dx_p.at[g], dx_r.at[g], ds.at[g], dr.at[g], sib)
+
+    dx_far = remote(dx_s, dx_y, ds.at[2], dr.at[2], xn)
+
+    def input_rows(n):
+        who = x * (n % 2) + (1 - x) * (1 - n % 2)
+        core = (1 - k) * (1 - n // 2) + k * (n // 2)
+        rows = rows_of(who * 512 + core * 256, 256)
+        terms_here = right_dot(dk[rows], w_b[1]) + right_dot(dv[rows], w_b[2])
+
+        @pl.when(n == 0)
+        def _():
+            dx_p[1] = terms_here.astype(BF)
+            dx_core(1).start()
+
+        @pl.when(n == 1)
+        def _():
+            dx_p[0] = terms_here.astype(BF)
+            dx_core(0).start()
+
+        @pl.when(n == 2)
+        def _():
+            pltpu.make_async_copy(dx_r.at[1], dx_r.at[1], dr.at[1]).wait()
+            dx_s[...] = (terms_here + dx_r[1].astype(F32)).astype(BF)
+            dx_far.start()
+
+        @pl.when(n == 3)
+        def _():
+            pltpu.make_async_copy(dx_r.at[0], dx_r.at[0], dr.at[0]).wait()
+            load_w(3).wait()
+            ga[...] = ga[...] + terms_here + dx_r[0].astype(F32) + right_dot(dq[...], w_b[3])
+
+    bias[...] = attention_bias(sq, sk)
+    acc[...] = gs[...]
+    keep(5, column(gb[...]))
+    keep(6, g2[...])
+    keep(7, s2[...])
 
     def tick(t, carry):
         def at(stage):
             i = t - stage
             return i, (i >= 0) & (i < CHUNKS)
 
-        i0, live0 = at(0)
-
-        @pl.when(live0)
-        def _():
-            clear(0, i0)
-
-        @pl.when(i0 < 8)
-        def _():
-            terms(i0, gel, gb, i0 * 128, 1024, every)
-
-        @pl.when((i0 >= 8) & (i0 < 16))
-        def _():
-            j = i0 - 8
-            terms(i0, fb, gh, (j % 2) * 128, 256, rows_of((j // 2) * 1024, 1024, 1024))
-
-        @pl.when((i0 >= 16) & (i0 < 18))
-        def _():
-            terms(i0, ctx, gal, (i0 - 16) * 128, 256, every)
-
-        @pl.when((i0 >= 18) & (i0 < 20))
-        def _():
-            terms(i0, xo, dq, (i0 - 18) * 128, 256, every)
-
-        @pl.when((i0 >= 20) & (i0 < 22))
-        def _():
-            terms(i0, xf, dk, (i0 - 20) * 128, 256, every)
-
-        @pl.when((i0 >= 22) & (i0 < 24))
-        def _():
-            terms(i0, xf, dv, (i0 - 22) * 128, 256, every)
-
-        @pl.when(live0)
-        def _():
-            launch(0, i0)
-
+        stage_zero(t)
         i1, live1 = at(1)
 
         @pl.when(live1)
         def _():
-            slot = i1 % SLOTS
+            slot, land = i1 % SLOTS, i1 % LAND
             clear(1, i1)
-            landed(0, i1, r_d.at[i1 % LAND])
+            landed(0, i1, r_d.at[land])
             for plane in range(2):
-                b_y[slot, plane] = add(l_d[slot, plane], r_d[i1 % LAND, plane])
+                b_y[slot, plane] = add(l_d[slot, plane], r_d[land, plane])
             launch(1, i1)
 
+        @pl.when(t < 8)
+        def _():
+            feed_forward(t)
+
+        @pl.when(t == 8)
+        def _():
+            first_norm()
+
+        @pl.when((t >= 9) & (t < 17))
+        def _():
+            attention(t - 9)
+
+        @pl.when(t == 17)
+        def _():
+            keep(0, column(dq[...]))
+            keep(1, column(dv[...]))
+            load_w(1).wait()
+            load_w(2).wait()
+
+        @pl.when((t >= 17) & (t < 21))
+        def _():
+            input_rows(t - 17)
+
+        for stage in range(6):
+
+            @pl.when(t == 18 + 2 * stage)
+            def _():
+                v_step(stage)
+
+        @pl.when(t == 23)
+        def _():
+            pltpu.make_async_copy(dx_y, dx_y, dr.at[2]).wait()
+            dx_b[...] = (ga[...] + dx_y[...].astype(F32)).astype(BF)
+            start_back(1)
+
         i2, live2 = at(2)
 
         @pl.when(live2)
         def _():
-            slot = i2 % SLOTS
+            slot, land = i2 % SLOTS, i2 % LAND
             clear(2, i2)
-            landed(1, i2, r_y.at[i2 % LAND])
-            b_x[slot] = add(b_y[slot, y], r_y[i2 % LAND])
+            landed(1, i2, r_y.at[land])
+            b_x[slot] = add(b_y[slot, y], r_y[land])
             launch(2, i2)
 
         i3, live3 = at(3)
 
         @pl.when(live3)
         def _():
-            slot = i3 % SLOTS
+            slot, land = i3 % SLOTS, i3 % LAND
             clear(3, i3)
-            landed(2, i3, r_x.at[i3 % LAND])
-            b_1[slot] = add(b_x[slot, rows_of(x * 64, 64)], r_x[i3 % LAND])
+            landed(2, i3, r_x.at[land])
+            b_1[slot] = add(b_x[slot, rows_of(x * 64, 64)], r_x[land])
             launch(3, i3)
 
         i4, live4 = at(4)
 
         @pl.when(live4)
         def _():
-            slot = i4 % SLOTS
+            slot, land = i4 % SLOTS, i4 % LAND
             clear(4, i4)
-            landed(3, i4, r_1.at[i4 % LAND])
-            b_2[slot] = add(b_1[slot, rows_of(bit1 * 32, 32)], r_1[i4 % LAND])
+            landed(3, i4, r_1.at[land])
+            b_2[slot] = add(b_1[slot, rows_of(bit1 * 32, 32)], r_1[land])
             launch(4, i4)
 
         i5, live5 = at(5)
 
         @pl.when(live5)
         def _():
-            slot = i5 % SLOTS
+            slot, land = i5 % SLOTS, i5 % LAND
             clear(5, i5)
-            landed(4, i5, r_2.at[i5 % LAND])
-            out[i5, rows_of(x * 64 + bit1 * 32 + bit2 * 16, 16)] = add(
-                b_2[slot, rows_of(bit2 * 16, 16)], r_2[i5 % LAND]
+            landed(4, i5, r_2.at[land])
+            o_b[i5 % ROOM, rows_of(x * 64 + bit1 * 32 + bit2 * 16, 16)] = add(
+                b_2[slot, rows_of(bit2 * 16, 16)], r_2[land]
             )
             launch(5, i5)
 
@@ -1035,7 +1171,7 @@
         @pl.when(live6)
         def _():
             clear(6, i6)
-            landed(5, i6, out.at[i6, rows_of(x * 64 + bit1 * 32 + (1 - bit2) * 16, 16)])
+            landed(5, i6, o_b.at[i6 % ROOM, rows_of(x * 64 + bit1 * 32 + (1 - bit2) * 16, 16)])
             launch(6, i6)
 
         i7, live7 = at(7)
@@ -1043,37 +1179,20 @@
         @pl.when(live7)
         def _():
             clear(7, i7)
-            landed(6, i7, out.at[i7, rows_of(x * 64 + (1 - bit1) * 32, 32)])
+            landed(6, i7, o_b.at[i7 % ROOM, rows_of(x * 64 + (1 - bit1) * 32, 32)])
             launch(7, i7)
 
         i8, live8 = at(8)
 
         @pl.when(live8)
         def _():
-            landed(7, i8, out.at[i8, rows_of((1 - x) * 64, 64)])
-
-        for stage in range(6):
-
-            @pl.when(t == 2 * stage)
-            def _():
-                v_step(stage)
-
-        @pl.when(t == 1)
-        def _():
-            pltpu.make_async_copy(dx_r.at[1], dx_r.at[1], dr.at[1]).wait()
-            dx_s[...] = add(dxp[rows_of((1 - x) * 512 + k * 256, 256)], dx_r[1])
-            dx_far.start()
-
-        @pl.when(t == 5)
-        def _():
-            pltpu.make_async_copy(dx_r.at[0], dx_r.at[0], dr.at[0]).wait()
-            pltpu.make_async_copy(dx_y, dx_y, dr.at[2]).wait()
-            dx_b[...] = (dxo[...] + dx_r[0].astype(F32) + dx_y[...].astype(F32)).astype(BF)
-            start_back(1)
+            landed(7, i8, o_b.at[i8 % ROOM, rows_of((1 - x) * 64, 64)])
+            store(i8)
 
         return carry
 
     lax.fori_loop(0, CHUNKS + 8, tick, 0)
+    stored()
     for stage in range(8):
         for i in range(CHUNKS - SLOTS, CHUNKS):
             copies(stage, i).wait_send()
@@ -1086,20 +1205,23 @@
     finish_back(1)
 
 
-def reduce_call(*operands):
+def backward_call(*operands):
     vmem = pl.BlockSpec(memory_space=pltpu.VMEM)
     any_spec = pl.BlockSpec(memory_space=pl.ANY)
     dma = pltpu.SemaphoreType.DMA
+    grad = jax.ShapeDtypeStruct((256, 1024), BF)
     return pl.pallas_call(
-        reduce_kernel,
+        backward_kernel,
         out_shape=[
-            jax.ShapeDtypeStruct((CHUNKS, 128, 1024), BF),
+            grad, grad, grad, grad,
+            jax.ShapeDtypeStruct((256, 4096), BF),
+            jax.ShapeDtypeStruct((1024, 1024), BF),
             jax.ShapeDtypeStruct((2, 1, 128, 1024), BF),
             jax.ShapeDtypeStruct((2, 1, 128, 1024), BF),
             jax.ShapeDtypeStruct((24, 128), F32),
         ],
-        in_specs=[vmem] * 15,
-        out_specs=[vmem, any_spec, any_spec, vmem],
+        in_specs=[vmem] * 18 + [any_spec] * 6,
+        out_specs=[any_spec] * 8 + [vmem],
         scratch_shapes=[
             pltpu.VMEM((SLOTS, 2, 128, 1024), BF),
             pltpu.VMEM((SLOTS, 2, 128, 1024), BF),
@@ -1112,20 +1234,35 @@
             pltpu.VMEM((LAND, 32, 1024), BF),
             pltpu.VMEM((SLOTS, 32, 1024), BF),
             pltpu.VMEM((LAND, 16, 1024), BF),
+            pltpu.VMEM((ROOM, 128, 1024), BF),
+            pltpu.VMEM((256, 4096), BF),
+            pltpu.VMEM((256, 1024), F32),
+            pltpu.VMEM((256, 1024), F32),
+            pltpu.VMEM((256, 1024), BF),
+            pltpu.VMEM((256, 1024), BF),
+            pltpu.VMEM((256, 1024), BF),
+            pltpu.VMEM((1024, 1024), BF),
+            pltpu.VMEM((1024, 1024), BF),
+            pltpu.VMEM((256, 1024), F32),
+            pltpu.VMEM((2, 1024, 512), BF),
+            pltpu.VMEM((2, 512, 1024), BF),
+            pltpu.VMEM((4, 1024, 1024), BF),
+            pltpu.VMEM((2, 256, 1024), BF),
             pltpu.VMEM((2, 256, 1024), BF),
             pltpu.VMEM((256, 1024), BF),
             pltpu.VMEM((256, 1024), BF),
             pltpu.VMEM((256, 1024), BF),
+            pltpu.VMEM((4, 24, 128), F32),
             pltpu.VMEM((4, 2, 24, 128), F32),
             pltpu.VMEM((3, 2, 24, 128), F32),
             pltpu.VMEM((4, 24, 128), F32),
             dma((8, SLOTS)), dma((8, LAND)), dma((3,)), dma((3,)), dma((2, 2)), dma((2, 2)),
-            dma((5,)), dma((5,)),
+            dma((5,)), dma((5,)), dma((8,)), dma(()),
         ],
         compiler_params=pltpu.CompilerParams(
             collective_id=1, has_side_effects=True, vmem_limit_bytes=61 << 20
         ),
-        name="reduce_all",
+        name="backward_all",
     )(*operands)
 
 
@@ -1164,58 +1301,33 @@
     first_out, normed_one, inverse_one = norm_forward(first_sum, gain_one, shift_one)
     first_bf = first_out.astype(BF)
     hidden = plain_dot(first_bf, we) + be
-    gelled = jax.nn.gelu(hidden, approximate=False).astype(BF)
+    below = 0.5 + 0.5 * lax.erf(hidden * 0.5**0.5)
+    gelled = (hidden * below).astype(BF)
+    gelu_slope = (
+        below + hidden * (jnp.exp(-0.5 * hidden * hidden) * (2 * jnp.pi) ** -0.5)
+    ).astype(BF)
     second_sum = first_out + plain_dot(gelled, wc) + bc
     result, normed_two, inverse_two = norm_forward(second_sum, gain_two, shift_two)
-    grad_out = cot.astype(F32)
     grad_second, gain_two_grad, shift_two_grad = norm_backward(
-        grad_out, normed_two, inverse_two, gain_two
-    )
-    gb = grad_second.astype(BF)
-    grad_gelled = right_dot(gb, wc)
-    gelu_pull = jax.vjp(lambda values: jax.nn.gelu(values, approximate=False), hidden)[1]
-    gh = gelu_pull(grad_gelled)[0].astype(BF)
-    grad_first = grad_second + right_dot(gh, we)
-    grad_attn, gain_one_grad, shift_one_grad = norm_backward(
-        grad_first, normed_one, inverse_one, gain_one
-    )
-    gal = grad_attn.astype(BF)
-    grad_ctx = right_dot(gal, wo).astype(BF)
-    dq, dk, dv = attend_back(q, key, val, grad_ctx, sq, sk)
-    dxp = right_dot(dk, wk) + right_dot(dv, wv)
-    dxo = grad_attn + right_dot(dq, wq) + lax.dynamic_slice_in_dim(dxp, own, 256, 0)
-
-    def column(v):
-        return jnp.sum(v.astype(F32), axis=0)
-
-    terms = [
-        column(dq), column(dv), column(gal), gain_one_grad, shift_one_grad, column(gb),
-        gain_two_grad, shift_two_grad,
-    ]
-    sums = jnp.concatenate(
-        [v.reshape(4, 256) for v in terms] + [column(gh).reshape(4, 1024)], axis=1
-    )
-    out, resf, dxf, vec = reduce_call(
-        gelled, gb, first_bf, gh, ctx, gal, xo, dq, xf, dk, dv, dxo, dxp.astype(BF),
-        result.astype(BF), sums.reshape(4, 24, 128),
+        cot.astype(F32), normed_two, inverse_two, gain_two
+    )
+    o_q, o_k, o_v, o_o, o_e, o_c, resf, dxf, vec = backward_call(
+        gelled, grad_second.astype(BF), grad_second, first_bf, gelu_slope, normed_one, inverse_one,
+        gain_one.reshape(1, 1024), ctx, q, key, val, xf, sq, sk, result.astype(BF),
+        gain_two_grad.reshape(1, 1024), shift_two_grad.reshape(1, 1024),
+        we, wc, wo, wq, wk, wv,
     )
     mine = vec.reshape(3072)
     vec_grads = [mine[i * 256 : (i + 1) * 256] for i in range(8)]
-    grads = out.astype(F32)
-
-    def square(start):
-        return grads[start : start + 2].reshape(256, 1024)
-
-    expand_grad = grads[8:16].reshape(4, 256, 1024).transpose(1, 0, 2).reshape(256, 4096)
     return (
         resf,
         dxf.astype(F32),
-        square(18),
-        square(20),
-        square(22),
-        square(16),
-        expand_grad,
-        grads[0:8].reshape(1024, 1024),
+        o_q.astype(F32),
+        o_k.astype(F32),
+        o_v.astype(F32),
+        o_o.astype(F32),
+        o_e.astype(F32),
+        o_c.astype(F32),
         vec_grads[0],
         vec_grads[1],
         vec_grads[2],

time: 421 us -> 361 us (0.86)
  matrix products: 54.8 us -> 18.7 us
  local copies, waits for them, and re-layouts: 43.9 us -> 28.3 us
  Pallas kernels: 308 us -> 294 us
  other arithmetic: 9.38 us -> 18.3 us
    dot_general x6 -> x0, matrix products: 30.6 us -> none  [right_dot(): lax.dot_general(left_side, right_side, (((1,), (1,)), ((), ())), preferre...]
    pallas_call x2 -> x1, Pallas kernels: 208 us -> 195 us  [backward_call(): pl.pallas_call(backward_kernel, out_shape=[grad, grad, grad, grad, jax.Sh...]
    convert_element_type x0 -> x7, other arithmetic: none -> 11.9 us  [the longest x1 2.5 us: per_group_device(): o_e.astype(F32)]
    unnamed x111 -> x82, local copies, waits for them, and re-layouts: 31.7 us -> 24.6 us
    slice x3 -> x0, local copies, waits for them, and re-layouts: 6.86 us -> none  [the longest x1 3.91 us: square(): return grads[start:start + 2].reshape(256, 1024)]
    reduce_sum x4 -> x0, other arithmetic: 5.89 us -> none  [column(): return jnp.sum(v.astype(F32), axis=0)]
    dot_general x6, matrix products: 24.1 us -> 18.7 us  [plain_dot(): return jnp.dot(left_side, right_side, preferred_element_type=jnp.float32)]
where the time goes in v3:
time: 361 us; the launch traced here: 360 us
  Pallas kernels  294 us (81%)
  local copies, waits for them, and re-layouts  28.3 us (8%)
  matrix products  18.7 us (5%)
  other arithmetic  18.3 us (5%)
    pallas_call x1, Pallas kernels, backward_call(): pl.pallas_call(backward_kernel, out_shape=[grad, grad, grad, grad, jax.Sh...  195 us
    pallas_call x1, Pallas kernels, gather_call(): pl.pallas_call(gather_kernel, out_shape=outs, in_specs=[any_spec] * 10, o...  84.1 us
    unnamed x82, local copies, waits for them, and re-layouts  24.6 us
    dot_general x6, matrix products, plain_dot(): return jnp.dot(left_side, right_side, preferred_element_type=jnp.float32)  18.7 us
    pallas_call x1, Pallas kernels, attend(): pl.pallas_call(attend_kernel, grid=(8,), out_shape=jax.ShapeDtypeStruct((...  15 us

profile of v3, /device:TPU:0, one launch (start us, length us, event | category | flops | bytes accessed | tf_op | source)
XLA Modules:
  0.0 360.0 jit_solution(1038929622699764465)
XLA Ops:
  8.1 1.6 copy-done.4
  9.7 1.6 copy-done.5
  11.3 1.0 copy-done.15
  12.3 1.0 copy-done.16
  13.4 1.0 copy-done.17
  14.4 1.0 copy-done.18
  15.4 1.0 copy-done.19
  16.5 1.0 copy-done.20
  18.2 84.1 %gather_all.1 = (bf16[1024,1024]{1,0:T(8,128)(2,1)S(1)}, bf16[256,1024]{1,0:T(8,128)(2,1)S(1)}, s32[8,1,128]{2,1,0:T(1,128)S(1)}, bf16[1024,1024]{1,0:T(8,128)(2...) custom-call(bf16[2,1,128,1024]{3,2,1,0:T(8,128)(2,1)S(1)} %copy-done, ...), custom_call_target="tpu_custom_call" | custom-call | tf_op jit(solution)/shard_map/gather_all/pallas_call | solution.py:686
  102.3 1.3 copy-done.7
  103.6 1.3 copy-done.8
  104.9 1.3 copy-done.10
  106.3 1.3 copy-done.12
  107.9 2.9 fusion.10.q_ref.q
  110.8 2.3 add_convert_fusion.v_ref.val
  113.1 2.3 convolution_convert_fusion.k_ref.key
  115.5 15.0 %attend.1.ctx = bf16[256,1024]{1,0:T(8,128)(2,1)S(1)} custom-call(bf16[256,1024]{1,0:T(8,128)(2,1)S(1)} %fusion.10.q_ref.q, bf16[1024,1024]{1,0:T(8,128)(2,1)S(1)} %convolution_convert_fusion.k_ref.key, bf16[1024,1024]{1,0:T(8,128)(2,1)S(1)} %add_convert_fusion.v_ref.val, s32[256,1]{1,0:T(8,128)S(1)} %copy.35.sq_ref.sq, s32[1,1024]{1,0:T(1,128)S(1)} %bitcast.55), custom_call_target="tpu_custom_call" | custom-call | tf_op jit(solution)/shard_map/attend/pallas_call | solution.py:743
  133.4 1.6 fusion.15
  135.1 7.9 %fusion.4 = (bf16[256,4096]{1,0:T(8,128)(2,1)}, bf16[256,4096]{1,0:T(8,128)(2,1)S(1)}) fusion(f32[4096]{0:T(1024)S(1)} %bitcast_convert_fusion, bf16[256,1024]{1,0:T(8,128)(2,1)S(1)} %get-tuple-element.61.fb, bf16[1024,4096]{1,0:T(8,128)(2,1)} %get-tuple-element.43.we), kind=kOutput, calls=%fused_computation.6 | convolution fusion | flops 2160066560 | bytes 13123584 | tf_op jit(solution)/shard_map/dot_general | solution.py:17
  143.1 2.4 fusion.22
  145.8 1.9 fusion.14
  147.7 1.5 fusion.18
  149.2 194.6 %backward_all.1 = (bf16[256,1024]{1,0:T(8,128)(2,1)}, bf16[256,1024]{1,0:T(8,128)(2,1)}, bf16[256,1024]{1,0:T(8,128)(2,1)}, bf16[256,1024]{1,0:T(8,128)(2,1)}, b...) custom-call(bf16[256,4096]{1,0:T(8,128)(2,1)} %copy-done.26, ...), custom_call_target="tpu_custom_call" | custom-call | tf_op jit(solution)/shard_map/backward_all/pallas_call | solution.py:1213
  343.8 1.3 slice_bitcast_fusion
  345.2 1.4 slice_bitcast_fusion.1
  346.6 2.2 convert_element_type.180
  348.8 2.2 convert_element_type.181
  351.0 1.1 convert_element_type.182
  352.1 1.1 convert_element_type.183
  353.1 1.1 convert_element_type.184
  354.2 2.5 convert_element_type.185
  356.7 2.5 convert_element_type.186
  (93 shorter events, 12.2 us)
Async XLA Ops:
  8.1 1.6 copy-start.4
  9.7 1.6 copy-start.5
  11.3 1.0 copy-start.15
  13.4 1.0 copy-start.17
  14.4 1.0 copy-start.18
  15.4 1.0 copy-start.19
  16.5 1.0 copy-start.20
  102.3 1.3 copy-start.7
  103.6 1.3 copy-start.8
  104.9 1.3 copy-start.10
  106.3 1.3 copy-start.12
  107.6 7.9 %copy-start.21 = (s32[8,1,128]{2,1,0:T(1,128)}, s32[8,1,128]{2,1,0:T(1,128)S(1)}, u32[]{:S(2)}) copy-start(s32[8,1,128]{2,1,0:T(1,128)S(1)} %get-tuple-element.41) | copy-start | bytes 12292
  107.6 23.0 %copy-start.6 = (bf16[1024,1024]{1,0:T(8,128)(2,1)}, bf16[1024,1024]{1,0:T(8,128)(2,1)S(1)}, u32[]{:S(2)}) copy-start(bf16[1024,1024]{1,0:T(8,128)(2,1)S(1)} %get-tuple-element.36.xf) | copy-start | bytes 6291460
  107.6 35.4 %copy-start.33 = (f32[4,2,128]{2,1,0:T(2,128)}, f32[4,2,128]{2,1,0:T(2,128)S(1)}, u32[]{:S(2)}) copy-start(f32[4,2,128]{2,1,0:T(2,128)S(1)} %get-tuple-element.70) | copy-start | bytes 12292
  107.8 7.6 %copy-start.14 = (s32[256,1]{1,0:T(8,128)}, s32[256,1]{1,0:T(8,128)S(1)}, u32[]{:S(2)}) copy-start(s32[256,1]{1,0:T(8,128)S(1)} %copy.35.sq_ref.sq) | copy-start | bytes 3076
  107.8 2.9 copy-start.11
  110.7 4.7 %copy-start.2 = (bf16[256,1024]{1,0:T(8,128)(2,1)}, bf16[256,1024]{1,0:T(8,128)(2,1)S(1)}, u32[]{:S(2)}) copy-start(bf16[256,1024]{1,0:T(8,128)(2,1)S(1)} %fusion.10.q_ref.q) | copy-start | bytes 1572868
  110.7 2.4 copy-start.9
  113.1 2.4 copy-start
  115.5 15.0 %copy-start.1 = (bf16[1024,1024]{1,0:T(8,128)(2,1)}, bf16[1024,1024]{1,0:T(8,128)(2,1)S(1)}, u32[]{:S(2)}) copy-start(bf16[1024,1024]{1,0:T(8,128)(2,1)S(1)} %convolution_convert_fusion.k_ref.key) | copy-start | bytes 6291460
  115.5 15.0 %copy-start.13 = (bf16[1024,1024]{1,0:T(8,128)(2,1)S(1)}, bf16[1024,1024]{1,0:T(8,128)(2,1)}, u32[]{:S(2)}) copy-start(bf16[1024,1024]{1,0:T(8,128)(2,1)} %copy-done.12) | copy-start | bytes 6291460
  133.4 9.6 %slice-start = ((s8[8388608]{0:T(1024)(128)(4,1)}), s8[4194304]{0:T(1024)(128)(4,1)S(1)}, s32[]{:S(2)}) async-start(s8[8388608]{0:T(1024)(128)(4,1)} %bitcast.58), calls=%async_computation | async-start | bytes 8388608
  135.1 7.9 %copy-start.25 = (bf16[256,1024]{1,0:T(8,128)(2,1)}, bf16[256,1024]{1,0:T(8,128)(2,1)S(1)}, u32[]{:S(2)}) copy-start(bf16[256,1024]{1,0:T(8,128)(2,1)S(1)} %get-tuple-element.61.fb) | copy-start | bytes 1572868
  135.1 7.9 %copy-start.23 = (f32[256,1024]{1,0:T(8,128)}, f32[256,1024]{1,0:T(8,128)S(1)}, u32[]{:S(2)}) copy-start(f32[256,1024]{1,0:T(8,128)S(1)} %get-tuple-element.62.n1) | copy-start | bytes 3145732
  135.1 8.0 %slice-start.1 = ((s8[8388608]{0:T(1024)(128)(4,1)}), s8[4194304]{0:T(1024)(128)(4,1)S(1)}, s32[]{:S(2)}) async-start(s8[8388608]{0:T(1024)(128)(4,1)} %bitcast.58), calls=%async_computation.1 | async-start | bytes 8388608
  143.0 2.5 copy-start.26
  343.8 7.1 %copy-start.31 = (bf16[256,1024]{1,0:T(8,128)(2,1)S(1)}, bf16[256,1024]{1,0:T(8,128)(2,1)}, u32[]{:S(2)}) copy-start(bf16[256,1024]{1,0:T(8,128)(2,1)} %get-tuple-element.49) | copy-start | bytes 1572868
  346.6 5.5 %copy-start.30 = (bf16[256,1024]{1,0:T(8,128)(2,1)S(1)}, bf16[256,1024]{1,0:T(8,128)(2,1)}, u32[]{:S(2)}) copy-start(bf16[256,1024]{1,0:T(8,128)(2,1)} %get-tuple-element.50) | copy-start | bytes 1572868
  348.8 4.4 %copy-start.29 = (bf16[256,1024]{1,0:T(8,128)(2,1)S(1)}, bf16[256,1024]{1,0:T(8,128)(2,1)}, u32[]{:S(2)}) copy-start(bf16[256,1024]{1,0:T(8,128)(2,1)} %get-tuple-element.51) | copy-start | bytes 1572868
  351.0 3.3 copy-start.28
  354.2 2.5 copy-start.27
  356.7 2.5 copy-start.32
  (4 other events, 3.5 us)

commit v4 on v3

--- a/solution.py
+++ b/solution.py
@@ -1,3 +1,5 @@
+import math
+
 import jax
 import jax.numpy as jnp
 from jax import lax
@@ -421,6 +423,7 @@
 SLOTS = 3
 LAND = 4
 ROOM = 8
+Y_ROWS, X_ROWS = 48, 8
 
 
 def coords():
@@ -454,19 +457,52 @@
     return pl.ds(pl.multiple_of(start, unit), size)
 
 
-def gather_kernel(
-    inp, cot, seg, wq, wk, wv, wo, we, wc, vec,
-    xf, cotf, segf, fq, fk, fv, fo, fe, fc, vecf,
-    own, a_send, a_recv, g_send, g_recv, w_send, w_recv, v_send, v_recv,
+def two_heads(block):
+    lane = lax.broadcasted_iota(jnp.int32, block.shape, 1)
+    zero = jnp.zeros_like(block)
+    return jnp.concatenate(
+        [jnp.where(lane < HEAD_DIM, block, zero), jnp.where(lane >= HEAD_DIM, block, zero)], axis=0
+    )
+
+
+def one_block(pair):
+    rows = pair.shape[0] // 2
+    lane = lax.broadcasted_iota(jnp.int32, (rows, pair.shape[1]), 1)
+    return jnp.where(lane < HEAD_DIM, pair[:rows], pair[rows:])
+
+
+def softmax_pair(queries, keys, bias):
+    scores = right_dot(queries, keys)
+    scores = scores + jnp.concatenate([bias, bias], axis=0)
+    numer = jnp.exp(scores - jnp.max(scores, axis=-1, keepdims=True))
+    return numer * (1.0 / jnp.sum(numer, axis=-1, keepdims=True))
+
+
+def layer_kernel(
+    inp, cot, seg, wq, wk, wv, wo, we, wc, *rest,
 ):
+    (
+        vecs, (fq, fk, fv, fo, fe, fc), (o_q, o_k, o_v, o_o, o_e, o_c), (resf, dxf, vec_out), rest
+    ) = (rest[:9], rest[9:15], rest[15:21], rest[21:24], rest[24:])
+    (
+        s_d, l_d, r_d, b_y, r_y, b_x, r_x, b_1, r_1, b_2, r_2, o_b,
+        gh, acc, ga, gal, dctx, dq, dk, dv, bias, we_b, wc_b, w_b,
+        dx_p, dx_r, dx_s, dx_y, vec, v_s, v_d, v_r,
+        gel, gb, fb, gp, n1, inv1, ctx, q, key, val, xf, res, cotf, segf, vec_in, vecf, row8, row_e,
+        ss, rs, ds, dr, a_send, a_recv, v_send, v_recv, w_sem, o_sem,
+        i_send, i_recv, g_send, g_recv, p_send, p_recv, f_send, f_recv,
+    ) = rest
+    dx_b = dctx
     z, x, y, k = coords()
     f = y * 2 + k
     other = (1 - y) * 2 + k
     sib, xn, yn = dev(z, x, y, 1 - k), dev(z, 1 - x, y, k), dev(z, x, 1 - y, k)
-    zn = dev(z + 1 - 2 * (z % 2), x, y, k)
-    color = (z % 2) * 2 + x
+    bit1, bit2 = z % 2, z // 2
+    z1 = dev(z + 1 - 2 * bit1, x, y, k)
+    z2 = dev((z + 2) % 4, x, y, k)
+    color = bit1 * 2 + x
     c_x, c_z, c_o = color + 1 - 2 * x, (color + 2) % 4, 3 - color
-    greet(z, x, y, k)
+    own_rows = rows_of(x * 512 + k * 256, 256)
 
     def block_moves(mb):
         to_z, to_k = mb * 2 + k, z // 2
@@ -489,11 +525,11 @@
 
                 @pl.when(mine)
                 def _():
-                    pltpu.make_async_copy(src, dst, a_recv.at[n, slot]).start()
+                    pltpu.make_async_copy(src, dst, i_recv.at[n, slot]).start()
 
                 @pl.when(jnp.logical_not(mine))
                 def _():
-                    remote(src, dst, a_send.at[n, mb], a_recv.at[n, slot], to).start()
+                    remote(src, dst, i_send.at[n, mb], i_recv.at[n, slot], to).start()
 
     def finish_blocks(which):
         for mb in range(2):
@@ -504,7 +540,7 @@
 
                 @pl.when(jnp.logical_not(mine))
                 def _():
-                    remote(src, dst, a_send.at[n, mb], a_recv.at[n, slot], to).wait_send()
+                    remote(src, dst, i_send.at[n, mb], i_recv.at[n, slot], to).wait_send()
 
     def arrive_blocks(which):
         for slot in range(2):
@@ -516,7 +552,7 @@
                     dst = segf.at[x * 4 + zz]
                 else:
                     dst = cotf.at[pl.ds(slot * 128, 128)]
-                pltpu.make_async_copy(dst, dst, a_recv.at[n, slot]).wait()
+                pltpu.make_async_copy(dst, dst, i_recv.at[n, slot]).wait()
 
     def group_copy(step):
         who = x if step < 2 else 1 - x
@@ -548,27 +584,27 @@
     def part(i, quarter, start, size, own_src=False):
         shard, full, row, col, step = items[i]
         if own_src:
-            return shard.at[rows_of(row + start, size), pl.ds(col, 1024)]
-        return full.at[rows_of(quarter * step + row + start, size), pl.ds(col, 1024)]
+            return shard.at[rows_of(row + start, size, 8), pl.ds(col, 1024)]
+        return full.at[rows_of(quarter * step + row + start, size, 8), pl.ds(col, 1024)]
 
     def send_copy(i, kind):
-        sems = (w_send.at[kind, i], w_recv.at[kind, i])
+        sems = (p_send.at[kind, i], p_recv.at[kind, i])
         if kind == 0:
             return remote(part(i, f, color * 64, 64, True), part(i, f, color * 64, 64), *sems, yn)
         if kind == 1:
-            return remote(part(i, f, c_o * 64, 32, True), part(i, f, c_o * 64, 32), *sems, yn)
+            return remote(part(i, f, c_o * 64, Y_ROWS, True), part(i, f, c_o * 64, Y_ROWS), *sems, yn)
         if kind == 2:
             src = part(i, other, color * 64, 64)
             return remote(src, src, *sems, xn)
         if kind == 3:
-            src = part(i, other, c_z * 64 + 32, 16)
+            src = part(i, other, c_z * 64 + Y_ROWS, X_ROWS)
             return remote(src, src, *sems, xn)
         if kind == 4:
             src = part(i, other, color * 64, 64)
-            return remote(src, src, *sems, zn)
+            return remote(src, src, *sems, z1)
         if kind == 5:
-            src = part(i, other, c_x * 64 + 48, 16)
-            return remote(src, src, *sems, zn)
+            src = part(i, other, c_x * 64 + Y_ROWS + X_ROWS, X_ROWS)
+            return remote(src, src, *sems, z1)
         if kind == 6:
             return remote(part(i, f, 0, 256, True), part(i, f, 0, 256), *sems, sib)
         src = part(i, other, 0, 256)
@@ -578,61 +614,98 @@
         if kind == 0:
             dst = part(i, other, color * 64, 64)
         elif kind == 1:
-            dst = part(i, other, c_o * 64, 32)
+            dst = part(i, other, c_o * 64, Y_ROWS)
         elif kind == 2:
             dst = part(i, other, c_x * 64, 64)
         elif kind == 3:
-            dst = part(i, other, c_o * 64 + 32, 16)
+            dst = part(i, other, c_o * 64 + Y_ROWS, X_ROWS)
         elif kind == 4:
             dst = part(i, other, c_z * 64, 64)
         elif kind == 5:
-            dst = part(i, other, c_o * 64 + 48, 16)
+            dst = part(i, other, c_o * 64 + Y_ROWS + X_ROWS, X_ROWS)
         elif kind == 6:
             dst = part(i, y * 2 + 1 - k, 0, 256)
         else:
             dst = part(i, (1 - y) * 2 + 1 - k, 0, 256)
-        pltpu.make_async_copy(dst, dst, w_recv.at[kind, i]).wait()
-
-    def own_in(i):
-        return pltpu.make_async_copy(part(i, f, 0, 256, True), own.at[i], w_recv.at[8, i])
-
-    def own_out(i):
-        return pltpu.make_async_copy(own.at[i], part(i, f, 0, 256), w_recv.at[9, i])
-
+        pltpu.make_async_copy(dst, dst, p_recv.at[kind, i]).wait()
+
+
+    for i in range(8):
+        packed = vecs[i][...].astype(F32).reshape(1, 256)
+        vec_in[pl.ds(2 * i, 1)] = packed[:, :128]
+        vec_in[pl.ds(2 * i + 1, 1)] = packed[:, 128:]
+    packed = vecs[8][...].astype(F32).reshape(1, 1024)
+    for n in range(8):
+        vec_in[pl.ds(16 + n, 1)] = packed[:, n * 128 : n * 128 + 128]
+    vecf[f] = vec_in[...]
     vec_copies = (
-        remote(vec, vecf.at[f], v_send.at[0], v_recv.at[0], yn),
-        remote(vec, vecf.at[f], v_send.at[1], v_recv.at[1], sib),
-        remote(vecf.at[other], vecf.at[other], v_send.at[2], v_recv.at[2], sib),
-    )
-    vec_own = pltpu.make_async_copy(vec, vecf.at[f], v_recv.at[3])
-
-    start_blocks((0, 1))
-    vec_own.start()
-    for i in range(n_items):
-        own_in(i).start()
-    vec_copies[0].start()
-    vec_copies[1].start()
-    for t in range(n_items + 3):
-        if t < n_items:
-            send_copy(t, 0).start()
-            send_copy(t, 1).start()
-            send_copy(t, 6).start()
-        if t == 1:
-            arrive_blocks((0, 1))
-            for step in range(2):
-                for move in group_copy(step):
-                    move.start()
-            pltpu.make_async_copy(vecf.at[other], vecf.at[other], v_recv.at[0]).wait()
-            vec_copies[2].start()
-        if t == 4:
-            group_arrive(1)
-            for move in group_copy(2):
-                move.start()
-            start_blocks((2,))
+        remote(vec_in, vecf.at[f], f_send.at[0], f_recv.at[0], yn),
+        remote(vec_in, vecf.at[f], f_send.at[1], f_recv.at[1], sib),
+        remote(vecf.at[other], vecf.at[other], f_send.at[2], f_recv.at[2], sib),
+    )
+
+    def load_square(shard, full, row, step, cols, dst, sem):
+        out = []
+        for d in range(4):
+            quarter = (f + d) % 4
+            src = shard.at[pl.ds(row, 256), cols]
+            if d > 0:
+                src = full.at[rows_of(quarter * step + row, 256), cols]
+            out.append(pltpu.make_async_copy(src, dst.at[rows_of(quarter * 256, 256)], sem))
+        return out
+
+    def load_c(j):
+        slot = j % 2
+        sem = w_sem.at[slot]
+
+        @pl.when(j // 2 == f)
+        def _():
+            src = wc.at[rows_of((j % 2) * 512, 512)]
+            pltpu.make_async_copy(src, wc_b.at[slot], sem).start()
+
+        @pl.when(j // 2 != f)
+        def _():
+            pltpu.make_async_copy(fc.at[rows_of(j * 512, 512)], wc_b.at[slot], sem).start()
+
+    def load_e(j):
+        for move in load_square(
+            we, fe, 0, 256, rows_of(j * 512, 512, 512), we_b.at[j % 2], w_sem.at[2 + j % 2]
+        ):
+            move.start()
+
+    def load_w(n):
+        shard, full = ((wo, fo), (wk, fk), (wv, fv), (wq, fq))[n]
+        for move in load_square(
+            shard, full, 0, 256, pl.ds(0, 1024), w_b.at[n], w_sem.at[4 + n]
+        ):
+            move.start()
+
+    def loaded_w(n):
+        pltpu.make_async_copy(w_b.at[n], w_b.at[n], w_sem.at[4 + n]).wait()
+
+    def load_item(i):
+        shard, full, row, col, step = items[i]
+        arrive(i, 6)
+        arrive(i, 7)
+        slot = i % 4
+        for move in load_square(
+            shard, full, row, step, pl.ds(col, 1024), w_b.at[slot], w_sem.at[4 + slot]
+        ):
+            move.start()
+
+    def item(i):
+        slot = i % 4
+        pltpu.make_async_copy(w_b.at[slot], w_b.at[slot], w_sem.at[4 + slot]).wait()
+        return w_b.at[slot]
+
+    def relay(t):
+        for u in (0, 1, 2) if t == 0 else (t + 2,):
+            if u < n_items:
+                send_copy(u, 0).start()
+                send_copy(u, 1).start()
+                send_copy(u, 6).start()
         if 1 <= t <= n_items:
             i = t - 1
-            own_in(i).wait()
-            own_out(i).start()
             arrive(i, 0)
             send_copy(i, 2).start()
             send_copy(i, 4).start()
@@ -642,149 +715,106 @@
             send_copy(i, 3).start()
             arrive(i, 2)
             send_copy(i, 5).start()
-        if 3 <= t:
+        if 3 <= t <= n_items + 2:
             i = t - 3
             arrive(i, 1)
             arrive(i, 3)
             arrive(i, 5)
             send_copy(i, 7).start()
-    for i in range(n_items):
-        arrive(i, 6)
-        arrive(i, 7)
-        own_out(i).wait()
-        for kind in range(8):
-            send_copy(i, kind).wait_send()
-    arrive_blocks((2,))
-    finish_blocks((0, 1, 2))
-    group_arrive(0)
-    group_arrive(2)
-    for step in range(3):
-        for move in group_copy(step):
-            move.wait_send()
-    sib_own, sib_other = vecf.at[y * 2 + 1 - k], vecf.at[(1 - y) * 2 + 1 - k]
-    pltpu.make_async_copy(sib_own, sib_own, v_recv.at[1]).wait()
-    pltpu.make_async_copy(sib_other, sib_other, v_recv.at[2]).wait()
-    for move in vec_copies:
-        move.wait_send()
-    vec_own.wait()
-
-
-def gather_call(inp, cot, seg, weights, vec):
-    any_spec = pl.BlockSpec(memory_space=pl.ANY)
-    outs = [
-        jax.ShapeDtypeStruct((1024, 1024), BF),
-        jax.ShapeDtypeStruct((256, 1024), BF),
-        jax.ShapeDtypeStruct((8, 1, 128), jnp.int32),
-    ]
-    outs += [jax.ShapeDtypeStruct((1024, 1024), BF)] * 4
-    outs += [
-        jax.ShapeDtypeStruct((1024, 4096), BF),
-        jax.ShapeDtypeStruct((4096, 1024), BF),
-        jax.ShapeDtypeStruct((4, 32, 128), BF),
-    ]
-    dma = pltpu.SemaphoreType.DMA
-    return pl.pallas_call(
-        gather_kernel,
-        out_shape=outs,
-        in_specs=[any_spec] * 10,
-        out_specs=[any_spec] * 10,
-        scratch_shapes=[
-            pltpu.VMEM((12, 256, 1024), BF),
-            dma((3, 2)), dma((3, 2)), dma((2, 3)), dma((2, 3)),
-            dma((8, 12)), dma((10, 12)), dma((3,)), dma((4,)),
-        ],
-        compiler_params=pltpu.CompilerParams(
-            collective_id=0, has_side_effects=True, vmem_limit_bytes=32 << 20
-        ),
-        name="gather_all",
-    )(inp, cot, seg, *weights, vec)
-
-
-def two_heads(block):
-    lane = lax.broadcasted_iota(jnp.int32, block.shape, 1)
-    zero = jnp.zeros_like(block)
-    return jnp.concatenate(
-        [jnp.where(lane < HEAD_DIM, block, zero), jnp.where(lane >= HEAD_DIM, block, zero)], axis=0
-    )
-
-
-def one_block(pair):
-    rows = pair.shape[0] // 2
-    lane = lax.broadcasted_iota(jnp.int32, (rows, pair.shape[1]), 1)
-    return jnp.where(lane < HEAD_DIM, pair[:rows], pair[rows:])
-
-
-def attention_bias(sq_ref, sk_ref):
-    return jnp.where(sq_ref[...] == sk_ref[...], 0.0, -1e30).astype(F32)
-
-
-def softmax_pair(queries, keys, bias):
-    scores = right_dot(queries, keys)
-    scores = scores + jnp.concatenate([bias, bias], axis=0)
-    numer = jnp.exp(scores - jnp.max(scores, axis=-1, keepdims=True))
-    return numer * (1.0 / jnp.sum(numer, axis=-1, keepdims=True))
-
-
-def attend_kernel(q_ref, k_ref, v_ref, sq_ref, sk_ref, o_ref, bias_ref):
-    @pl.when(pl.program_id(0) == 0)
-    def _():
-        bias_ref[...] = attention_bias(sq_ref, sk_ref)
-
-    queries = two_heads(q_ref[...] * BF(HEAD_DIM**-0.5))
-    probs = softmax_pair(queries, k_ref[...], bias_ref[...])
-    o_ref[...] = one_block(plain_dot(probs.astype(BF), v_ref[...])).astype(BF)
-
-
-def attend(q, k, v, sq, sk):
-    rows = pl.BlockSpec((256, 128), lambda h: (0, h))
-    full = pl.BlockSpec((1024, 128), lambda h: (0, h))
-    sqs = pl.BlockSpec((256, 1), lambda h: (0, 0))
-    sks = pl.BlockSpec((1, 1024), lambda h: (0, 0))
-    return pl.pallas_call(
-        attend_kernel,
-        grid=(8,),
-        out_shape=jax.ShapeDtypeStruct((256, 1024), BF),
-        in_specs=[rows, full, full, sqs, sks],
-        out_specs=rows,
-        scratch_shapes=[pltpu.VMEM((256, 1024), F32)],
-        compiler_params=pltpu.CompilerParams(vmem_limit_bytes=40 << 20),
-        name="attend",
-    )(q, k, v, sq, sk)
-
-
-def backward_kernel(
-    gel, gb, gs, fb, gp, n1, inv1, gain1, ctx, q, key, val, xf, sq, sk, res, g2, s2,
-    we, wc, wo, wq, wk, wv,
-    o_q, o_k, o_v, o_o, o_e, o_c, resf, dxf, vec_out,
-    s_d, l_d, r_d, b_y, r_y, b_x, r_x, b_1, r_1, b_2, r_2, o_b,
-    gh, acc, ga, gal, dctx, dq, dk, dv, bias, we_b, wc_b, w_b,
-    dx_p, dx_r, dx_s, dx_y, dx_b, vec, v_s, v_d, v_r,
-    ss, rs, ds, dr, a_send, a_recv, v_send, v_recv, w_sem, o_sem,
-):
-    z, x, y, k = coords()
-    sib, xn, yn = dev(z, x, y, 1 - k), dev(z, 1 - x, y, k), dev(z, x, 1 - y, k)
-    bit1, bit2 = z % 2, z // 2
-    z1 = dev(z + 1 - 2 * bit1, x, y, k)
-    z2 = dev((z + 2) % 4, x, y, k)
-
-    def load_c(j):
-        return pltpu.make_async_copy(
-            wc.at[rows_of(j * 512, 512)], wc_b.at[j % 2], w_sem.at[j % 2]
+
+    def fill_rows():
+        pltpu.make_async_copy(vec_in, vec_in, f_recv.at[1]).wait()
+        pltpu.make_async_copy(vec_in, vec_in, f_recv.at[2]).wait()
+        for quarter in range(4):
+            for i in range(8):
+                for half in range(2):
+                    col = quarter * 256 + half * 128
+                    row8[pl.ds(i, 1), col : col + 128] = vecf[quarter, pl.ds(2 * i + half, 1)]
+            for n in range(8):
+                col = quarter * 1024 + n * 128
+                row_e[:, col : col + 128] = vecf[quarter, pl.ds(16 + n, 1)]
+
+    def fill_bias():
+        for block in range(2):
+            own = segf[x * 4 + k * 2 + block].astype(F32)
+            down = jnp.transpose(jnp.broadcast_to(own, (128, 128)))
+            for n in range(8):
+                across = segf[n].astype(F32)
+                bias[block * 128 : block * 128 + 128, n * 128 : n * 128 + 128] = jnp.where(
+                    down == across, 0.0, -1e30
+                )
+
+    def project_own(w):
+        q[...] = (plain_dot(xf[own_rows], w[...]) + row8[0:1]).astype(BF)
+
+    def project_all(w, dst, add_row):
+        def block(n, carry):
+            rows = rows_of(n * 256, 256)
+            dst[rows] = (plain_dot(xf[rows], w[...]) + add_row).astype(BF)
+            return carry
+
+        lax.fori_loop(0, 4, block, 0)
+
+    def heads(first, last):
+        def one(h, carry):
+            cols = rows_of(h * 128, 128, 128)
+            queries = two_heads(q[:, cols] * BF(HEAD_DIM**-0.5))
+            probs = softmax_pair(queries, key[:, cols], bias[...])
+            ctx[:, cols] = one_block(plain_dot(probs.astype(BF), val[:, cols])).astype(BF)
+            return carry
+
+        lax.fori_loop(first, last, one, 0)
+
+    def norm(v):
+        centre = v - jnp.mean(v, axis=-1, keepdims=True)
+        inverse = lax.rsqrt(jnp.mean(centre * centre, axis=-1, keepdims=True) + 1e-05)
+        return centre * inverse, inverse
+
+    def attention_out(w):
+        normed, inverse = norm(
+            xf[own_rows].astype(F32) + plain_dot(ctx[...], w[...]) + row8[2:3]
         )
-
-    def load_e(j):
-        return pltpu.make_async_copy(
-            we.at[:, rows_of(j * 512, 512, 512)], we_b.at[j % 2], w_sem.at[2 + j % 2]
+        n1[...] = normed
+        inv1[...] = inverse
+        first_out = normed * row8[3:4] + row8[4:5]
+        acc[...] = first_out
+        fb[...] = first_out.astype(BF)
+
+    def expand(j, w):
+        def block(n, carry):
+            cols = rows_of(n * 256, 256, 256)
+            out = rows_of(j * 1024 + n * 256, 256, 256)
+            hidden = plain_dot(fb[...], w[:, cols]) + row_e[:, out]
+            below = 0.5 + 0.5 * lax.erf(hidden * 0.5**0.5)
+            gel[:, out] = (hidden * below).astype(BF)
+            bell = jnp.exp(-0.5 * hidden * hidden) * (2 * math.pi) ** -0.5
+            gp[:, out] = (below + hidden * bell).astype(BF)
+            return carry
+
+        lax.fori_loop(0, 4, block, 0)
+
+    def contract(j, w):
+        for quarter in range(4):
+            cols = pl.ds(quarter * 1024 + j * 256, 256)
+            acc[...] += plain_dot(gel[:, cols], w[quarter * 256 : quarter * 256 + 256])
+
+    def second_norm():
+        normed, inverse = norm(acc[...] + row8[5:6])
+        res[...] = (normed * row8[6:7] + row8[7:8]).astype(BF)
+        grad_out = cotf[...].astype(F32)
+        keep(6, column(grad_out * normed))
+        keep(7, column(grad_out))
+        scaled = grad_out * row8[6:7]
+        grad = inverse * (
+            scaled
+            - jnp.mean(scaled, axis=-1, keepdims=True)
+            - normed * jnp.mean(scaled * normed, axis=-1, keepdims=True)
         )
-
-    def load_w(n):
-        return pltpu.make_async_copy((wo, wk, wv, wq)[n], w_b.at[n], w_sem.at[4 + n])
-
-    load_c(0).start()
-    load_e(0).start()
-    for n in range(4):
-        load_w(n).start()
-    greet(z, x, y, k)
+        acc[...] = grad
+        low = grad.astype(BF)
+        gb[...] = low
+        keep(5, column(low))
+
 
     def back(n, slot):
         to_z = 2 * k + slot
@@ -827,8 +857,6 @@
         for mb in range(2):
             dst = (resf, dxf)[n].at[mb, 0]
             pltpu.make_async_copy(dst, dst, a_recv.at[n, mb]).wait()
-
-    start_back(0)
 
     def column(v):
         return jnp.sum(v.astype(F32), axis=0, keepdims=True)
@@ -920,7 +948,6 @@
                     s_d[slot, plane] = product
 
     every = pl.ds(0, 1024)
-    own_rows = rows_of(x * 512 + k * 256, 256)
 
     def stage_zero(i):
         @pl.when((i >= 0) & (i < CHUNKS))
@@ -987,13 +1014,13 @@
     def feed_forward(j):
         slot = j % 2
         cols = rows_of(j * 512, 512, 512)
-        load_c(j).wait()
-        load_e(j).wait()
+        pltpu.make_async_copy(wc_b.at[slot], wc_b.at[slot], w_sem.at[slot]).wait()
+        pltpu.make_async_copy(we_b.at[slot], we_b.at[slot], w_sem.at[2 + slot]).wait()
 
         @pl.when(j < 7)
         def _():
-            load_c(j + 1).start()
-            load_e(j + 1).start()
+            load_c(j + 1)
+            load_e(j + 1)
 
         grads = (right_dot(gb[...], wc_b[slot]) * gp[:, cols].astype(F32)).astype(BF)
         gh[:, cols] = grads
@@ -1007,7 +1034,7 @@
         grad_first = acc[...]
         keep(3, column(grad_first * normed))
         keep(4, column(grad_first))
-        scaled = grad_first * gain1[...]
+        scaled = grad_first * row8[3:4]
         grad_attn = inv1[...] * (
             scaled
             - jnp.mean(scaled, axis=-1, keepdims=True)
@@ -1017,7 +1044,7 @@
         low = grad_attn.astype(BF)
         gal[...] = low
         keep(2, column(low))
-        load_w(0).wait()
+        loaded_w(0)
         dctx[...] = right_dot(low, w_b[0]).astype(BF)
 
     def attention(h):
@@ -1063,14 +1090,66 @@
         @pl.when(n == 3)
         def _():
             pltpu.make_async_copy(dx_r.at[0], dx_r.at[0], dr.at[0]).wait()
-            load_w(3).wait()
+            loaded_w(3)
             ga[...] = ga[...] + terms_here + dx_r[0].astype(F32) + right_dot(dq[...], w_b[3])
 
-    bias[...] = attention_bias(sq, sk)
-    acc[...] = gs[...]
-    keep(5, column(gb[...]))
-    keep(6, g2[...])
-    keep(7, s2[...])
+    greet(z, x, y, k)
+    start_blocks((0, 1))
+    vec_copies[0].start()
+    vec_copies[1].start()
+    relay(0)
+    relay(1)
+    arrive_blocks((0, 1))
+    for step in range(2):
+        for move in group_copy(step):
+            move.start()
+    pltpu.make_async_copy(vec_in, vec_in, f_recv.at[0]).wait()
+    vec_copies[2].start()
+    relay(2)
+    relay(3)
+    group_arrive(1)
+    for move in group_copy(2):
+        move.start()
+    start_blocks((2,))
+    relay(4)
+    load_item(0)
+    fill_rows()
+    relay(5)
+    load_item(1)
+    project_own(item(0))
+    relay(6)
+    load_item(2)
+    group_arrive(0)
+    group_arrive(2)
+    fill_bias()
+    project_all(item(1), key, 0.0)
+    relay(7)
+    load_item(3)
+    project_all(item(2), val, row8[1:2])
+    relay(8)
+    load_item(4)
+    heads(0, 3)
+    relay(9)
+    load_item(5)
+    heads(3, 6)
+    relay(10)
+    load_item(6)
+    heads(6, 8)
+    attention_out(item(3))
+    for j in range(4):
+        relay(11 + j)
+        load_item(7 + j)
+        expand(j, item(4 + j))
+    load_item(11)
+    for j in range(4):
+        contract(j, item(8 + j))
+    arrive_blocks((2,))
+    load_c(0)
+    load_e(0)
+    for n in range(4):
+        load_w(n)
+    second_norm()
+    start_back(0)
 
     def tick(t, carry):
         def at(stage):
@@ -1105,8 +1184,8 @@
         def _():
             keep(0, column(dq[...]))
             keep(1, column(dv[...]))
-            load_w(1).wait()
-            load_w(2).wait()
+            loaded_w(1)
+            loaded_w(2)
 
         @pl.when((t >= 17) & (t < 21))
         def _():
@@ -1203,16 +1282,29 @@
     dx_far.wait_send()
     finish_back(0)
     finish_back(1)
-
-
-def backward_call(*operands):
+    for i in range(n_items):
+        for kind in range(8):
+            send_copy(i, kind).wait_send()
+    finish_blocks((0, 1, 2))
+    for step in range(3):
+        for move in group_copy(step):
+            move.wait_send()
+    for move in vec_copies:
+        move.wait_send()
+
+
+def layer_call(inp, cot, seg, weights, vectors):
     vmem = pl.BlockSpec(memory_space=pltpu.VMEM)
     any_spec = pl.BlockSpec(memory_space=pl.ANY)
     dma = pltpu.SemaphoreType.DMA
     grad = jax.ShapeDtypeStruct((256, 1024), BF)
+    square = jax.ShapeDtypeStruct((1024, 1024), BF)
+    full_weights = [square] * 4 + [
+        jax.ShapeDtypeStruct((1024, 4096), BF), jax.ShapeDtypeStruct((4096, 1024), BF)
+    ]
     return pl.pallas_call(
-        backward_kernel,
-        out_shape=[
+        layer_kernel,
+        out_shape=full_weights + [
             grad, grad, grad, grad,
             jax.ShapeDtypeStruct((256, 4096), BF),
             jax.ShapeDtypeStruct((1024, 1024), BF),
@@ -1220,8 +1312,8 @@
             jax.ShapeDtypeStruct((2, 1, 128, 1024), BF),
             jax.ShapeDtypeStruct((24, 128), F32),
         ],
-        in_specs=[vmem] * 18 + [any_spec] * 6,
-        out_specs=[any_spec] * 8 + [vmem],
+        in_specs=[any_spec] * 9 + [vmem] * 9,
+        out_specs=[any_spec] * 14 + [vmem],
         scratch_shapes=[
             pltpu.VMEM((SLOTS, 2, 128, 1024), BF),
             pltpu.VMEM((SLOTS, 2, 128, 1024), BF),
@@ -1251,19 +1343,38 @@
             pltpu.VMEM((2, 256, 1024), BF),
             pltpu.VMEM((256, 1024), BF),
             pltpu.VMEM((256, 1024), BF),
-            pltpu.VMEM((256, 1024), BF),
             pltpu.VMEM((4, 24, 128), F32),
             pltpu.VMEM((4, 2, 24, 128), F32),
             pltpu.VMEM((3, 2, 24, 128), F32),
             pltpu.VMEM((4, 24, 128), F32),
+            pltpu.VMEM((256, 4096), BF),
+            pltpu.VMEM((256, 1024), BF),
+            pltpu.VMEM((256, 1024), BF),
+            pltpu.VMEM((256, 4096), BF),
+            pltpu.VMEM((256, 1024), F32),
+            pltpu.VMEM((256, 1), F32),
+            pltpu.VMEM((256, 1024), BF),
+            pltpu.VMEM((256, 1024), BF),
+            pltpu.VMEM((1024, 1024), BF),
+            pltpu.VMEM((1024, 1024), BF),
+            pltpu.VMEM((1024, 1024), BF),
+            pltpu.VMEM((256, 1024), BF),
+            pltpu.VMEM((256, 1024), BF),
+            pltpu.VMEM((8, 1, 128), jnp.int32),
+            pltpu.VMEM((24, 128), F32),
+            pltpu.VMEM((4, 24, 128), F32),
+            pltpu.VMEM((8, 1024), F32),
+            pltpu.VMEM((1, 4096), F32),
             dma((8, SLOTS)), dma((8, LAND)), dma((3,)), dma((3,)), dma((2, 2)), dma((2, 2)),
             dma((5,)), dma((5,)), dma((8,)), dma(()),
+            dma((3, 2)), dma((3, 2)), dma((2, 3)), dma((2, 3)),
+            dma((8, 12)), dma((8, 12)), dma((3,)), dma((3,)),
         ],
         compiler_params=pltpu.CompilerParams(
-            collective_id=1, has_side_effects=True, vmem_limit_bytes=61 << 20
+            collective_id=0, has_side_effects=True, vmem_limit_bytes=61 << 20
         ),
-        name="backward_all",
-    )(*operands)
+        name="layer",
+    )(inp, cot, seg, *weights, *vectors)
 
 
 def per_group_device(
@@ -1272,51 +1383,15 @@
     query_bias, value_bias, output_bias, first_gain, first_shift, expand_bias, contract_bias,
     second_gain, second_shift,
 ):
-    weights = (
-        query_weight, key_weight, value_weight, output_weight, expand_weight, contract_weight
-    )
-    packed = jnp.concatenate(
-        [
+    outs = layer_call(
+        layer_input, cotangent, segments,
+        (query_weight, key_weight, value_weight, output_weight, expand_weight, contract_weight),
+        (
             query_bias, value_bias, output_bias, first_gain, first_shift, contract_bias,
-            second_gain, second_shift, expand_bias, jnp.zeros((1024,), BF),
-        ]
-    ).reshape(32, 128)
-    xf, cot, seg, wq, wk, wv, wo, we, wc, vecs = gather_call(
-        layer_input, cotangent, segments, weights, packed
-    )
-    small = [vecs[:, 2 * i : 2 * i + 2].reshape(1024).astype(F32) for i in range(8)]
-    bq, bv, bo, gain_one, shift_one, bc, gain_two, shift_two = small
-    be = vecs[:, 16:24].reshape(4096).astype(F32)
-    z, x, y, k = coords()
-    own = x * 512 + k * 256
-    xo = lax.dynamic_slice_in_dim(xf, own, 256, 0)
-    sk = seg.reshape(1, 1024)
-    sq = lax.dynamic_slice_in_dim(seg, x * 4 + k * 2, 2, 0).reshape(256, 1)
-
-    q = (plain_dot(xo, wq) + bq).astype(BF)
-    key = plain_dot(xf, wk).astype(BF)
-    val = (plain_dot(xf, wv) + bv).astype(BF)
-    ctx = attend(q, key, val, sq, sk)
-    first_sum = xo.astype(F32) + plain_dot(ctx, wo) + bo
-    first_out, normed_one, inverse_one = norm_forward(first_sum, gain_one, shift_one)
-    first_bf = first_out.astype(BF)
-    hidden = plain_dot(first_bf, we) + be
-    below = 0.5 + 0.5 * lax.erf(hidden * 0.5**0.5)
-    gelled = (hidden * below).astype(BF)
-    gelu_slope = (
-        below + hidden * (jnp.exp(-0.5 * hidden * hidden) * (2 * jnp.pi) ** -0.5)
-    ).astype(BF)
-    second_sum = first_out + plain_dot(gelled, wc) + bc
-    result, normed_two, inverse_two = norm_forward(second_sum, gain_two, shift_two)
-    grad_second, gain_two_grad, shift_two_grad = norm_backward(
-        cot.astype(F32), normed_two, inverse_two, gain_two
-    )
-    o_q, o_k, o_v, o_o, o_e, o_c, resf, dxf, vec = backward_call(
-        gelled, grad_second.astype(BF), grad_second, first_bf, gelu_slope, normed_one, inverse_one,
-        gain_one.reshape(1, 1024), ctx, q, key, val, xf, sq, sk, result.astype(BF),
-        gain_two_grad.reshape(1, 1024), shift_two_grad.reshape(1, 1024),
-        we, wc, wo, wq, wk, wv,
-    )
+            second_gain, second_shift, expand_bias,
+        ),
+    )
+    o_q, o_k, o_v, o_o, o_e, o_c, resf, dxf, vec = outs[6:]
     mine = vec.reshape(3072)
     vec_grads = [mine[i * 256 : (i + 1) * 256] for i in range(8)]
     return (

time: 361 us -> 296 us (0.82)
  local copies, waits for them, and re-layouts: 28.3 us -> 3.57 us
  matrix products: 18.7 us -> 0 us
  Pallas kernels: 294 us -> 279 us
  other arithmetic: 18.3 us -> 12.6 us
    unnamed x82 -> x13, local copies, waits for them, and re-layouts: 24.6 us -> 0.82 us
    dot_general x6 -> x0, matrix products: 18.7 us -> none  [plain_dot(): return jnp.dot(left_side, right_side, preferred_element_type=jnp.float32)]
    pallas_call x3 -> x1, Pallas kernels: 294 us -> 279 us  [layer_call(): pl.pallas_call(layer_kernel, out_shape=full_weights + [grad, grad, grad,...]
where the time goes in v4:
time: 296 us
  Pallas kernels  279 us (94%)
  other arithmetic  12.6 us (4%)
  local copies, waits for them, and re-layouts  3.57 us (1%)
    pallas_call x1, Pallas kernels, layer_call(): pl.pallas_call(layer_kernel, out_shape=full_weights + [grad, grad, grad,...  279 us

profile of v4, /device:TPU:0, one launch (start us, length us, event | category | flops | bytes accessed | tf_op | source)
XLA Modules:
  0.0 296.2 jit_solution(15143616933516713437)
XLA Ops:
  0.7 279.4 %layer.1 = (bf16[1024,1024]{1,0:T(8,128)(2,1)}, bf16[1024,1024]{1,0:T(8,128)(2,1)}, bf16[1024,1024]{1,0:T(8,128)(2,1)}, bf16[1024,1024]{1,0:T(8,128)(2,1)}, bf16...) custom-call(bf16[2,1,128,1024]{3,2,1,0:T(8,128)(2,1)} %inp.1, ...), custom_call_target="tpu_custom_call" | custom-call | tf_op jit(solution)/shard_map/layer/pallas_call | solution.py:1305
  280.0 0.0 copy-start.4
  280.0 1.3 slice_bitcast_fusion
  281.4 1.4 slice_bitcast_fusion.1
  282.8 0.0 copy-start.3
  282.8 2.2 convert_element_type.21
  285.0 0.0 copy-start.2
  285.0 2.2 convert_element_type.22
  287.2 0.0 copy-done.4
  287.2 0.0 copy-start.1
  287.2 1.1 convert_element_type.23
  288.3 0.0 copy-done.3
  288.3 1.1 convert_element_type.24
  289.4 0.0 copy-done.2
  289.4 1.1 convert_element_type.25
  290.4 0.0 copy-done.1
  290.4 0.0 copy-start
  290.4 2.5 convert_element_type.26
  292.9 0.0 copy-done
  293.0 0.0 copy-start.5
  293.0 2.5 convert_element_type.27
  295.4 0.0 copy-done.5
  295.4 0.8 copy.36
Async XLA Ops:
  280.0 7.1 %copy-start.4 = (bf16[256,1024]{1,0:T(8,128)(2,1)S(1)}, bf16[256,1024]{1,0:T(8,128)(2,1)}, u32[]{:S(2)}) copy-start(bf16[256,1024]{1,0:T(8,128)(2,1)} %get-tuple-element.29) | copy-start | bytes 1572868
  282.8 5.5 %copy-start.3 = (bf16[256,1024]{1,0:T(8,128)(2,1)S(1)}, bf16[256,1024]{1,0:T(8,128)(2,1)}, u32[]{:S(2)}) copy-start(bf16[256,1024]{1,0:T(8,128)(2,1)} %get-tuple-element.30) | copy-start | bytes 1572868
  285.0 4.4 %copy-start.2 = (bf16[256,1024]{1,0:T(8,128)(2,1)S(1)}, bf16[256,1024]{1,0:T(8,128)(2,1)}, u32[]{:S(2)}) copy-start(bf16[256,1024]{1,0:T(8,128)(2,1)} %get-tuple-element.31) | copy-start | bytes 1572868
  287.2 3.3 %copy-start.1 = (bf16[256,4096]{1,0:T(8,128)(2,1)S(1)}, bf16[256,4096]{1,0:T(8,128)(2,1)}, u32[]{:S(2)}) copy-start(bf16[256,4096]{1,0:T(8,128)(2,1)} %get-tuple-element.32) | copy-start | bytes 6291460
  290.4 2.5 copy-start
  293.0 2.5 copy-start.5

commit v5 on v4

--- a/solution.py
+++ b/solution.py
@@ -421,9 +421,12 @@
 F32 = jnp.float32
 CHUNKS = 24
 SLOTS = 3
-LAND = 4
-ROOM = 8
-Y_ROWS, X_ROWS = 48, 8
+LAND = 6
+LAND_D = 4
+ROOM = 10
+LAG = (0, 1, 3, 5, 6, 7, 8, 9, 11)
+Z_FROM, Z_TO = 12, 14
+Y_ROWS, X_ROWS, Z_ROWS = 40, 16, 8
 
 
 def coords():
@@ -487,12 +490,13 @@
     (
         s_d, l_d, r_d, b_y, r_y, b_x, r_x, b_1, r_1, b_2, r_2, o_b,
         gh, acc, ga, gal, dctx, dq, dk, dv, bias, we_b, wc_b, w_b,
-        dx_p, dx_r, dx_s, dx_y, vec, v_s, v_d, v_r,
-        gel, gb, fb, gp, n1, inv1, ctx, q, key, val, xf, res, cotf, segf, vec_in, vecf, row8, row_e,
+        dx_r, dx_y, vec, v_s, v_d, v_r,
+        gel, gb, fb, gp, n1, inv1, ctx, q, key, val, xf, res, segf, vec_in, vecf, row8, row_e,
         ss, rs, ds, dr, a_send, a_recv, v_send, v_recv, w_sem, o_sem,
         i_send, i_recv, g_send, g_recv, p_send, p_recv, f_send, f_recv,
     ) = rest
-    dx_b = dctx
+    dx_b, dx_s = dctx, gb
+    cotf = gh.at[:, pl.ds(0, 1024)]
     z, x, y, k = coords()
     f = y * 2 + k
     other = (1 - y) * 2 + k
@@ -603,7 +607,7 @@
             src = part(i, other, color * 64, 64)
             return remote(src, src, *sems, z1)
         if kind == 5:
-            src = part(i, other, c_x * 64 + Y_ROWS + X_ROWS, X_ROWS)
+            src = part(i, other, c_x * 64 + Y_ROWS + X_ROWS, Z_ROWS)
             return remote(src, src, *sems, z1)
         if kind == 6:
             return remote(part(i, f, 0, 256, True), part(i, f, 0, 256), *sems, sib)
@@ -622,7 +626,7 @@
         elif kind == 4:
             dst = part(i, other, c_z * 64, 64)
         elif kind == 5:
-            dst = part(i, other, c_o * 64 + Y_ROWS + X_ROWS, X_ROWS)
+            dst = part(i, other, c_o * 64 + Y_ROWS + X_ROWS, Z_ROWS)
         elif kind == 6:
             dst = part(i, y * 2 + 1 - k, 0, 256)
         else:
@@ -901,26 +905,39 @@
     def landed(stage, i, dst):
         pltpu.make_async_copy(dst, dst, rs.at[stage, i % LAND]).wait()
 
+    def order(i):
+        late = (i // Z_FROM) * (1 - i // Z_TO) if Z_FROM < Z_TO else 0
+        bits = tuple(
+            (1 - late) * p + late * q
+            for p, q in ((x, bit1), (bit1, bit2), (bit2, x))
+        )
+        peers = tuple(
+            tuple((1 - late) * p + late * q for p, q in zip(one, two))
+            for one, two in ((xn, z1), (z1, z2), (z2, xn))
+        )
+        return bits, peers
+
     def copies(stage, i):
         slot, land, room = i % SLOTS, i % LAND, i % ROOM
+        (first, second, third), peers = order(i)
         if stage == 0:
-            return send(0, i, s_d.at[slot], r_d.at[land], sib)
+            return send(0, i, s_d.at[slot], r_d.at[i % LAND_D], sib)
         if stage == 1:
             return send(1, i, b_y.at[slot, 1 - y], r_y.at[land], yn)
         if stage == 2:
-            return send(2, i, b_x.at[slot, rows_of((1 - x) * 64, 64)], r_x.at[land], xn)
+            return send(2, i, b_x.at[slot, rows_of((1 - first) * 64, 64)], r_x.at[land], peers[0])
         if stage == 3:
-            return send(3, i, b_1.at[slot, rows_of((1 - bit1) * 32, 32)], r_1.at[land], z1)
+            return send(3, i, b_1.at[slot, rows_of((1 - second) * 32, 32)], r_1.at[land], peers[1])
         if stage == 4:
-            return send(4, i, b_2.at[slot, rows_of((1 - bit2) * 16, 16)], r_2.at[land], z2)
+            return send(4, i, b_2.at[slot, rows_of((1 - third) * 16, 16)], r_2.at[land], peers[2])
         if stage == 5:
-            own = o_b.at[room, rows_of(x * 64 + bit1 * 32 + bit2 * 16, 16)]
-            return send(5, i, own, own, z2)
+            own = o_b.at[room, rows_of(first * 64 + second * 32 + third * 16, 16)]
+            return send(5, i, own, own, peers[2])
         if stage == 6:
-            own = o_b.at[room, rows_of(x * 64 + bit1 * 32, 32)]
-            return send(6, i, own, own, z1)
-        own = o_b.at[room, rows_of(x * 64, 64)]
-        return send(7, i, own, own, xn)
+            own = o_b.at[room, rows_of(first * 64 + second * 32, 32)]
+            return send(6, i, own, own, peers[1])
+        own = o_b.at[room, rows_of(first * 64, 64)]
+        return send(7, i, own, own, peers[0])
 
     def launch(stage, i):
         copies(stage, i).start()
@@ -1017,17 +1034,17 @@
         pltpu.make_async_copy(wc_b.at[slot], wc_b.at[slot], w_sem.at[slot]).wait()
         pltpu.make_async_copy(we_b.at[slot], we_b.at[slot], w_sem.at[2 + slot]).wait()
 
-        @pl.when(j < 7)
-        def _():
-            load_c(j + 1)
-            load_e(j + 1)
-
         grads = (right_dot(gb[...], wc_b[slot]) * gp[:, cols].astype(F32)).astype(BF)
         gh[:, cols] = grads
         acc[...] += right_dot(grads, we_b[slot])
         row = column(grads)
         for n in range(4):
             vec[j // 2, pl.ds(16 + (j % 2) * 4 + n, 1)] = row[:, n * 128 : n * 128 + 128]
+
+        @pl.when(j < 6)
+        def _():
+            load_c(j + 2)
+            load_e(j + 2)
 
     def first_norm():
         normed = n1[...]
@@ -1061,7 +1078,7 @@
         dq[:, cols] = (one_block(plain_dot(grad_scores, keys)) * HEAD_DIM**-0.5).astype(BF)
 
     def dx_core(g):
-        return remote(dx_p.at[g], dx_r.at[g], ds.at[g], dr.at[g], sib)
+        return remote(gel.at[:, pl.ds(g * 1024, 1024)], dx_r.at[g], ds.at[g], dr.at[g], sib)
 
     dx_far = remote(dx_s, dx_y, ds.at[2], dr.at[2], xn)
 
@@ -1073,12 +1090,12 @@
 
         @pl.when(n == 0)
         def _():
-            dx_p[1] = terms_here.astype(BF)
+            gel[:, pl.ds(1024, 1024)] = terms_here.astype(BF)
             dx_core(1).start()
 
         @pl.when(n == 1)
         def _():
-            dx_p[0] = terms_here.astype(BF)
+            gel[:, pl.ds(0, 1024)] = terms_here.astype(BF)
             dx_core(0).start()
 
         @pl.when(n == 2)
@@ -1144,8 +1161,9 @@
     for j in range(4):
         contract(j, item(8 + j))
     arrive_blocks((2,))
-    load_c(0)
-    load_e(0)
+    for j in range(2):
+        load_c(j)
+        load_e(j)
     for n in range(4):
         load_w(n)
     second_norm()
@@ -1153,7 +1171,7 @@
 
     def tick(t, carry):
         def at(stage):
-            i = t - stage
+            i = t - LAG[stage]
             return i, (i >= 0) & (i < CHUNKS)
 
         stage_zero(t)
@@ -1161,43 +1179,47 @@
 
         @pl.when(live1)
         def _():
-            slot, land = i1 % SLOTS, i1 % LAND
+            slot, land = i1 % SLOTS, i1 % LAND_D
             clear(1, i1)
-            landed(0, i1, r_d.at[land])
+            landed(0, i1, r_d.at[i1 % LAND_D])
             for plane in range(2):
                 b_y[slot, plane] = add(l_d[slot, plane], r_d[land, plane])
             launch(1, i1)
 
-        @pl.when(t < 8)
-        def _():
-            feed_forward(t)
-
-        @pl.when(t == 8)
+        @pl.when(t < 4)
+        def _():
+            def one(n, c):
+                feed_forward(2 * t + n)
+                return c
+
+            lax.fori_loop(0, 2, one, 0)
+
+        @pl.when(t == 4)
         def _():
             first_norm()
 
-        @pl.when((t >= 9) & (t < 17))
-        def _():
-            attention(t - 9)
-
-        @pl.when(t == 17)
+        @pl.when((t >= 5) & (t < 13))
+        def _():
+            attention(t - 5)
+
+        @pl.when(t == 13)
         def _():
             keep(0, column(dq[...]))
             keep(1, column(dv[...]))
             loaded_w(1)
             loaded_w(2)
 
-        @pl.when((t >= 17) & (t < 21))
-        def _():
-            input_rows(t - 17)
+        @pl.when((t >= 13) & (t < 17))
+        def _():
+            input_rows(t - 13)
 
         for stage in range(6):
 
-            @pl.when(t == 18 + 2 * stage)
+            @pl.when(t == 14 + 2 * stage)
             def _():
                 v_step(stage)
 
-        @pl.when(t == 23)
+        @pl.when(t == 18)
         def _():
             pltpu.make_async_copy(dx_y, dx_y, dr.at[2]).wait()
             dx_b[...] = (ga[...] + dx_y[...].astype(F32)).astype(BF)
@@ -1220,7 +1242,8 @@
             slot, land = i3 % SLOTS, i3 % LAND
             clear(3, i3)
             landed(2, i3, r_x.at[land])
-            b_1[slot] = add(b_x[slot, rows_of(x * 64, 64)], r_x[land])
+            first = order(i3)[0][0]
+            b_1[slot] = add(b_x[slot, rows_of(first * 64, 64)], r_x[land])
             launch(3, i3)
 
         i4, live4 = at(4)
@@ -1230,7 +1253,8 @@
             slot, land = i4 % SLOTS, i4 % LAND
             clear(4, i4)
             landed(3, i4, r_1.at[land])
-            b_2[slot] = add(b_1[slot, rows_of(bit1 * 32, 32)], r_1[land])
+            second = order(i4)[0][1]
+            b_2[slot] = add(b_1[slot, rows_of(second * 32, 32)], r_1[land])
             launch(4, i4)
 
         i5, live5 = at(5)
@@ -1240,8 +1264,9 @@
             slot, land = i5 % SLOTS, i5 % LAND
             clear(5, i5)
             landed(4, i5, r_2.at[land])
-            o_b[i5 % ROOM, rows_of(x * 64 + bit1 * 32 + bit2 * 16, 16)] = add(
-                b_2[slot, rows_of(bit2 * 16, 16)], r_2[land]
+            first, second, third = order(i5)[0]
+            o_b[i5 % ROOM, rows_of(first * 64 + second * 32 + third * 16, 16)] = add(
+                b_2[slot, rows_of(third * 16, 16)], r_2[land]
             )
             launch(5, i5)
 
@@ -1250,7 +1275,9 @@
         @pl.when(live6)
         def _():
             clear(6, i6)
-            landed(5, i6, o_b.at[i6 % ROOM, rows_of(x * 64 + bit1 * 32 + (1 - bit2) * 16, 16)])
+            first, second, third = order(i6)[0]
+            row = first * 64 + second * 32 + (1 - third) * 16
+            landed(5, i6, o_b.at[i6 % ROOM, rows_of(row, 16)])
             launch(6, i6)
 
         i7, live7 = at(7)
@@ -1258,19 +1285,21 @@
         @pl.when(live7)
         def _():
             clear(7, i7)
-            landed(6, i7, o_b.at[i7 % ROOM, rows_of(x * 64 + (1 - bit1) * 32, 32)])
+            first, second, _ = order(i7)[0]
+            landed(6, i7, o_b.at[i7 % ROOM, rows_of(first * 64 + (1 - second) * 32, 32)])
             launch(7, i7)
 
         i8, live8 = at(8)
 
         @pl.when(live8)
         def _():
-            landed(7, i8, o_b.at[i8 % ROOM, rows_of((1 - x) * 64, 64)])
+            first = order(i8)[0][0]
+            landed(7, i8, o_b.at[i8 % ROOM, rows_of((1 - first) * 64, 64)])
             store(i8)
 
         return carry
 
-    lax.fori_loop(0, CHUNKS + 8, tick, 0)
+    lax.fori_loop(0, CHUNKS + LAG[8], tick, 0)
     stored()
     for stage in range(8):
         for i in range(CHUNKS - SLOTS, CHUNKS):
@@ -1317,7 +1346,7 @@
         scratch_shapes=[
             pltpu.VMEM((SLOTS, 2, 128, 1024), BF),
             pltpu.VMEM((SLOTS, 2, 128, 1024), BF),
-            pltpu.VMEM((LAND, 2, 128, 1024), BF),
+            pltpu.VMEM((LAND_D, 2, 128, 1024), BF),
             pltpu.VMEM((SLOTS, 2, 128, 1024), BF),
             pltpu.VMEM((LAND, 128, 1024), BF),
             pltpu.VMEM((SLOTS, 128, 1024), BF),
@@ -1340,8 +1369,6 @@
             pltpu.VMEM((2, 512, 1024), BF),
             pltpu.VMEM((4, 1024, 1024), BF),
             pltpu.VMEM((2, 256, 1024), BF),
-            pltpu.VMEM((2, 256, 1024), BF),
-            pltpu.VMEM((256, 1024), BF),
             pltpu.VMEM((256, 1024), BF),
             pltpu.VMEM((4, 24, 128), F32),
             pltpu.VMEM((4, 2, 24, 128), F32),
@@ -1359,7 +1386,6 @@
             pltpu.VMEM((1024, 1024), BF),
             pltpu.VMEM((1024, 1024), BF),
             pltpu.VMEM((256, 1024), BF),
-            pltpu.VMEM((256, 1024), BF),
             pltpu.VMEM((8, 1, 128), jnp.int32),
             pltpu.VMEM((24, 128), F32),
             pltpu.VMEM((4, 24, 128), F32),
@@ -1377,6 +1403,49 @@
     )(inp, cot, seg, *weights, *vectors)
 
 
+def widen_kernel(*refs):
+    ins, outs = refs[:9], refs[9:]
+    for src, dst in zip(ins[:8], outs[:8]):
+        dst[...] = src[...].astype(dst.dtype)
+    vec, smalls = ins[8], outs[8:]
+
+    @pl.when(pl.program_id(0) == 0)
+    def _():
+        for i in range(8):
+            for half in range(2):
+                smalls[i][pl.ds(half * 128, 128)] = vec[2 * i + half]
+        for n in range(8):
+            smalls[8][pl.ds(n * 128, 128)] = vec[16 + n]
+
+
+def widen(narrow, vec):
+    steps = 8
+    in_specs, out_specs, shapes = [], [], []
+    for n, v in enumerate(narrow):
+        at = v.ndim - 2
+        block = v.shape[:at] + (v.shape[at] // steps,) + v.shape[at + 1 :]
+
+        def place(i, at=at, rank=v.ndim):
+            return tuple(i if d == at else 0 for d in range(rank))
+
+        in_specs.append(pl.BlockSpec(block, place))
+        out_specs.append(pl.BlockSpec(block, place))
+        shapes.append(jax.ShapeDtypeStruct(v.shape, BF if n == 7 else F32))
+    in_specs.append(pl.BlockSpec((24, 128), lambda i: (0, 0)))
+    for size in (256,) * 8 + (1024,):
+        out_specs.append(pl.BlockSpec((size,), lambda i: (0,)))
+        shapes.append(jax.ShapeDtypeStruct((size,), F32))
+    return pl.pallas_call(
+        widen_kernel,
+        grid=(steps,),
+        out_shape=shapes,
+        in_specs=in_specs,
+        out_specs=out_specs,
+        compiler_params=pltpu.CompilerParams(vmem_limit_bytes=61 << 20),
+        name="widen",
+    )(*narrow, vec)
+
+
 def per_group_device(
     layer_input, segments, cotangent,
     query_weight, key_weight, value_weight, output_weight, expand_weight, contract_weight,
@@ -1392,26 +1461,12 @@
         ),
     )
     o_q, o_k, o_v, o_o, o_e, o_c, resf, dxf, vec = outs[6:]
-    mine = vec.reshape(3072)
-    vec_grads = [mine[i * 256 : (i + 1) * 256] for i in range(8)]
+    wide = widen((o_q, o_k, o_v, o_o, o_e, o_c, dxf, resf), vec)
+    g_q, g_k, g_v, g_o, g_e, g_c, input_grad, layer_output = wide[:8]
+    b_q, b_v, b_o, g_one, s_one, b_c, g_two, s_two, b_e = wide[8:]
     return (
-        resf,
-        dxf.astype(F32),
-        o_q.astype(F32),
-        o_k.astype(F32),
-        o_v.astype(F32),
-        o_o.astype(F32),
-        o_e.astype(F32),
-        o_c.astype(F32),
-        vec_grads[0],
-        vec_grads[1],
-        vec_grads[2],
-        vec_grads[3],
-        vec_grads[4],
-        mine[2048:],
-        vec_grads[5],
-        vec_grads[6],
-        vec_grads[7],
+        layer_output, input_grad, g_q, g_k, g_v, g_o, g_e, g_c,
+        b_q, b_v, b_o, g_one, s_one, b_e, b_c, g_two, s_two,
     )
 
 

time: 296 us -> 283 us (0.956)
  other arithmetic: 12.6 us -> 0 us
  local copies, waits for them, and re-layouts: 3.57 us -> 0 us
  Pallas kernels: 279 us -> 282 us
    convert_element_type x7 -> x0, other arithmetic: 12.6 us -> none  [the longest x1 2.5 us: per_group_device(): o_e.astype(F32)]
    pallas_call x0 -> x1, Pallas kernels: none -> 9.42 us  [widen(): pl.pallas_call(widen_kernel, grid=(steps,), out_shape=shapes, in_specs=in...]
    pallas_call x1, Pallas kernels: 279 us -> 273 us  [layer_call(): pl.pallas_call(layer_kernel, out_shape=full_weights + [grad, grad, grad,...]
where the time goes in v5:
time: 283 us
  Pallas kernels  282 us (100%)
    pallas_call x1, Pallas kernels, layer_call(): pl.pallas_call(layer_kernel, out_shape=full_weights + [grad, grad, grad,...  273 us
    pallas_call x1, Pallas kernels, widen(): pl.pallas_call(widen_kernel, grid=(steps,), out_shape=shapes, in_specs=in...  9.42 us

profile of v5, /device:TPU:0, one launch (start us, length us, event | category | flops | bytes accessed | tf_op | source)
XLA Modules:
  0.0 282.9 jit_solution(9073810585687741158)
XLA Ops:
  0.7 272.7 %layer.1 = (bf16[1024,1024]{1,0:T(8,128)(2,1)}, bf16[1024,1024]{1,0:T(8,128)(2,1)}, bf16[1024,1024]{1,0:T(8,128)(2,1)}, bf16[1024,1024]{1,0:T(8,128)(2,1)}, bf16...) custom-call(bf16[2,1,128,1024]{3,2,1,0:T(8,128)(2,1)} %inp.1, ...), custom_call_target="tpu_custom_call" | custom-call | tf_op jit(solution)/shard_map/layer/pallas_call | solution.py:1334
  273.4 9.4 %widen.1 = (f32[256,1024]{1,0:T(8,128)}, f32[256,1024]{1,0:T(8,128)}, f32[256,1024]{1,0:T(8,128)}, f32[256,1024]{1,0:T(8,128)}, f32[256,4096]{1,0:T(8,128)}, /*i...) custom-call(bf16[256,1024]{1,0:T(8,128)(2,1)} %get-tuple-element.43., ...), custom_call_target="tpu_custom_call" | custom-call | tf_op jit(solution)/shard_map/widen/pallas_call | solution.py:1438

commit v6 on v5

--- a/solution.py
+++ b/solution.py
@@ -424,9 +424,10 @@
 LAND = 6
 LAND_D = 4
 ROOM = 10
-LAG = (0, 1, 3, 5, 6, 7, 8, 9, 11)
+LAG = (0, 0, 2, 4, 5, 6, 7, 8, 10)
 Z_FROM, Z_TO = 12, 14
-Y_ROWS, X_ROWS, Z_ROWS = 40, 16, 8
+SPLIT = ((64, 0, 0), (48, 16, 0))
+EARLY = 4
 
 
 def coords():
@@ -546,35 +547,38 @@
                 def _():
                     remote(src, dst, i_send.at[n, mb], i_recv.at[n, slot], to).wait_send()
 
-    def arrive_blocks(which):
-        for slot in range(2):
-            zz = 2 * k + slot
-            for n in which:
-                if n == 0:
-                    dst = xf.at[rows_of(x * 512 + zz * 128, 128)]
-                elif n == 1:
-                    dst = segf.at[x * 4 + zz]
-                else:
-                    dst = cotf.at[pl.ds(slot * 128, 128)]
-                pltpu.make_async_copy(dst, dst, i_recv.at[n, slot]).wait()
-
-    def group_copy(step):
+    def arrive_block(slot, which):
+        zz = 2 * k + slot
+        for n in which:
+            if n == 0:
+                dst = xf.at[rows_of(x * 512 + zz * 128, 128)]
+            elif n == 1:
+                dst = segf.at[x * 4 + zz]
+            else:
+                dst = cotf.at[pl.ds(slot * 128, 128)]
+            pltpu.make_async_copy(dst, dst, i_recv.at[n, slot]).wait()
+
+    def group_copy(step, block):
         who = x if step < 2 else 1 - x
-        src = xf.at[rows_of(who * 512 + k * 256, 256)]
-        sseg = segf.at[pl.ds(who * 4 + k * 2, 2)]
+        src = xf.at[rows_of(who * 512 + k * 256 + block * 128, 128)]
+        sseg = segf.at[who * 4 + k * 2 + block]
         to = (sib, xn, sib)[step]
         return (
-            remote(src, src, g_send.at[0, step], g_recv.at[0, step], to),
-            remote(sseg, sseg, g_send.at[1, step], g_recv.at[1, step], to),
-        )
-
-    def group_arrive(step):
+            remote(src, src, g_send.at[0, step, block], g_recv.at[0, step, block], to),
+            remote(sseg, sseg, g_send.at[1, step, block], g_recv.at[1, step, block], to),
+        )
+
+    def group_start(step, block):
+        for move in group_copy(step, block):
+            move.start()
+
+    def group_arrive(step, block):
         who = (x, 1 - x, 1 - x)[step]
         kk = (1 - k, k, 1 - k)[step]
-        src = xf.at[rows_of(who * 512 + kk * 256, 256)]
-        sseg = segf.at[pl.ds(who * 4 + kk * 2, 2)]
-        pltpu.make_async_copy(src, src, g_recv.at[0, step]).wait()
-        pltpu.make_async_copy(sseg, sseg, g_recv.at[1, step]).wait()
+        src = xf.at[rows_of(who * 512 + kk * 256 + block * 128, 128)]
+        sseg = segf.at[who * 4 + kk * 2 + block]
+        pltpu.make_async_copy(src, src, g_recv.at[0, step, block]).wait()
+        pltpu.make_async_copy(sseg, sseg, g_recv.at[1, step, block]).wait()
 
     items = []
     for shard, full in ((wq, fq), (wk, fk), (wv, fv), (wo, fo)):
@@ -585,6 +589,9 @@
         items.append((wc, fc, j * 256, 0, 1024))
     n_items = len(items)
 
+    def split(i):
+        return SPLIT[0] if i < EARLY else SPLIT[1]
+
     def part(i, quarter, start, size, own_src=False):
         shard, full, row, col, step = items[i]
         if own_src:
@@ -596,18 +603,19 @@
         if kind == 0:
             return remote(part(i, f, color * 64, 64, True), part(i, f, color * 64, 64), *sems, yn)
         if kind == 1:
-            return remote(part(i, f, c_o * 64, Y_ROWS, True), part(i, f, c_o * 64, Y_ROWS), *sems, yn)
+            rows = split(i)[0]
+            return remote(part(i, f, c_o * 64, rows, True), part(i, f, c_o * 64, rows), *sems, yn)
         if kind == 2:
             src = part(i, other, color * 64, 64)
             return remote(src, src, *sems, xn)
         if kind == 3:
-            src = part(i, other, c_z * 64 + Y_ROWS, X_ROWS)
+            src = part(i, other, c_z * 64 + split(i)[0], split(i)[1])
             return remote(src, src, *sems, xn)
         if kind == 4:
             src = part(i, other, color * 64, 64)
             return remote(src, src, *sems, z1)
         if kind == 5:
-            src = part(i, other, c_x * 64 + Y_ROWS + X_ROWS, Z_ROWS)
+            src = part(i, other, c_x * 64 + 64 - split(i)[2], split(i)[2])
             return remote(src, src, *sems, z1)
         if kind == 6:
             return remote(part(i, f, 0, 256, True), part(i, f, 0, 256), *sems, sib)
@@ -618,15 +626,15 @@
         if kind == 0:
             dst = part(i, other, color * 64, 64)
         elif kind == 1:
-            dst = part(i, other, c_o * 64, Y_ROWS)
+            dst = part(i, other, c_o * 64, split(i)[0])
         elif kind == 2:
             dst = part(i, other, c_x * 64, 64)
         elif kind == 3:
-            dst = part(i, other, c_o * 64 + Y_ROWS, X_ROWS)
+            dst = part(i, other, c_o * 64 + split(i)[0], split(i)[1])
         elif kind == 4:
             dst = part(i, other, c_z * 64, 64)
         elif kind == 5:
-            dst = part(i, other, c_o * 64 + Y_ROWS + X_ROWS, Z_ROWS)
+            dst = part(i, other, c_o * 64 + 64 - split(i)[2], split(i)[2])
         elif kind == 6:
             dst = part(i, y * 2 + 1 - k, 0, 256)
         else:
@@ -713,17 +721,25 @@
             arrive(i, 0)
             send_copy(i, 2).start()
             send_copy(i, 4).start()
-        if 2 <= t <= n_items + 1:
-            i = t - 2
+        if EARLY <= t - 3 < n_items:
+            i = t - 3
             arrive(i, 4)
             send_copy(i, 3).start()
             arrive(i, 2)
-            send_copy(i, 5).start()
-        if 3 <= t <= n_items + 2:
+            if split(i)[2]:
+                send_copy(i, 5).start()
+        if 0 <= t - 3 < EARLY:
             i = t - 3
             arrive(i, 1)
+            arrive(i, 2)
+            arrive(i, 4)
+            send_copy(i, 7).start()
+        if EARLY <= t - 6 < n_items:
+            i = t - 6
+            arrive(i, 1)
             arrive(i, 3)
-            arrive(i, 5)
+            if split(i)[2]:
+                arrive(i, 5)
             send_copy(i, 7).start()
 
     def fill_rows():
@@ -1116,51 +1132,54 @@
     vec_copies[1].start()
     relay(0)
     relay(1)
-    arrive_blocks((0, 1))
-    for step in range(2):
-        for move in group_copy(step):
-            move.start()
+    for block in range(2):
+        arrive_block(block, (0, 1))
+        group_start(0, block)
+        group_start(1, block)
     pltpu.make_async_copy(vec_in, vec_in, f_recv.at[0]).wait()
     vec_copies[2].start()
+    start_blocks((2,))
     relay(2)
+    group_arrive(1, 0)
+    group_start(2, 0)
     relay(3)
-    group_arrive(1)
-    for move in group_copy(2):
-        move.start()
-    start_blocks((2,))
-    relay(4)
+    group_arrive(1, 1)
+    group_start(2, 1)
     load_item(0)
     fill_rows()
+    for step in (0, 2):
+        for block in range(2):
+            group_arrive(step, block)
+    fill_bias()
+    relay(4)
+    project_own(item(0))
+    load_item(1)
     relay(5)
-    load_item(1)
-    project_own(item(0))
+    project_all(item(1), key, 0.0)
+    load_item(2)
     relay(6)
-    load_item(2)
-    group_arrive(0)
-    group_arrive(2)
-    fill_bias()
-    project_all(item(1), key, 0.0)
+    project_all(item(2), val, row8[1:2])
+    load_item(3)
     relay(7)
-    load_item(3)
-    project_all(item(2), val, row8[1:2])
+    heads(0, 3)
     relay(8)
+    heads(3, 6)
+    relay(9)
+    heads(6, 8)
+    relay(10)
+    attention_out(item(3))
     load_item(4)
-    heads(0, 3)
-    relay(9)
-    load_item(5)
-    heads(3, 6)
-    relay(10)
-    load_item(6)
-    heads(6, 8)
-    attention_out(item(3))
     for j in range(4):
         relay(11 + j)
-        load_item(7 + j)
         expand(j, item(4 + j))
-    load_item(11)
-    for j in range(4):
+        load_item(5 + j)
+    for j in range(3):
+        relay(15 + j)
         contract(j, item(8 + j))
-    arrive_blocks((2,))
+        load_item(9 + j)
+    contract(3, item(11))
+    for slot in range(2):
+        arrive_block(slot, (2,))
     for j in range(2):
         load_c(j)
         load_e(j)
@@ -1175,6 +1194,45 @@
             return i, (i >= 0) & (i < CHUNKS)
 
         stage_zero(t)
+        @pl.when(t < 4)
+        def _():
+            def one(n, c):
+                feed_forward(2 * t + n)
+                return c
+
+            lax.fori_loop(0, 2, one, 0)
+
+        @pl.when(t == 4)
+        def _():
+            first_norm()
+
+        @pl.when((t >= 5) & (t < 13))
+        def _():
+            attention(t - 5)
+
+        @pl.when(t == 13)
+        def _():
+            keep(0, column(dq[...]))
+            keep(1, column(dv[...]))
+            loaded_w(1)
+            loaded_w(2)
+
+        @pl.when((t >= 13) & (t < 17))
+        def _():
+            input_rows(t - 13)
+
+        for stage in range(6):
+
+            @pl.when(t == 14 + 2 * stage)
+            def _():
+                v_step(stage)
+
+        @pl.when(t == 18)
+        def _():
+            pltpu.make_async_copy(dx_y, dx_y, dr.at[2]).wait()
+            dx_b[...] = (ga[...] + dx_y[...].astype(F32)).astype(BF)
+            start_back(1)
+
         i1, live1 = at(1)
 
         @pl.when(live1)
@@ -1185,45 +1243,6 @@
             for plane in range(2):
                 b_y[slot, plane] = add(l_d[slot, plane], r_d[land, plane])
             launch(1, i1)
-
-        @pl.when(t < 4)
-        def _():
-            def one(n, c):
-                feed_forward(2 * t + n)
-                return c
-
-            lax.fori_loop(0, 2, one, 0)
-
-        @pl.when(t == 4)
-        def _():
-            first_norm()
-
-        @pl.when((t >= 5) & (t < 13))
-        def _():
-            attention(t - 5)
-
-        @pl.when(t == 13)
-        def _():
-            keep(0, column(dq[...]))
-            keep(1, column(dv[...]))
-            loaded_w(1)
-            loaded_w(2)
-
-        @pl.when((t >= 13) & (t < 17))
-        def _():
-            input_rows(t - 13)
-
-        for stage in range(6):
-
-            @pl.when(t == 14 + 2 * stage)
-            def _():
-                v_step(stage)
-
-        @pl.when(t == 18)
-        def _():
-            pltpu.make_async_copy(dx_y, dx_y, dr.at[2]).wait()
-            dx_b[...] = (ga[...] + dx_y[...].astype(F32)).astype(BF)
-            start_back(1)
 
         i2, live2 = at(2)
 
@@ -1313,11 +1332,13 @@
     finish_back(1)
     for i in range(n_items):
         for kind in range(8):
-            send_copy(i, kind).wait_send()
+            if kind not in (3, 5) or split(i)[kind // 2]:
+                send_copy(i, kind).wait_send()
     finish_blocks((0, 1, 2))
     for step in range(3):
-        for move in group_copy(step):
-            move.wait_send()
+        for block in range(2):
+            for move in group_copy(step, block):
+                move.wait_send()
     for move in vec_copies:
         move.wait_send()
 
@@ -1393,7 +1414,7 @@
             pltpu.VMEM((1, 4096), F32),
             dma((8, SLOTS)), dma((8, LAND)), dma((3,)), dma((3,)), dma((2, 2)), dma((2, 2)),
             dma((5,)), dma((5,)), dma((8,)), dma(()),
-            dma((3, 2)), dma((3, 2)), dma((2, 3)), dma((2, 3)),
+            dma((3, 2)), dma((3, 2)), dma((2, 3, 2)), dma((2, 3, 2)),
             dma((8, 12)), dma((8, 12)), dma((3,)), dma((3,)),
         ],
         compiler_params=pltpu.CompilerParams(

time: 283 us -> 275 us (0.972)
  Pallas kernels: 282 us -> 274 us
    pallas_call x1, Pallas kernels: 273 us -> 264 us  [layer_call(): pl.pallas_call(layer_kernel, out_shape=full_weights + [grad, grad, grad,...]
where the time goes in v6:
time: 275 us
  Pallas kernels  274 us (100%)
    pallas_call x1, Pallas kernels, layer_call(): pl.pallas_call(layer_kernel, out_shape=full_weights + [grad, grad, grad,...  264 us
    pallas_call x1, Pallas kernels, widen(): pl.pallas_call(widen_kernel, grid=(steps,), out_shape=shapes, in_specs=in...  9.42 us

profile of v6, /device:TPU:0, one launch (start us, length us, event | category | flops | bytes accessed | tf_op | source)
XLA Modules:
  0.0 274.7 jit_solution(221242553067372277)
XLA Ops:
  0.7 264.4 %layer.1 = (bf16[1024,1024]{1,0:T(8,128)(2,1)}, bf16[1024,1024]{1,0:T(8,128)(2,1)}, bf16[1024,1024]{1,0:T(8,128)(2,1)}, bf16[1024,1024]{1,0:T(8,128)(2,1)}, bf16...) custom-call(bf16[2,1,128,1024]{3,2,1,0:T(8,128)(2,1)} %inp.1, ...), custom_call_target="tpu_custom_call" | custom-call | tf_op jit(solution)/shard_map/layer/pallas_call | solution.py:1355
  265.1 9.4 %widen.1 = (f32[256,1024]{1,0:T(8,128)}, f32[256,1024]{1,0:T(8,128)}, f32[256,1024]{1,0:T(8,128)}, f32[256,1024]{1,0:T(8,128)}, f32[256,4096]{1,0:T(8,128)}, /*i...) custom-call(bf16[256,1024]{1,0:T(8,128)(2,1)} %get-tuple-element.43., ...), custom_call_target="tpu_custom_call" | custom-call | tf_op jit(solution)/shard_map/widen/pallas_call | solution.py:1459

commit v7 on v6

--- a/solution.py
+++ b/solution.py
@@ -426,8 +426,8 @@
 ROOM = 10
 LAG = (0, 0, 2, 4, 5, 6, 7, 8, 10)
 Z_FROM, Z_TO = 12, 14
-SPLIT = ((64, 0, 0), (48, 16, 0))
-EARLY = 4
+SPLIT = ((64, 0, 0), (40, 24, 0))
+EARLY, LATE = 4, 10
 
 
 def coords():
@@ -589,8 +589,11 @@
         items.append((wc, fc, j * 256, 0, 1024))
     n_items = len(items)
 
+    def direct(i):
+        return i < EARLY or LATE <= i < n_items
+
     def split(i):
-        return SPLIT[0] if i < EARLY else SPLIT[1]
+        return SPLIT[0] if direct(i) else SPLIT[1]
 
     def part(i, quarter, start, size, own_src=False):
         shard, full, row, col, step = items[i]
@@ -721,20 +724,20 @@
             arrive(i, 0)
             send_copy(i, 2).start()
             send_copy(i, 4).start()
-        if EARLY <= t - 3 < n_items:
+        if 0 <= t - 3 < n_items and not direct(t - 3):
             i = t - 3
             arrive(i, 4)
             send_copy(i, 3).start()
             arrive(i, 2)
             if split(i)[2]:
                 send_copy(i, 5).start()
-        if 0 <= t - 3 < EARLY:
+        if 0 <= t - 3 and direct(t - 3):
             i = t - 3
             arrive(i, 1)
             arrive(i, 2)
             arrive(i, 4)
             send_copy(i, 7).start()
-        if EARLY <= t - 6 < n_items:
+        if 0 <= t - 6 < n_items and not direct(t - 6):
             i = t - 6
             arrive(i, 1)
             arrive(i, 3)
@@ -1173,11 +1176,11 @@
         relay(11 + j)
         expand(j, item(4 + j))
         load_item(5 + j)
-    for j in range(3):
-        relay(15 + j)
+    relay(15)
+    for j in range(1, 4):
+        load_item(8 + j)
+    for j in range(4):
         contract(j, item(8 + j))
-        load_item(9 + j)
-    contract(3, item(11))
     for slot in range(2):
         arrive_block(slot, (2,))
     for j in range(2):
@@ -1440,7 +1443,7 @@
 
 
 def widen(narrow, vec):
-    steps = 8
+    steps = 2
     in_specs, out_specs, shapes = [], [], []
     for n, v in enumerate(narrow):
         at = v.ndim - 2

time: 275 us -> 269 us (0.978)
  Pallas kernels: 274 us -> 268 us
    pallas_call x1, Pallas kernels: 264 us -> 260 us  [layer_call(): pl.pallas_call(layer_kernel, out_shape=full_weights + [grad, grad, grad,...]
where the time goes in v7:
time: 269 us
  Pallas kernels  268 us (100%)
    pallas_call x1, Pallas kernels, layer_call(): pl.pallas_call(layer_kernel, out_shape=full_weights + [grad, grad, grad,...  260 us
    pallas_call x1, Pallas kernels, widen(): pl.pallas_call(widen_kernel, grid=(steps,), out_shape=shapes, in_specs=in...  7.53 us

profile of v7, /device:TPU:0, one launch (start us, length us, event | category | flops | bytes accessed | tf_op | source)
XLA Modules:
  0.0 268.8 jit_solution(7241746827345874272)
XLA Ops:
  0.7 260.5 %layer.1 = (bf16[1024,1024]{1,0:T(8,128)(2,1)}, bf16[1024,1024]{1,0:T(8,128)(2,1)}, bf16[1024,1024]{1,0:T(8,128)(2,1)}, bf16[1024,1024]{1,0:T(8,128)(2,1)}, bf16...) custom-call(bf16[2,1,128,1024]{3,2,1,0:T(8,128)(2,1)} %inp.1, ...), custom_call_target="tpu_custom_call" | custom-call | tf_op jit(solution)/shard_map/layer/pallas_call | solution.py:1358
  261.2 7.5 %widen.1 = (f32[256,1024]{1,0:T(8,128)}, f32[256,1024]{1,0:T(8,128)}, f32[256,1024]{1,0:T(8,128)}, f32[256,1024]{1,0:T(8,128)}, f32[256,4096]{1,0:T(8,128)}, /*i...) custom-call(bf16[256,1024]{1,0:T(8,128)(2,1)} %get-tuple-element.43., ...), custom_call_target="tpu_custom_call" | custom-call | tf_op jit(solution)/shard_map/widen/pallas_call | solution.py:1462

commit v8 on v7

--- a/solution.py
+++ b/solution.py
@@ -427,7 +427,7 @@
 LAG = (0, 0, 2, 4, 5, 6, 7, 8, 10)
 Z_FROM, Z_TO = 12, 14
 SPLIT = ((64, 0, 0), (40, 24, 0))
-EARLY, LATE = 4, 10
+EARLY, LATE = 4, 9
 
 
 def coords():

time: 269 us -> 269 us (level)
  no operation moved by 1% of the time
where the time goes in v8:
time: 269 us
  Pallas kernels  268 us (100%)
    pallas_call x1, Pallas kernels, layer_call(): pl.pallas_call(layer_kernel, out_shape=full_weights + [grad, grad, grad,...  260 us
    pallas_call x1, Pallas kernels, widen(): pl.pallas_call(widen_kernel, grid=(steps,), out_shape=shapes, in_specs=in...  7.53 us

profile of v8, /device:TPU:0, one launch (start us, length us, event | category | flops | bytes accessed | tf_op | source)
XLA Modules:
  0.0 268.6 jit_solution(6290606879101189412)
XLA Ops:
  0.7 260.2 %layer.1 = (bf16[1024,1024]{1,0:T(8,128)(2,1)}, bf16[1024,1024]{1,0:T(8,128)(2,1)}, bf16[1024,1024]{1,0:T(8,128)(2,1)}, bf16[1024,1024]{1,0:T(8,128)(2,1)}, bf16...) custom-call(bf16[2,1,128,1024]{3,2,1,0:T(8,128)(2,1)} %inp.1, ...), custom_call_target="tpu_custom_call" | custom-call | tf_op jit(solution)/shard_map/layer/pallas_call | solution.py:1358
  260.9 7.5 %widen.1 = (f32[256,1024]{1,0:T(8,128)}, f32[256,1024]{1,0:T(8,128)}, f32[256,1024]{1,0:T(8,128)}, f32[256,1024]{1,0:T(8,128)}, f32[256,4096]{1,0:T(8,128)}, /*i...) custom-call(bf16[256,1024]{1,0:T(8,128)(2,1)} %get-tuple-element.43., ...), custom_call_target="tpu_custom_call" | custom-call | tf_op jit(solution)/shard_map/widen/pallas_call | solution.py:1462
